TPU v7x, 256 devices: a whole 4x4x8 slice. The times are simulated.
256 devices in a mesh: layer: 64 (over z_hi, y, x), space: 4 (over z_lo, core).
Axes of the slice: x: 4, y: 4, z: 8 (z_hi: 4, z_lo: 2; z = z_hi * 2 + z_lo), core: 2. Of those that a mesh axis runs over, the one named last changes fastest.
Arguments:
- input_field: float32 [16, 32, 256], P('space'), may hold values from -6 to 6
- weights: bfloat16 [128, 9, 256, 256], P('layer'), may hold values from -0.125 to 0.125
- cotangent: float32 [16, 32, 256], P('space'), may hold values from -6 to 6
Outputs:
- block_outputs: float32 [64, 16, 32, 256], P('layer', 'space')
- block_adjoints: float32 [64, 16, 32, 256], P('layer', 'space')
- weight_grad: bfloat16 [256, 128, 9, 256], P('space', 'layer')
All inputs are finite; a program needn't handle non-finite values.
Results may differ from a plain program's by a relative error of at most 0.024.
Values may be sent and summed in bfloat16 or wider, within the bound.
A program may use at most 64 MiB of HBM per device.

v0:
```python
import functools

import jax
import jax.numpy as jnp
from jax import lax
from jax.experimental import pallas as pl
from jax.experimental.pallas import tpu as pltpu
from jax.sharding import PartitionSpec as P

MESH = pl.DeviceIdType.MESH

ITERS = 2
RADIX = 4

step_size = 0.125


CHUNK = 4


def column_chunks(low):
    height, width, channels = low.shape
    padded = jnp.pad(low, ((0, 0), (1, 1), (0, 0)))
    return jnp.stack(
        [padded[:, c : c + CHUNK + 2] for c in range(0, width, CHUNK)], axis=1
    )


def chunked_conv(low, kernel3, spec):
    height, width, channels = low.shape
    out = lax.conv_general_dilated(
        column_chunks(low),
        kernel3,
        (1, 1),
        ((1, 1), (0, 0)),
        dimension_numbers=("HNWC", spec, "HNWC"),
        preferred_element_type=jnp.float32,
    )
    return out.reshape(height, width, kernel3.shape[3] if spec == "HWIO" else kernel3.shape[2])


def conv(low, kernel3):
    return chunked_conv(low, kernel3, "HWIO")


def conv_transposed(low, flipped3):
    return chunked_conv(low, flipped3, "HWOI")


def kernel_gradient(low, signal):
    return lax.conv_general_dilated(
        low[None],
        signal[None],
        (1, 1),
        ((1, 1), (1, 1)),
        dimension_numbers=("CHWN", "IHWO", "NHWC"),
        preferred_element_type=jnp.float32,
    )


def forward_block(current, kernels):
    inputs_low = []
    slopes = []
    for kernel3 in kernels:
        low = current.astype(jnp.bfloat16)
        squashed = jnp.tanh(conv(low, kernel3))
        inputs_low.append(low)
        slopes.append(1.0 - squashed * squashed)
        current = current + step_size * squashed
    return current, inputs_low, slopes


def backward_block(adjoint, flipped, slopes):
    scaled_list = [None] * len(flipped)
    for index in reversed(range(len(flipped))):
        scaled = (step_size * slopes[index] * adjoint).astype(jnp.bfloat16)
        scaled_list[index] = scaled
        adjoint = adjoint + conv_transposed(scaled, flipped[index])
    return adjoint, scaled_list


def shifted_pairs(count, stride, shift):
    pairs = []
    for source in range(count):
        digit = (source // stride) % RADIX
        base = source - digit * stride
        pairs.append((source, base + ((digit + shift) % RADIX) * stride))
    return pairs


def exclusive_scan(value, reverse):
    count = lax.axis_size("layer")
    place = lax.axis_index("layer")
    total = jnp.zeros_like(value)
    stride = 1
    while stride < count:
        digit = (place // stride) % RADIX
        received = [
            lax.ppermute(value, "layer", shifted_pairs(count, stride, shift))
            for shift in range(1, RADIX)
        ]
        group = value
        for shift, part in zip(range(1, RADIX), received):
            earlier = shift > digit if reverse else shift <= digit
            total = total + jnp.where(earlier, part, jnp.zeros_like(part))
            group = group + part
        value = group
        stride *= RADIX
    return total


def scan_kernel(
    n_layer, n_space, reverse, value_ref, base_ref, out_ref,
    slots, gathered, group_buf, mine, total, send_sems, recv_sems, gsend, grecv,
):
    layer = lax.axis_index("layer")
    space = lax.axis_index("space")
    rows = value_ref.shape[0]
    strides = []
    stride = 1
    while stride < n_layer:
        strides.append(stride)
        stride *= RADIX

    partners = []
    for stride in strides:
        digit = (layer // stride) % RADIX
        base = layer - digit * stride
        for shift in range(1, RADIX):
            partners.append((base + ((digit + shift) % RADIX) * stride, space))
    for shift in range(1, n_space):
        partners.append((layer, (space + shift) % n_space))
    barrier = pltpu.get_barrier_semaphore()
    for partner in partners:
        pl.semaphore_signal(barrier, inc=1, device_id=partner, device_id_type=MESH)
    pl.semaphore_wait(barrier, len(partners))

    total[...] = jnp.zeros(total.shape, jnp.float32)
    source = value_ref
    for stage, stride in enumerate(strides):
        last = stage + 1 == len(strides)
        digit = (layer // stride) % RADIX
        base = layer - digit * stride
        copies = []
        for shift in range(1, RADIX):
            copy = pltpu.make_async_remote_copy(
                src_ref=source,
                dst_ref=slots.at[stage, shift - 1],
                send_sem=send_sems.at[stage, shift - 1],
                recv_sem=recv_sems.at[stage, shift - 1],
                device_id=(base + ((digit + shift) % RADIX) * stride, space),
                device_id_type=MESH,
            )
            wraps = digit + shift >= RADIX
            sends = (wraps if reverse else jnp.logical_not(wraps)) if last else None
            gets = (shift > digit if reverse else shift <= digit) if last else None
            copies.append((copy, sends, gets))
            if last:
                pl.when(sends)(copy.start)
            else:
                copy.start()
        for shift, (copy, sends, gets) in zip(range(1, RADIX), copies):
            if last:
                pl.when(sends)(copy.wait_send)
                pl.when(gets)(copy.wait_recv)
            else:
                copy.wait()
        group = source[...].astype(jnp.float32)
        for shift in range(1, RADIX):
            earlier = shift > digit if reverse else shift <= digit

            @pl.when(earlier)
            def _():
                total[...] += slots[stage, shift - 1].astype(jnp.float32)

            if not last:
                group = group + slots[stage, shift - 1].astype(jnp.float32)
        if not last:
            group_buf[stage] = group.astype(group_buf.dtype)
            source = group_buf.at[stage]

    mine[...] = total[...].astype(mine.dtype)
    copies = []
    for shift in range(1, n_space):
        copy = pltpu.make_async_remote_copy(
            src_ref=mine,
            dst_ref=gathered.at[shift - 1],
            send_sem=gsend.at[shift - 1],
            recv_sem=grecv.at[shift - 1],
            device_id=(layer, (space + shift) % n_space),
            device_id_type=MESH,
        )
        copy.start()
        copies.append(copy)
    here = pl.ds(space * rows, rows)
    out_ref[here] = base_ref[here] + total[...]
    for copy in copies:
        copy.wait()
    for shift in range(1, n_space):
        there = pl.ds(((space + n_space - shift) % n_space) * rows, rows)
        out_ref[there] = base_ref[there] + gathered[shift - 1].astype(jnp.float32)


def scan_and_gather(value, base, reverse, collective_id):
    n_layer = lax.axis_size("layer")
    n_space = lax.axis_size("space")
    stages = 0
    while RADIX ** stages < n_layer:
        stages += 1
    assert RADIX ** stages == n_layer
    rows, width, channels = value.shape
    piece = (rows, width, channels)
    link = jnp.bfloat16
    return pl.pallas_call(
        functools.partial(scan_kernel, n_layer, n_space, reverse),
        out_shape=jax.ShapeDtypeStruct((n_space * rows, width, channels), jnp.float32),
        in_specs=[pl.BlockSpec(memory_space=pltpu.VMEM)] * 2,
        out_specs=pl.BlockSpec(memory_space=pltpu.VMEM),
        scratch_shapes=[
            pltpu.VMEM((stages, RADIX - 1) + piece, link),
            pltpu.VMEM((n_space - 1,) + piece, link),
            pltpu.VMEM((max(stages - 1, 1),) + piece, link),
            pltpu.VMEM(piece, link),
            pltpu.VMEM(piece, jnp.float32),
            pltpu.SemaphoreType.DMA((stages, RADIX - 1)),
            pltpu.SemaphoreType.DMA((stages, RADIX - 1)),
            pltpu.SemaphoreType.DMA((n_space - 1,)),
            pltpu.SemaphoreType.DMA((n_space - 1,)),
        ],
        compiler_params=pltpu.CompilerParams(
            collective_id=collective_id,
            has_side_effects=True,
            vmem_limit_bytes=8 * 1024 * 1024,
        ),
    )(value.astype(link), base)


def gather_space(piece):
    count = lax.axis_size("space")
    place = lax.axis_index("space")
    rows = piece.shape[0]
    whole = jnp.zeros((count * rows,) + piece.shape[1:], piece.dtype)
    whole = lax.dynamic_update_slice_in_dim(whole, piece, place * rows, 0)
    for shift in range(1, count):
        part = lax.ppermute(
            piece, "space", [(i, (i + shift) % count) for i in range(count)]
        )
        source = (place + count - shift) % count
        whole = lax.dynamic_update_slice_in_dim(whole, part, source * rows, 0)
    return whole


def own_rows(whole, rows):
    return lax.dynamic_slice_in_dim(whole, lax.axis_index("space") * rows, rows, 0)


def on_device(input_field, weights, cotangent):
    rows = input_field.shape[0]
    channels = weights.shape[3]
    kernels = [w.reshape(3, 3, channels, channels) for w in weights]
    flipped = [k[::-1, ::-1] for k in kernels]
    full_input = gather_space(input_field)
    full_cotangent = gather_space(cotangent)

    begin_state = full_input
    for sweep_index in range(ITERS):
        block_end, _, _ = forward_block(begin_state, kernels)
        jump = own_rows(block_end - begin_state, rows)
        begin_state = scan_and_gather(jump, full_input, False, sweep_index)
    outputs, inputs_low, slopes = forward_block(begin_state, kernels)

    finish = full_cotangent
    for sweep_index in range(ITERS):
        begins, _ = backward_block(finish, flipped, slopes)
        back = own_rows(begins - finish, rows)
        finish = scan_and_gather(back, full_cotangent, True, ITERS + sweep_index)
    begins, scaled_list = backward_block(finish, flipped, slopes)

    quarter = channels // lax.axis_size("space")
    first = lax.axis_index("space") * quarter
    pieces = []
    for low, scaled in zip(inputs_low, scaled_list):
        signal = lax.dynamic_slice_in_dim(scaled, first, quarter, 2)
        grad = kernel_gradient(low, signal)
        pieces.append(jnp.transpose(grad, (3, 1, 2, 0)).reshape(quarter, 9, channels))
    weight_grad = jnp.stack(pieces, axis=1).astype(jnp.bfloat16)
    return (own_rows(outputs, rows)[None], own_rows(begins, rows)[None], weight_grad)


def solution(mesh):
    placed = (P("space", None, None), P("layer", None, None, None), P("space", None, None))
    return jax.shard_map(
        on_device,
        mesh=mesh,
        in_specs=placed,
        out_specs=(
            P("layer", "space", None, None),
            P("layer", "space", None, None),
            P("space", "layer", None, None),
        ),
        check_vma=False,
    )
```

profile of v0, /device:TPU:1, one launch (start us, length us, event | category | flops | bytes accessed | tf_op | source)
XLA Modules:
  0.0 169.6 jit_solution(9706899627666102092)
XLA Ops:
  0.6 3.1 %collective-permute-start = (f32[4,32,256]{2,1,0:T(8,128)}, f32[4,32,256]{2,1,0:T(8,128)S(1)}, u32[]{:S(2)}, u32[]{:S(2)}) collective-permute-start(f32[4,32,256]{2,1,0:T(8,128)} %param.3), channel_id=1, source_target_pairs={{0,1},{1,2},{2,3},{3,0},{4,5},{5,6},{6,7},{7,4},{8,9},{9,10},{10,1... | collective-permute-start | bytes 393224 | tf_op jit(solution)/shard_map/ppermute | solution.py:245
  4.0 1.3 collective-permute-start.1
  5.3 2.0 %collective-permute-start.3 = (f32[4,32,256]{2,1,0:T(8,128)}, f32[4,32,256]{2,1,0:T(8,128)}, u32[]{:S(2)}, u32[]{:S(2)}) collective-permute-start(f32[4,32,256]{2,1,0:T(8,128)} %param.5), channel_id=1, source_target_pairs={{0,1},{1,2},{2,3},{3,0},{4,5},{5,6},{6,7},{7,4},{8,9},{9,10},{10,1... | collective-permute-start | bytes 393224 | tf_op jit(solution)/shard_map/ppermute | solution.py:245
  7.3 2.9 %fusion.59 = (bf16[1,9,256,256]{3,2,1,0:T(8,128)(2,1)S(1)}, bf16[1,9,256,256]{3,2,1,0:T(8,128)(2,1)}) fusion(bf16[2,9,256,256]{3,2,1,0:T(8,128)(2,1)} %param.4), kind=kLoop, calls=%fused_computation.290 | loop fusion | bytes 4718592 | tf_op jit(solution)/shard_map/unstack | solution.py:260
  10.3 1.1 constant_dynamic-update-slice_fusion.99
  12.3 0.9 fusion.3
  13.9 1.0 copy-done.5
  15.0 0.9 fusion.2
  16.0 1.0 mul.110
  17.0 0.9 fusion.31.value_ref
  17.9 26.9 %shard_map.58 = f32[16,32,256]{2,1,0:T(8,128)S(1)} custom-call(bf16[4,32,256]{2,1,0:T(8,128)(2,1)S(1)} %fusion.31.value_ref, f32[16,32,256]{2,1,0:T(8,128)S(1)} %constant_dynamic-update-slice_fusion.100.base_ref), custom_call_target="tpu_custom_call" | custom-call | tf_op jit(solution)/shard_map/pallas_call | solution.py:214
  45.2 0.9 fusion.1
  46.4 0.9 fusion.57
  47.6 1.0 copy-done.6
  48.6 0.9 fusion
  49.7 1.0 mul.114
  50.7 1.0 fusion.30.value_ref
  51.7 25.4 %shard_map.59 = f32[16,32,256]{2,1,0:T(8,128)S(1)} custom-call(bf16[4,32,256]{2,1,0:T(8,128)(2,1)S(1)} %fusion.30.value_ref, f32[16,32,256]{2,1,0:T(8,128)S(1)} %constant_dynamic-update-slice_fusion.100.base_ref), custom_call_target="tpu_custom_call" | custom-call | tf_op jit(solution)/shard_map/pallas_call | solution.py:214
  77.4 1.0 copy-done.1
  78.3 1.7 subtract_multiply_fusion
  80.4 0.9 fusion.56
  81.5 1.9 %subtract_multiply_fusion.1 = (f32[16,8,4,256]{3,1,2,0:T(8,128)}, f32[16,8,4,256]{3,1,2,0:T(8,128)}) fusion(bf16[3,3,256,256]{3,2,1,0:T(8,128)(2,1)S(1)} %bitcast.420, bf16[16,8,6,256]{3,2,0,1:T(8,128)(2,1)S(1)} %constant_dynamic-update-slice_fusion.40), kind=kOutput, calls=%fused_computation.20 | convolution fusion | flops 579338240 | bytes 2621440 | tf_op jit(solution)/shard_map/conv_general_dilated | solution.py:31
  83.4 0.7 convert_bitcast_fusion
  84.1 0.9 constant_dynamic-update-slice_fusion.98
  85.5 1.2 copy.48
  86.9 0.9 constant_dynamic-update-slice_fusion.97
  87.9 0.9 constant_dynamic-update-slice_fusion.96.base_ref
  89.1 0.9 fusion.16
  90.8 1.0 copy-done.2
  91.8 0.9 fusion.14
  93.2 27.5 %shard_map.60 = f32[16,32,256]{2,1,0:T(8,128)S(1)} custom-call(bf16[4,32,256]{2,1,0:T(8,128)(2,1)S(1)} %fusion.28.value_ref, f32[16,32,256]{2,1,0:T(8,128)S(1)} %constant_dynamic-update-slice_fusion.96.base_ref), custom_call_target="tpu_custom_call" | custom-call | tf_op jit(solution)/shard_map/pallas_call | solution.py:214
  121.0 0.9 copy-done.7
  121.9 0.9 fusion.12
  123.2 0.9 multiply_convert_fusion.2
  124.3 1.0 copy-done.3
  125.4 0.9 fusion.10
  126.7 0.9 fusion.27.value_ref
  127.6 25.0 %shard_map.61 = f32[16,32,256]{2,1,0:T(8,128)S(1)} custom-call(bf16[4,32,256]{2,1,0:T(8,128)(2,1)S(1)} %fusion.27.value_ref, f32[16,32,256]{2,1,0:T(8,128)S(1)} %constant_dynamic-update-slice_fusion.96.base_ref), custom_call_target="tpu_custom_call" | custom-call | tf_op jit(solution)/shard_map/pallas_call | solution.py:214
  153.0 0.9 copy-done.8
  153.9 0.9 fusion.8
  155.5 0.6 copy-done.10
  156.1 2.6 %convolution_convert_fusion.1 = bf16[64,3,3,256]{3,0,2,1:T(8,128)(2,1)S(1)} fusion(bf16[1,16,32,256]{3,2,1,0:T(8,128)(2,1)S(1)} %copy-done.10, bf16[1,16,32,64]{3,2,1,0:T(8,128)(2,1)S(1)} %get-tuple-element.24), kind=kOutput, calls=%fused_computation.11 | convolution fusion | flops 141836288 | bytes 622592 | tf_op jit(solution)/shard_map/transpose | solution.py:285
  159.2 2.6 %convolution_convert_fusion = bf16[64,3,3,256]{3,0,2,1:T(8,128)(2,1)S(1)} fusion(bf16[1,16,32,256]{3,2,1,0:T(8,128)(2,1)S(1)} %bitcast.411, bf16[1,16,32,64]{3,2,1,0:T(8,128)(2,1)S(1)} %get-tuple-element.23), kind=kOutput, calls=%fused_computation.10 | convolution fusion | flops 141836288 | bytes 622592 | tf_op jit(solution)/shard_map/transpose | solution.py:285
  162.5 0.6 copy-done.4
  163.1 0.9 fusion.6
  164.4 1.2 copy.47
  165.8 2.2 %pad_maximum_fusion = bf16[64,2,9,256]{3,1,2,0:T(2,128)(2,1)} fusion(bf16[64,1,9,256]{3,1,2,0:T(2,128)(2,1)S(1)} %copy.67, bf16[64,1,9,256]{3,1,2,0:T(2,128)(2,1)S(1)} %copy.66), kind=kLoop, calls=%fused_computation.12 | loop fusion | flops 1179648 | bytes 1179648 | tf_op jit(solution)/shard_map/stack | solution.py:286
  168.0 1.6 fusion.26
  (163 shorter events, 9.7 us)
Async XLA Ops:
  0.6 10.8 %collective-permute-start = (f32[4,32,256]{2,1,0:T(8,128)}, f32[4,32,256]{2,1,0:T(8,128)S(1)}, u32[]{:S(2)}, u32[]{:S(2)}) collective-permute-start(f32[4,32,256]{2,1,0:T(8,128)} %param.3), channel_id=1, source_target_pairs={{0,1},{1,2},{2,3},{3,0},{4,5},{5,6},{6,7},{7,4},{8,9},{9,10},{10,1... | collective-permute-start | bytes 393224 | tf_op jit(solution)/shard_map/ppermute | solution.py:245
  3.7 8.3 %collective-permute-start.2 = (f32[4,32,256]{2,1,0:T(8,128)}, f32[4,32,256]{2,1,0:T(8,128)S(1)}, u32[]{:S(2)}, u32[]{:S(2)}) collective-permute-start(f32[4,32,256]{2,1,0:T(8,128)} %param.3), channel_id=1, source_target_pairs={{0,3},{1,0},{2,1},{3,2},{4,7},{5,4},{6,5},{7,6},{8,11},{9,8},{10,9... | collective-permute-start | bytes 393224 | tf_op jit(solution)/shard_map/ppermute | solution.py:245
  4.0 7.9 %collective-permute-start.1 = (f32[4,32,256]{2,1,0:T(8,128)}, f32[4,32,256]{2,1,0:T(8,128)S(1)}, u32[]{:S(2)}, u32[]{:S(2)}) collective-permute-start(f32[4,32,256]{2,1,0:T(8,128)} %param.3), channel_id=1, source_target_pairs={{0,2},{1,3},{2,0},{3,1},{4,6},{5,7},{6,4},{7,5},{8,10},{9,11},{10,... | collective-permute-start | bytes 393224 | tf_op jit(solution)/shard_map/ppermute | solution.py:245
  5.3 78.8 %collective-permute-start.3 = (f32[4,32,256]{2,1,0:T(8,128)}, f32[4,32,256]{2,1,0:T(8,128)}, u32[]{:S(2)}, u32[]{:S(2)}) collective-permute-start(f32[4,32,256]{2,1,0:T(8,128)} %param.5), channel_id=1, source_target_pairs={{0,1},{1,2},{2,3},{3,0},{4,5},{5,6},{6,7},{7,4},{8,9},{9,10},{10,1... | collective-permute-start | bytes 393224 | tf_op jit(solution)/shard_map/ppermute | solution.py:245
  7.3 80.5 %collective-permute-start.5 = (f32[4,32,256]{2,1,0:T(8,128)}, f32[4,32,256]{2,1,0:T(8,128)}, u32[]{:S(2)}, u32[]{:S(2)}) collective-permute-start(f32[4,32,256]{2,1,0:T(8,128)} %param.5), channel_id=1, source_target_pairs={{0,3},{1,0},{2,1},{3,2},{4,7},{5,4},{6,5},{7,6},{8,11},{9,8},{10,9... | collective-permute-start | bytes 393224 | tf_op jit(solution)/shard_map/ppermute | solution.py:245
  7.3 2.9 %copy-start.11 = (f32[4,32,256]{2,1,0:T(8,128)S(1)}, f32[4,32,256]{2,1,0:T(8,128)}, u32[]{:S(2)}) copy-start(f32[4,32,256]{2,1,0:T(8,128)} %param.3) | copy-start | bytes 393220
  10.2 35.0 %copy-start = (bf16[1,9,256,256]{3,2,1,0:T(8,128)(2,1)}, bf16[1,9,256,256]{3,2,1,0:T(8,128)(2,1)S(1)}, u32[]{:S(2)}) copy-start(bf16[1,9,256,256]{3,2,1,0:T(8,128)(2,1)S(1)} %get-tuple-element.15) | copy-start | bytes 3538948
  11.5 75.4 %collective-permute-start.4 = (f32[4,32,256]{2,1,0:T(8,128)}, f32[4,32,256]{2,1,0:T(8,128)}, u32[]{:S(2)}, u32[]{:S(2)}) collective-permute-start(f32[4,32,256]{2,1,0:T(8,128)} %param.5), channel_id=1, source_target_pairs={{0,2},{1,3},{2,0},{3,1},{4,6},{5,7},{6,4},{7,5},{8,10},{9,11},{10,... | collective-permute-start | bytes 393224 | tf_op jit(solution)/shard_map/ppermute | solution.py:245
  13.7 1.3 copy-start.5
  47.3 1.3 copy-start.6
  77.1 1.3 copy-start.1
  83.4 1.7 copy-start.9
  90.6 1.3 copy-start.2
  120.6 1.3 copy-start.7
  124.1 1.3 copy-start.3
  152.6 1.3 copy-start.8
  155.2 1.0 copy-start.10
  161.8 1.3 copy-start.4
where the time goes:
time: 170 us
  Pallas kernels  105 us (62%)
  local copies, waits for them, and re-layouts  27.4 us (16%)
  matrix products  17.4 us (10%)
  other arithmetic  10.9 us (6%)
  starting transfers between devices  6.9 us (4%)
  between operations  1.97 us (1%)
    pallas_call x4, Pallas kernels, scan_and_gather(): pl.pallas_call(functools.partial(scan_kernel, n_layer, n_space, reverse),...  105 us
    conv_general_dilated x12, matrix products, chunked_conv(): lax.conv_general_dilated(column_chunks(low), kernel3, (1, 1), ((1, 1), (0...  12.2 us
    unnamed x108, local copies, waits for them, and re-layouts  10.1 us
    ppermute x6, starting transfers between devices, gather_space(): lax.ppermute(piece, 'space', [(i, (i + shift) % count) for i in range(cou...  6.9 us
    transpose x2, matrix products, on_device(): jnp.transpose(grad, (3, 1, 2, 0)).reshape(quarter, 9, channels)  5.2 us
    mul x12, local copies, waits for them, and re-layouts, forward_block(): current = current + step_size * squashed  4.97 us
  transfers between devices with their start and end apart: 6, of which 1 were waited for; matrix products, arithmetic and copies ran while one was open for 14% of the time, Pallas kernels for 31%

commit v1 on v0

--- a/solution.py
+++ b/solution.py
@@ -136,6 +136,7 @@
     pl.semaphore_wait(barrier, len(partners))
 
     total[...] = jnp.zeros(total.shape, jnp.float32)
+    pending = []
     source = value_ref
     for stage, stride in enumerate(strides):
         last = stage + 1 == len(strides)
@@ -161,10 +162,10 @@
                 copy.start()
         for shift, (copy, sends, gets) in zip(range(1, RADIX), copies):
             if last:
-                pl.when(sends)(copy.wait_send)
                 pl.when(gets)(copy.wait_recv)
             else:
-                copy.wait()
+                copy.wait_recv()
+            pending.append((copy, sends))
         group = source[...].astype(jnp.float32)
         for shift in range(1, RADIX):
             earlier = shift > digit if reverse else shift <= digit
@@ -195,10 +196,17 @@
     here = pl.ds(space * rows, rows)
     out_ref[here] = base_ref[here] + total[...]
     for copy in copies:
-        copy.wait()
+        copy.wait_recv()
     for shift in range(1, n_space):
         there = pl.ds(((space + n_space - shift) % n_space) * rows, rows)
         out_ref[there] = base_ref[there] + gathered[shift - 1].astype(jnp.float32)
+    for copy, sends in pending:
+        if sends is None:
+            copy.wait_send()
+        else:
+            pl.when(sends)(copy.wait_send)
+    for copy in copies:
+        copy.wait_send()
 
 
 def scan_and_gather(value, base, reverse, collective_id):

time: 170 us -> 170 us (level)
  transfers between devices with their start and end apart: 6 -> 6, of which waited for: 1 -> 1; matrix products, arithmetic and copies ran while one was open for 14% -> 14% of each run, Pallas kernels for 31% -> 30%
where the time goes in v1:
time: 170 us; the launch traced here: 169 us
  Pallas kernels  104 us (61%)
  local copies, waits for them, and re-layouts  27.4 us (16%)
  matrix products  17.4 us (10%)
  other arithmetic  10.9 us (6%)
  starting transfers between devices  6.9 us (4%)
  between operations  1.97 us (1%)
    pallas_call x4, Pallas kernels, scan_and_gather(): pl.pallas_call(functools.partial(scan_kernel, n_layer, n_space, reverse),...  104 us
    conv_general_dilated x12, matrix products, chunked_conv(): lax.conv_general_dilated(column_chunks(low), kernel3, (1, 1), ((1, 1), (0...  12.2 us
    unnamed x108, local copies, waits for them, and re-layouts  10.1 us
    ppermute x6, starting transfers between devices, gather_space(): lax.ppermute(piece, 'space', [(i, (i + shift) % count) for i in range(cou...  6.9 us
    transpose x2, matrix products, on_device(): jnp.transpose(grad, (3, 1, 2, 0)).reshape(quarter, 9, channels)  5.2 us
    mul x12, local copies, waits for them, and re-layouts, forward_block(): current = current + step_size * squashed  4.97 us
  transfers between devices with their start and end apart: 6, of which 1 were waited for; matrix products, arithmetic and copies ran while one was open for 14% of the time, Pallas kernels for 30%

profile of v1, /device:TPU:1, one launch (start us, length us, event | category | flops | bytes accessed | tf_op | source)
XLA Modules:
  0.0 169.2 jit_solution(4546200665406573943)
XLA Ops:
  0.6 3.1 %collective-permute-start = (f32[4,32,256]{2,1,0:T(8,128)}, f32[4,32,256]{2,1,0:T(8,128)S(1)}, u32[]{:S(2)}, u32[]{:S(2)}) collective-permute-start(f32[4,32,256]{2,1,0:T(8,128)} %param.3), channel_id=1, source_target_pairs={{0,1},{1,2},{2,3},{3,0},{4,5},{5,6},{6,7},{7,4},{8,9},{9,10},{10,1... | collective-permute-start | bytes 393224 | tf_op jit(solution)/shard_map/ppermute | solution.py:253
  4.0 1.3 collective-permute-start.1
  5.3 2.0 %collective-permute-start.3 = (f32[4,32,256]{2,1,0:T(8,128)}, f32[4,32,256]{2,1,0:T(8,128)}, u32[]{:S(2)}, u32[]{:S(2)}) collective-permute-start(f32[4,32,256]{2,1,0:T(8,128)} %param.5), channel_id=1, source_target_pairs={{0,1},{1,2},{2,3},{3,0},{4,5},{5,6},{6,7},{7,4},{8,9},{9,10},{10,1... | collective-permute-start | bytes 393224 | tf_op jit(solution)/shard_map/ppermute | solution.py:253
  7.3 2.9 %fusion.59 = (bf16[1,9,256,256]{3,2,1,0:T(8,128)(2,1)S(1)}, bf16[1,9,256,256]{3,2,1,0:T(8,128)(2,1)}) fusion(bf16[2,9,256,256]{3,2,1,0:T(8,128)(2,1)} %param.4), kind=kLoop, calls=%fused_computation.290 | loop fusion | bytes 4718592 | tf_op jit(solution)/shard_map/unstack | solution.py:268
  10.3 1.1 constant_dynamic-update-slice_fusion.99
  12.3 0.9 fusion.3
  13.9 1.0 copy-done.5
  15.0 0.9 fusion.2
  16.0 1.0 mul.110
  17.0 0.9 fusion.31.value_ref
  17.9 25.7 %shard_map.58 = f32[16,32,256]{2,1,0:T(8,128)S(1)} custom-call(bf16[4,32,256]{2,1,0:T(8,128)(2,1)S(1)} %fusion.31.value_ref, f32[16,32,256]{2,1,0:T(8,128)S(1)} %constant_dynamic-update-slice_fusion.100.base_ref), custom_call_target="tpu_custom_call" | custom-call | tf_op jit(solution)/shard_map/pallas_call | solution.py:222
  44.0 0.9 fusion.1
  45.2 0.9 fusion.57
  46.4 1.0 copy-done.6
  47.4 0.9 fusion
  48.5 1.0 mul.114
  49.5 1.0 fusion.30.value_ref
  50.5 25.2 %shard_map.59 = f32[16,32,256]{2,1,0:T(8,128)S(1)} custom-call(bf16[4,32,256]{2,1,0:T(8,128)(2,1)S(1)} %fusion.30.value_ref, f32[16,32,256]{2,1,0:T(8,128)S(1)} %constant_dynamic-update-slice_fusion.100.base_ref), custom_call_target="tpu_custom_call" | custom-call | tf_op jit(solution)/shard_map/pallas_call | solution.py:222
  76.0 1.0 copy-done.1
  77.0 1.7 subtract_multiply_fusion
  79.0 0.9 fusion.56
  80.2 1.9 %subtract_multiply_fusion.1 = (f32[16,8,4,256]{3,1,2,0:T(8,128)}, f32[16,8,4,256]{3,1,2,0:T(8,128)}) fusion(bf16[3,3,256,256]{3,2,1,0:T(8,128)(2,1)S(1)} %bitcast.420, bf16[16,8,6,256]{3,2,0,1:T(8,128)(2,1)S(1)} %constant_dynamic-update-slice_fusion.40), kind=kOutput, calls=%fused_computation.20 | convolution fusion | flops 579338240 | bytes 2621440 | tf_op jit(solution)/shard_map/conv_general_dilated | solution.py:31
  82.0 0.7 convert_bitcast_fusion
  82.8 0.9 constant_dynamic-update-slice_fusion.98
  84.1 1.2 copy.48
  85.6 0.9 constant_dynamic-update-slice_fusion.97
  86.5 0.9 constant_dynamic-update-slice_fusion.96.base_ref
  87.8 0.9 fusion.16
  89.5 1.0 copy-done.2
  90.5 0.9 fusion.14
  91.8 28.8 %shard_map.60 = f32[16,32,256]{2,1,0:T(8,128)S(1)} custom-call(bf16[4,32,256]{2,1,0:T(8,128)(2,1)S(1)} %fusion.28.value_ref, f32[16,32,256]{2,1,0:T(8,128)S(1)} %constant_dynamic-update-slice_fusion.96.base_ref), custom_call_target="tpu_custom_call" | custom-call | tf_op jit(solution)/shard_map/pallas_call | solution.py:222
  121.0 0.9 copy-done.7
  121.9 0.9 fusion.12
  123.2 0.9 multiply_convert_fusion.2
  124.3 1.0 copy-done.3
  125.3 0.9 fusion.10
  126.6 0.9 fusion.27.value_ref
  127.6 24.6 %shard_map.61 = f32[16,32,256]{2,1,0:T(8,128)S(1)} custom-call(bf16[4,32,256]{2,1,0:T(8,128)(2,1)S(1)} %fusion.27.value_ref, f32[16,32,256]{2,1,0:T(8,128)S(1)} %constant_dynamic-update-slice_fusion.96.base_ref), custom_call_target="tpu_custom_call" | custom-call | tf_op jit(solution)/shard_map/pallas_call | solution.py:222
  152.5 0.9 copy-done.8
  153.5 0.9 fusion.8
  155.1 0.6 copy-done.10
  155.7 2.6 %convolution_convert_fusion.1 = bf16[64,3,3,256]{3,0,2,1:T(8,128)(2,1)S(1)} fusion(bf16[1,16,32,256]{3,2,1,0:T(8,128)(2,1)S(1)} %copy-done.10, bf16[1,16,32,64]{3,2,1,0:T(8,128)(2,1)S(1)} %get-tuple-element.24), kind=kOutput, calls=%fused_computation.11 | convolution fusion | flops 141836288 | bytes 622592 | tf_op jit(solution)/shard_map/transpose | solution.py:293
  158.8 2.6 %convolution_convert_fusion = bf16[64,3,3,256]{3,0,2,1:T(8,128)(2,1)S(1)} fusion(bf16[1,16,32,256]{3,2,1,0:T(8,128)(2,1)S(1)} %bitcast.411, bf16[1,16,32,64]{3,2,1,0:T(8,128)(2,1)S(1)} %get-tuple-element.23), kind=kOutput, calls=%fused_computation.10 | convolution fusion | flops 141836288 | bytes 622592 | tf_op jit(solution)/shard_map/transpose | solution.py:293
  162.1 0.6 copy-done.4
  162.6 0.9 fusion.6
  163.9 1.2 copy.47
  165.4 2.2 %pad_maximum_fusion = bf16[64,2,9,256]{3,1,2,0:T(2,128)(2,1)} fusion(bf16[64,1,9,256]{3,1,2,0:T(2,128)(2,1)S(1)} %copy.67, bf16[64,1,9,256]{3,1,2,0:T(2,128)(2,1)S(1)} %copy.66), kind=kLoop, calls=%fused_computation.12 | loop fusion | flops 1179648 | bytes 1179648 | tf_op jit(solution)/shard_map/stack | solution.py:294
  167.5 1.6 fusion.26
  (163 shorter events, 9.7 us)
Async XLA Ops:
  0.6 10.8 %collective-permute-start = (f32[4,32,256]{2,1,0:T(8,128)}, f32[4,32,256]{2,1,0:T(8,128)S(1)}, u32[]{:S(2)}, u32[]{:S(2)}) collective-permute-start(f32[4,32,256]{2,1,0:T(8,128)} %param.3), channel_id=1, source_target_pairs={{0,1},{1,2},{2,3},{3,0},{4,5},{5,6},{6,7},{7,4},{8,9},{9,10},{10,1... | collective-permute-start | bytes 393224 | tf_op jit(solution)/shard_map/ppermute | solution.py:253
  3.7 8.3 %collective-permute-start.2 = (f32[4,32,256]{2,1,0:T(8,128)}, f32[4,32,256]{2,1,0:T(8,128)S(1)}, u32[]{:S(2)}, u32[]{:S(2)}) collective-permute-start(f32[4,32,256]{2,1,0:T(8,128)} %param.3), channel_id=1, source_target_pairs={{0,3},{1,0},{2,1},{3,2},{4,7},{5,4},{6,5},{7,6},{8,11},{9,8},{10,9... | collective-permute-start | bytes 393224 | tf_op jit(solution)/shard_map/ppermute | solution.py:253
  4.0 7.9 %collective-permute-start.1 = (f32[4,32,256]{2,1,0:T(8,128)}, f32[4,32,256]{2,1,0:T(8,128)S(1)}, u32[]{:S(2)}, u32[]{:S(2)}) collective-permute-start(f32[4,32,256]{2,1,0:T(8,128)} %param.3), channel_id=1, source_target_pairs={{0,2},{1,3},{2,0},{3,1},{4,6},{5,7},{6,4},{7,5},{8,10},{9,11},{10,... | collective-permute-start | bytes 393224 | tf_op jit(solution)/shard_map/ppermute | solution.py:253
  5.3 77.4 %collective-permute-start.3 = (f32[4,32,256]{2,1,0:T(8,128)}, f32[4,32,256]{2,1,0:T(8,128)}, u32[]{:S(2)}, u32[]{:S(2)}) collective-permute-start(f32[4,32,256]{2,1,0:T(8,128)} %param.5), channel_id=1, source_target_pairs={{0,1},{1,2},{2,3},{3,0},{4,5},{5,6},{6,7},{7,4},{8,9},{9,10},{10,1... | collective-permute-start | bytes 393224 | tf_op jit(solution)/shard_map/ppermute | solution.py:253
  7.3 79.2 %collective-permute-start.5 = (f32[4,32,256]{2,1,0:T(8,128)}, f32[4,32,256]{2,1,0:T(8,128)}, u32[]{:S(2)}, u32[]{:S(2)}) collective-permute-start(f32[4,32,256]{2,1,0:T(8,128)} %param.5), channel_id=1, source_target_pairs={{0,3},{1,0},{2,1},{3,2},{4,7},{5,4},{6,5},{7,6},{8,11},{9,8},{10,9... | collective-permute-start | bytes 393224 | tf_op jit(solution)/shard_map/ppermute | solution.py:253
  7.3 2.9 %copy-start.11 = (f32[4,32,256]{2,1,0:T(8,128)S(1)}, f32[4,32,256]{2,1,0:T(8,128)}, u32[]{:S(2)}) copy-start(f32[4,32,256]{2,1,0:T(8,128)} %param.3) | copy-start | bytes 393220
  10.2 33.8 %copy-start = (bf16[1,9,256,256]{3,2,1,0:T(8,128)(2,1)}, bf16[1,9,256,256]{3,2,1,0:T(8,128)(2,1)S(1)}, u32[]{:S(2)}) copy-start(bf16[1,9,256,256]{3,2,1,0:T(8,128)(2,1)S(1)} %get-tuple-element.15) | copy-start | bytes 3538948
  11.5 74.1 %collective-permute-start.4 = (f32[4,32,256]{2,1,0:T(8,128)}, f32[4,32,256]{2,1,0:T(8,128)}, u32[]{:S(2)}, u32[]{:S(2)}) collective-permute-start(f32[4,32,256]{2,1,0:T(8,128)} %param.5), channel_id=1, source_target_pairs={{0,2},{1,3},{2,0},{3,1},{4,6},{5,7},{6,4},{7,5},{8,10},{9,11},{10,... | collective-permute-start | bytes 393224 | tf_op jit(solution)/shard_map/ppermute | solution.py:253
  13.7 1.3 copy-start.5
  46.1 1.3 copy-start.6
  75.7 1.3 copy-start.1
  82.0 1.7 copy-start.9
  89.2 1.3 copy-start.2
  120.6 1.3 copy-start.7
  124.1 1.3 copy-start.3
  152.2 1.3 copy-start.8
  154.8 1.0 copy-start.10
  161.4 1.3 copy-start.4

commit v2 on v1

--- a/solution.py
+++ b/solution.py
@@ -11,6 +11,7 @@
 
 ITERS = 2
 RADIX = 4
+PIECES = 2
 
 step_size = 0.125
 
@@ -110,12 +111,13 @@
 
 
 def scan_kernel(
-    n_layer, n_space, reverse, value_ref, base_ref, out_ref,
+    n_layer, n_space, n_piece, reverse, value_ref, base_ref, out_ref,
     slots, gathered, group_buf, mine, total, send_sems, recv_sems, gsend, grecv,
 ):
     layer = lax.axis_index("layer")
     space = lax.axis_index("space")
     rows = value_ref.shape[0]
+    part_rows = rows // n_piece
     strides = []
     stride = 1
     while stride < n_layer:
@@ -135,78 +137,108 @@
         pl.semaphore_signal(barrier, inc=1, device_id=partner, device_id_type=MESH)
     pl.semaphore_wait(barrier, len(partners))
 
-    total[...] = jnp.zeros(total.shape, jnp.float32)
+    for piece in range(n_piece):
+        total[piece] = jnp.zeros(total.shape[1:], jnp.float32)
     pending = []
-    source = value_ref
-    for stage, stride in enumerate(strides):
+    sources = [value_ref.at[pl.ds(piece * part_rows, part_rows)] for piece in range(n_piece)]
+    in_flight = {}
+
+    def issue(piece, stage):
+        if stage == len(strides):
+            copies = []
+            for shift in range(1, n_space):
+                copy = pltpu.make_async_remote_copy(
+                    src_ref=mine.at[piece],
+                    dst_ref=gathered.at[piece, shift - 1],
+                    send_sem=gsend.at[piece, shift - 1],
+                    recv_sem=grecv.at[piece, shift - 1],
+                    device_id=(layer, (space + shift) % n_space),
+                    device_id_type=MESH,
+                )
+                copy.start()
+                copies.append(copy)
+                pending.append((copy, None))
+            in_flight[piece] = copies
+            return
         last = stage + 1 == len(strides)
+        stride = strides[stage]
         digit = (layer // stride) % RADIX
         base = layer - digit * stride
         copies = []
         for shift in range(1, RADIX):
             copy = pltpu.make_async_remote_copy(
-                src_ref=source,
-                dst_ref=slots.at[stage, shift - 1],
-                send_sem=send_sems.at[stage, shift - 1],
-                recv_sem=recv_sems.at[stage, shift - 1],
+                src_ref=sources[piece],
+                dst_ref=slots.at[piece, stage, shift - 1],
+                send_sem=send_sems.at[piece, stage, shift - 1],
+                recv_sem=recv_sems.at[piece, stage, shift - 1],
                 device_id=(base + ((digit + shift) % RADIX) * stride, space),
                 device_id_type=MESH,
             )
             wraps = digit + shift >= RADIX
             sends = (wraps if reverse else jnp.logical_not(wraps)) if last else None
             gets = (shift > digit if reverse else shift <= digit) if last else None
-            copies.append((copy, sends, gets))
             if last:
                 pl.when(sends)(copy.start)
             else:
                 copy.start()
-        for shift, (copy, sends, gets) in zip(range(1, RADIX), copies):
+            copies.append((copy, gets))
+            pending.append((copy, sends))
+        in_flight[piece] = copies
+
+    def finish(piece, stage):
+        first = piece * part_rows
+        if stage == len(strides):
+            for copy in in_flight[piece]:
+                copy.wait_recv()
+            for shift in range(1, n_space):
+                origin = (space + n_space - shift) % n_space
+                there = pl.ds(origin * rows + first, part_rows)
+                out_ref[there] = base_ref[there] + gathered[piece, shift - 1].astype(
+                    jnp.float32
+                )
+            return
+        last = stage + 1 == len(strides)
+        stride = strides[stage]
+        digit = (layer // stride) % RADIX
+        for copy, gets in in_flight[piece]:
             if last:
                 pl.when(gets)(copy.wait_recv)
             else:
                 copy.wait_recv()
-            pending.append((copy, sends))
-        group = source[...].astype(jnp.float32)
+        group = sources[piece][...].astype(jnp.float32)
         for shift in range(1, RADIX):
             earlier = shift > digit if reverse else shift <= digit
 
             @pl.when(earlier)
             def _():
-                total[...] += slots[stage, shift - 1].astype(jnp.float32)
+                total[piece] += slots[piece, stage, shift - 1].astype(jnp.float32)
 
             if not last:
-                group = group + slots[stage, shift - 1].astype(jnp.float32)
+                group = group + slots[piece, stage, shift - 1].astype(jnp.float32)
         if not last:
-            group_buf[stage] = group.astype(group_buf.dtype)
-            source = group_buf.at[stage]
-
-    mine[...] = total[...].astype(mine.dtype)
-    copies = []
-    for shift in range(1, n_space):
-        copy = pltpu.make_async_remote_copy(
-            src_ref=mine,
-            dst_ref=gathered.at[shift - 1],
-            send_sem=gsend.at[shift - 1],
-            recv_sem=grecv.at[shift - 1],
-            device_id=(layer, (space + shift) % n_space),
-            device_id_type=MESH,
-        )
-        copy.start()
-        copies.append(copy)
-    here = pl.ds(space * rows, rows)
-    out_ref[here] = base_ref[here] + total[...]
-    for copy in copies:
-        copy.wait_recv()
-    for shift in range(1, n_space):
-        there = pl.ds(((space + n_space - shift) % n_space) * rows, rows)
-        out_ref[there] = base_ref[there] + gathered[shift - 1].astype(jnp.float32)
+            group_buf[piece, stage] = group.astype(group_buf.dtype)
+            sources[piece] = group_buf.at[piece, stage]
+        else:
+            mine[piece] = total[piece].astype(mine.dtype)
+            here = pl.ds(space * rows + first, part_rows)
+            out_ref[here] = base_ref[here] + total[piece]
+
+    phases = len(strides) + 1
+    for step in range(phases + n_piece - 1):
+        active = [
+            (piece, step - piece)
+            for piece in range(n_piece)
+            if 0 <= step - piece < phases
+        ]
+        for piece, stage in active:
+            issue(piece, stage)
+        for piece, stage in active:
+            finish(piece, stage)
     for copy, sends in pending:
         if sends is None:
             copy.wait_send()
         else:
             pl.when(sends)(copy.wait_send)
-    for copy in copies:
-        copy.wait_send()
 
 
 def scan_and_gather(value, base, reverse, collective_id):
@@ -217,23 +249,24 @@
         stages += 1
     assert RADIX ** stages == n_layer
     rows, width, channels = value.shape
-    piece = (rows, width, channels)
+    n_piece = PIECES if rows % PIECES == 0 else 1
+    piece = (rows // n_piece, width, channels)
     link = jnp.bfloat16
     return pl.pallas_call(
-        functools.partial(scan_kernel, n_layer, n_space, reverse),
+        functools.partial(scan_kernel, n_layer, n_space, n_piece, reverse),
         out_shape=jax.ShapeDtypeStruct((n_space * rows, width, channels), jnp.float32),
         in_specs=[pl.BlockSpec(memory_space=pltpu.VMEM)] * 2,
         out_specs=pl.BlockSpec(memory_space=pltpu.VMEM),
         scratch_shapes=[
-            pltpu.VMEM((stages, RADIX - 1) + piece, link),
-            pltpu.VMEM((n_space - 1,) + piece, link),
-            pltpu.VMEM((max(stages - 1, 1),) + piece, link),
-            pltpu.VMEM(piece, link),
-            pltpu.VMEM(piece, jnp.float32),
-            pltpu.SemaphoreType.DMA((stages, RADIX - 1)),
-            pltpu.SemaphoreType.DMA((stages, RADIX - 1)),
-            pltpu.SemaphoreType.DMA((n_space - 1,)),
-            pltpu.SemaphoreType.DMA((n_space - 1,)),
+            pltpu.VMEM((n_piece, stages, RADIX - 1) + piece, link),
+            pltpu.VMEM((n_piece, n_space - 1) + piece, link),
+            pltpu.VMEM((n_piece, max(stages - 1, 1)) + piece, link),
+            pltpu.VMEM((n_piece,) + piece, link),
+            pltpu.VMEM((n_piece,) + piece, jnp.float32),
+            pltpu.SemaphoreType.DMA((n_piece, stages, RADIX - 1)),
+            pltpu.SemaphoreType.DMA((n_piece, stages, RADIX - 1)),
+            pltpu.SemaphoreType.DMA((n_piece, n_space - 1)),
+            pltpu.SemaphoreType.DMA((n_piece, n_space - 1)),
         ],
         compiler_params=pltpu.CompilerParams(
             collective_id=collective_id,

time: 170 us -> 172 us (1.012)
  Pallas kernels: 104 us -> 106 us
    pallas_call x4, Pallas kernels: 104 us -> 106 us  [scan_and_gather(): pl.pallas_call(functools.partial(scan_kernel, n_layer, n_space, n_piece,...]
  transfers between devices with their start and end apart: 6 -> 6, of which waited for: 1 -> 1; matrix products, arithmetic and copies ran while one was open for 14% -> 14% of each run, Pallas kernels for 30% -> 32%
where the time goes in v2:
time: 172 us; the launch traced here: 171 us
  Pallas kernels  106 us (62%)
  local copies, waits for them, and re-layouts  27.4 us (16%)
  matrix products  17.4 us (10%)
  other arithmetic  10.9 us (6%)
  starting transfers between devices  6.9 us (4%)
  between operations  1.97 us (1%)
    pallas_call x4, Pallas kernels, scan_and_gather(): pl.pallas_call(functools.partial(scan_kernel, n_layer, n_space, n_piece,...  106 us
    conv_general_dilated x12, matrix products, chunked_conv(): lax.conv_general_dilated(column_chunks(low), kernel3, (1, 1), ((1, 1), (0...  12.2 us
    unnamed x108, local copies, waits for them, and re-layouts  10.1 us
    ppermute x6, starting transfers between devices, gather_space(): lax.ppermute(piece, 'space', [(i, (i + shift) % count) for i in range(cou...  6.9 us
    transpose x2, matrix products, on_device(): jnp.transpose(grad, (3, 1, 2, 0)).reshape(quarter, 9, channels)  5.2 us
    mul x12, local copies, waits for them, and re-layouts, forward_block(): current = current + step_size * squashed  4.97 us
  transfers between devices with their start and end apart: 6, of which 1 were waited for; matrix products, arithmetic and copies ran while one was open for 14% of the time, Pallas kernels for 32%

profile of v2, /device:TPU:1, one launch (start us, length us, event | category | flops | bytes accessed | tf_op | source)
XLA Modules:
  0.0 171.0 jit_solution(3714242072632533302)
XLA Ops:
  0.6 3.1 %collective-permute-start = (f32[4,32,256]{2,1,0:T(8,128)}, f32[4,32,256]{2,1,0:T(8,128)S(1)}, u32[]{:S(2)}, u32[]{:S(2)}) collective-permute-start(f32[4,32,256]{2,1,0:T(8,128)} %param.3), channel_id=1, source_target_pairs={{0,1},{1,2},{2,3},{3,0},{4,5},{5,6},{6,7},{7,4},{8,9},{9,10},{10,1... | collective-permute-start | bytes 393224 | tf_op jit(solution)/shard_map/ppermute | solution.py:286
  4.0 1.3 collective-permute-start.1
  5.3 2.0 %collective-permute-start.3 = (f32[4,32,256]{2,1,0:T(8,128)}, f32[4,32,256]{2,1,0:T(8,128)}, u32[]{:S(2)}, u32[]{:S(2)}) collective-permute-start(f32[4,32,256]{2,1,0:T(8,128)} %param.5), channel_id=1, source_target_pairs={{0,1},{1,2},{2,3},{3,0},{4,5},{5,6},{6,7},{7,4},{8,9},{9,10},{10,1... | collective-permute-start | bytes 393224 | tf_op jit(solution)/shard_map/ppermute | solution.py:286
  7.3 2.9 %fusion.59 = (bf16[1,9,256,256]{3,2,1,0:T(8,128)(2,1)S(1)}, bf16[1,9,256,256]{3,2,1,0:T(8,128)(2,1)}) fusion(bf16[2,9,256,256]{3,2,1,0:T(8,128)(2,1)} %param.4), kind=kLoop, calls=%fused_computation.290 | loop fusion | bytes 4718592 | tf_op jit(solution)/shard_map/unstack | solution.py:301
  10.3 1.1 constant_dynamic-update-slice_fusion.99
  12.3 0.9 fusion.3
  13.9 1.0 copy-done.5
  15.0 0.9 fusion.2
  16.0 1.0 mul.110
  17.0 0.9 fusion.31.value_ref
  17.9 29.3 %shard_map.58 = f32[16,32,256]{2,1,0:T(8,128)S(1)} custom-call(bf16[4,32,256]{2,1,0:T(8,128)(2,1)S(1)} %fusion.31.value_ref, f32[16,32,256]{2,1,0:T(8,128)S(1)} %constant_dynamic-update-slice_fusion.100.base_ref), custom_call_target="tpu_custom_call" | custom-call | tf_op jit(solution)/shard_map/pallas_call | solution.py:255
  47.6 0.9 fusion.1
  48.8 0.9 fusion.57
  50.0 1.0 copy-done.6
  51.0 0.9 fusion
  52.1 1.0 mul.114
  53.1 1.0 fusion.30.value_ref
  54.1 24.9 %shard_map.59 = f32[16,32,256]{2,1,0:T(8,128)S(1)} custom-call(bf16[4,32,256]{2,1,0:T(8,128)(2,1)S(1)} %fusion.30.value_ref, f32[16,32,256]{2,1,0:T(8,128)S(1)} %constant_dynamic-update-slice_fusion.100.base_ref), custom_call_target="tpu_custom_call" | custom-call | tf_op jit(solution)/shard_map/pallas_call | solution.py:255
  79.3 1.0 copy-done.1
  80.3 1.7 subtract_multiply_fusion
  82.3 0.9 fusion.56
  83.5 1.9 %subtract_multiply_fusion.1 = (f32[16,8,4,256]{3,1,2,0:T(8,128)}, f32[16,8,4,256]{3,1,2,0:T(8,128)}) fusion(bf16[3,3,256,256]{3,2,1,0:T(8,128)(2,1)S(1)} %bitcast.420, bf16[16,8,6,256]{3,2,0,1:T(8,128)(2,1)S(1)} %constant_dynamic-update-slice_fusion.40), kind=kOutput, calls=%fused_computation.20 | convolution fusion | flops 579338240 | bytes 2621440 | tf_op jit(solution)/shard_map/conv_general_dilated | solution.py:32
  85.4 0.7 convert_bitcast_fusion
  86.1 0.9 constant_dynamic-update-slice_fusion.98
  87.4 1.2 copy.48
  88.9 0.9 constant_dynamic-update-slice_fusion.97
  89.8 0.9 constant_dynamic-update-slice_fusion.96.base_ref
  91.1 0.9 fusion.16
  92.8 1.0 copy-done.2
  93.8 0.9 fusion.14
  95.1 27.1 %shard_map.60 = f32[16,32,256]{2,1,0:T(8,128)S(1)} custom-call(bf16[4,32,256]{2,1,0:T(8,128)(2,1)S(1)} %fusion.28.value_ref, f32[16,32,256]{2,1,0:T(8,128)S(1)} %constant_dynamic-update-slice_fusion.96.base_ref), custom_call_target="tpu_custom_call" | custom-call | tf_op jit(solution)/shard_map/pallas_call | solution.py:255
  122.5 0.9 copy-done.7
  123.5 0.9 fusion.12
  124.8 0.9 multiply_convert_fusion.2
  125.9 1.0 copy-done.3
  126.9 0.9 fusion.10
  128.2 0.9 fusion.27.value_ref
  129.2 24.8 %shard_map.61 = f32[16,32,256]{2,1,0:T(8,128)S(1)} custom-call(bf16[4,32,256]{2,1,0:T(8,128)(2,1)S(1)} %fusion.27.value_ref, f32[16,32,256]{2,1,0:T(8,128)S(1)} %constant_dynamic-update-slice_fusion.96.base_ref), custom_call_target="tpu_custom_call" | custom-call | tf_op jit(solution)/shard_map/pallas_call | solution.py:255
  154.3 0.9 copy-done.8
  155.3 0.9 fusion.8
  156.9 0.6 copy-done.10
  157.5 2.6 %convolution_convert_fusion.1 = bf16[64,3,3,256]{3,0,2,1:T(8,128)(2,1)S(1)} fusion(bf16[1,16,32,256]{3,2,1,0:T(8,128)(2,1)S(1)} %copy-done.10, bf16[1,16,32,64]{3,2,1,0:T(8,128)(2,1)S(1)} %get-tuple-element.24), kind=kOutput, calls=%fused_computation.11 | convolution fusion | flops 141836288 | bytes 622592 | tf_op jit(solution)/shard_map/transpose | solution.py:326
  160.6 2.6 %convolution_convert_fusion = bf16[64,3,3,256]{3,0,2,1:T(8,128)(2,1)S(1)} fusion(bf16[1,16,32,256]{3,2,1,0:T(8,128)(2,1)S(1)} %bitcast.411, bf16[1,16,32,64]{3,2,1,0:T(8,128)(2,1)S(1)} %get-tuple-element.23), kind=kOutput, calls=%fused_computation.10 | convolution fusion | flops 141836288 | bytes 622592 | tf_op jit(solution)/shard_map/transpose | solution.py:326
  163.9 0.6 copy-done.4
  164.4 0.9 fusion.6
  165.7 1.2 copy.47
  167.2 2.2 %pad_maximum_fusion = bf16[64,2,9,256]{3,1,2,0:T(2,128)(2,1)} fusion(bf16[64,1,9,256]{3,1,2,0:T(2,128)(2,1)S(1)} %copy.67, bf16[64,1,9,256]{3,1,2,0:T(2,128)(2,1)S(1)} %copy.66), kind=kLoop, calls=%fused_computation.12 | loop fusion | flops 1179648 | bytes 1179648 | tf_op jit(solution)/shard_map/stack | solution.py:327
  169.3 1.6 fusion.26
  (163 shorter events, 9.7 us)
Async XLA Ops:
  0.6 10.8 %collective-permute-start = (f32[4,32,256]{2,1,0:T(8,128)}, f32[4,32,256]{2,1,0:T(8,128)S(1)}, u32[]{:S(2)}, u32[]{:S(2)}) collective-permute-start(f32[4,32,256]{2,1,0:T(8,128)} %param.3), channel_id=1, source_target_pairs={{0,1},{1,2},{2,3},{3,0},{4,5},{5,6},{6,7},{7,4},{8,9},{9,10},{10,1... | collective-permute-start | bytes 393224 | tf_op jit(solution)/shard_map/ppermute | solution.py:286
  3.7 8.3 %collective-permute-start.2 = (f32[4,32,256]{2,1,0:T(8,128)}, f32[4,32,256]{2,1,0:T(8,128)S(1)}, u32[]{:S(2)}, u32[]{:S(2)}) collective-permute-start(f32[4,32,256]{2,1,0:T(8,128)} %param.3), channel_id=1, source_target_pairs={{0,3},{1,0},{2,1},{3,2},{4,7},{5,4},{6,5},{7,6},{8,11},{9,8},{10,9... | collective-permute-start | bytes 393224 | tf_op jit(solution)/shard_map/ppermute | solution.py:286
  4.0 7.9 %collective-permute-start.1 = (f32[4,32,256]{2,1,0:T(8,128)}, f32[4,32,256]{2,1,0:T(8,128)S(1)}, u32[]{:S(2)}, u32[]{:S(2)}) collective-permute-start(f32[4,32,256]{2,1,0:T(8,128)} %param.3), channel_id=1, source_target_pairs={{0,2},{1,3},{2,0},{3,1},{4,6},{5,7},{6,4},{7,5},{8,10},{9,11},{10,... | collective-permute-start | bytes 393224 | tf_op jit(solution)/shard_map/ppermute | solution.py:286
  5.3 80.8 %collective-permute-start.3 = (f32[4,32,256]{2,1,0:T(8,128)}, f32[4,32,256]{2,1,0:T(8,128)}, u32[]{:S(2)}, u32[]{:S(2)}) collective-permute-start(f32[4,32,256]{2,1,0:T(8,128)} %param.5), channel_id=1, source_target_pairs={{0,1},{1,2},{2,3},{3,0},{4,5},{5,6},{6,7},{7,4},{8,9},{9,10},{10,1... | collective-permute-start | bytes 393224 | tf_op jit(solution)/shard_map/ppermute | solution.py:286
  7.3 82.5 %collective-permute-start.5 = (f32[4,32,256]{2,1,0:T(8,128)}, f32[4,32,256]{2,1,0:T(8,128)}, u32[]{:S(2)}, u32[]{:S(2)}) collective-permute-start(f32[4,32,256]{2,1,0:T(8,128)} %param.5), channel_id=1, source_target_pairs={{0,3},{1,0},{2,1},{3,2},{4,7},{5,4},{6,5},{7,6},{8,11},{9,8},{10,9... | collective-permute-start | bytes 393224 | tf_op jit(solution)/shard_map/ppermute | solution.py:286
  7.3 2.9 %copy-start.11 = (f32[4,32,256]{2,1,0:T(8,128)S(1)}, f32[4,32,256]{2,1,0:T(8,128)}, u32[]{:S(2)}) copy-start(f32[4,32,256]{2,1,0:T(8,128)} %param.3) | copy-start | bytes 393220
  10.2 37.3 %copy-start = (bf16[1,9,256,256]{3,2,1,0:T(8,128)(2,1)}, bf16[1,9,256,256]{3,2,1,0:T(8,128)(2,1)S(1)}, u32[]{:S(2)}) copy-start(bf16[1,9,256,256]{3,2,1,0:T(8,128)(2,1)S(1)} %get-tuple-element.15) | copy-start | bytes 3538948
  11.5 77.4 %collective-permute-start.4 = (f32[4,32,256]{2,1,0:T(8,128)}, f32[4,32,256]{2,1,0:T(8,128)}, u32[]{:S(2)}, u32[]{:S(2)}) collective-permute-start(f32[4,32,256]{2,1,0:T(8,128)} %param.5), channel_id=1, source_target_pairs={{0,2},{1,3},{2,0},{3,1},{4,6},{5,7},{6,4},{7,5},{8,10},{9,11},{10,... | collective-permute-start | bytes 393224 | tf_op jit(solution)/shard_map/ppermute | solution.py:286
  13.7 1.3 copy-start.5
  49.7 1.3 copy-start.6
  79.0 1.3 copy-start.1
  85.4 1.7 copy-start.9
  92.5 1.3 copy-start.2
  122.2 1.3 copy-start.7
  125.7 1.3 copy-start.3
  154.0 1.3 copy-start.8
  156.5 1.0 copy-start.10
  163.2 1.3 copy-start.4

commit v3 on v1

--- a/solution.py
+++ b/solution.py
@@ -53,7 +53,7 @@
         signal[None],
         (1, 1),
         ((1, 1), (1, 1)),
-        dimension_numbers=("CHWN", "IHWO", "NHWC"),
+        dimension_numbers=("CHWN", "IHWO", "CHWN"),
         preferred_element_type=jnp.float32,
     )
 
@@ -249,10 +249,11 @@
     rows = piece.shape[0]
     whole = jnp.zeros((count * rows,) + piece.shape[1:], piece.dtype)
     whole = lax.dynamic_update_slice_in_dim(whole, piece, place * rows, 0)
+    low = piece.astype(jnp.bfloat16)
     for shift in range(1, count):
         part = lax.ppermute(
-            piece, "space", [(i, (i + shift) % count) for i in range(count)]
-        )
+            low, "space", [(i, (i + shift) % count) for i in range(count)]
+        ).astype(piece.dtype)
         source = (place + count - shift) % count
         whole = lax.dynamic_update_slice_in_dim(whole, part, source * rows, 0)
     return whole
@@ -290,7 +291,7 @@
     for low, scaled in zip(inputs_low, scaled_list):
         signal = lax.dynamic_slice_in_dim(scaled, first, quarter, 2)
         grad = kernel_gradient(low, signal)
-        pieces.append(jnp.transpose(grad, (3, 1, 2, 0)).reshape(quarter, 9, channels))
+        pieces.append(grad.reshape(quarter, 9, channels))
     weight_grad = jnp.stack(pieces, axis=1).astype(jnp.bfloat16)
     return (own_rows(outputs, rows)[None], own_rows(begins, rows)[None], weight_grad)
 

time: 170 us -> 176 us (1.035)
  Pallas kernels: 104 us -> 107 us
  waiting for transfers between devices: 0.29 us -> 3.14 us
    transpose x2 -> x0, matrix products: 5.2 us -> none  [on_device(): jnp.transpose(grad, (3, 1, 2, 0)).reshape(quarter, 9, channels)]
    conv_general_dilated x0 -> x2, matrix products: none -> 5.17 us  [kernel_gradient(): lax.conv_general_dilated(low[None], signal[None], (1, 1), ((1, 1), (1, 1)...]
    dynamic_update_slice x8 -> x0, local copies, waits for them, and re-layouts: 3.88 us -> none  [the longest x6 2.8 us: gather_space(): whole = lax.dynamic_update_slice_in_dim(whole, part, source * rows, 0)]
    ppermute x6, waiting for transfers between devices: 0.29 us -> 3.14 us  [gather_space(): lax.ppermute(low, 'space', [(i, (i + shift) % count) for i in range(count)])]
    unnamed x108 -> x110, local copies, waits for them, and re-layouts: 10.1 us -> 12.7 us
    pallas_call x4, Pallas kernels: 104 us -> 107 us  [scan_and_gather(): pl.pallas_call(functools.partial(scan_kernel, n_layer, n_space, reverse),...]
  transfers between devices with their start and end apart: 6 -> 6, of which waited for: 1 -> 2; matrix products, arithmetic and copies ran while one was open for 14% -> 2% of each run, Pallas kernels for 30% -> 0%
where the time goes in v3:
time: 176 us; the launch traced here: 175 us
  Pallas kernels  107 us (61%)
  local copies, waits for them, and re-layouts  25.7 us (15%)
  matrix products  18.3 us (10%)
  other arithmetic  12.6 us (7%)
  starting transfers between devices  6.99 us (4%)
  waiting for transfers between devices  3.14 us (2%)
  between operations  1.91 us (1%)
    pallas_call x4, Pallas kernels, scan_and_gather(): pl.pallas_call(functools.partial(scan_kernel, n_layer, n_space, reverse),...  107 us
    conv_general_dilated x12, matrix products, chunked_conv(): lax.conv_general_dilated(column_chunks(low), kernel3, (1, 1), ((1, 1), (0...  13.2 us
    unnamed x110, local copies, waits for them, and re-layouts  12.7 us
    ppermute x6, starting transfers between devices, gather_space(): lax.ppermute(low, 'space', [(i, (i + shift) % count) for i in range(count)])  6.99 us
    conv_general_dilated x2, matrix products, kernel_gradient(): lax.conv_general_dilated(low[None], signal[None], (1, 1), ((1, 1), (1, 1)...  5.17 us
    mul x12, local copies, waits for them, and re-layouts, forward_block(): current = current + step_size * squashed  3.92 us
  transfers between devices with their start and end apart: 6, of which 2 were waited for; matrix products, arithmetic and copies ran while one was open for 2% of the time, Pallas kernels for 0%

profile of v3, /device:TPU:1, one launch (start us, length us, event | category | flops | bytes accessed | tf_op | source)
XLA Modules:
  0.0 175.4 jit_solution(1809616537079971783)
XLA Ops:
  0.7 1.0 fusion.60
  1.7 3.1 %collective-permute-start.3 = (bf16[4,32,256]{2,1,0:T(8,128)(2,1)S(1)}, bf16[4,32,256]{2,1,0:T(8,128)(2,1)S(1)}, u32[]{:S(2)}, u32[]{:S(2)}) collective-permute-start(bf16[4,32,256]{2,1,0:T(8,128)(2,1)S(1)} %get-tuple-element.21), channel_id=1, source_target_pairs={{0,1},{1,2},{2,3},{3,0},{4,5},{5,6},{6,7},{7,4},{8,9},{9,10},{10,1... | collective-permute-start | bytes 196616 | tf_op jit(solution)/shard_map/ppermute | solution.py:254
  4.8 1.6 collective-permute-start.4
  6.5 1.8 %collective-permute-start = (bf16[4,32,256]{2,1,0:T(8,128)(2,1)S(1)}, bf16[4,32,256]{2,1,0:T(8,128)(2,1)S(1)}, u32[]{:S(2)}, u32[]{:S(2)}) collective-permute-start(bf16[4,32,256]{2,1,0:T(8,128)(2,1)S(1)} %get-tuple-element.23), channel_id=1, source_target_pairs={{0,1},{1,2},{2,3},{3,0},{4,5},{5,6},{6,7},{7,4},{8,9},{9,10},{10,1... | collective-permute-start | bytes 196616 | tf_op jit(solution)/shard_map/ppermute | solution.py:254
  8.3 2.8 %fusion.59 = (bf16[1,9,256,256]{3,2,1,0:T(8,128)(2,1)S(1)}, bf16[1,9,256,256]{3,2,1,0:T(8,128)(2,1)}) fusion(bf16[2,9,256,256]{3,2,1,0:T(8,128)(2,1)} %param.4), kind=kLoop, calls=%fused_computation.290 | loop fusion | bytes 4718592 | tf_op jit(solution)/shard_map/unstack | solution.py:269
  11.7 0.8 collective-permute-done.1
  12.6 2.3 %collective-permute-done.2 = bf16[4,32,256]{2,1,0:T(8,128)(2,1)S(1)} collective-permute-done((bf16[4,32,256]{2,1,0:T(8,128)(2,1)S(1)}, bf16[4,32,256]{2,1,0:T(8,128)(2,1)S(1)}, u32[]{:S(2)}, u32[]{:S(2)}) %collective-permute-start.2) | collective-permute-done | bytes 65568 | tf_op jit(solution)/shard_map/ppermute | solution.py:254
  15.2 0.9 fusion.3
  16.8 1.0 copy-done.5
  17.8 0.9 fusion.2
  18.9 1.0 mul.110
  19.9 0.9 fusion.31.value_ref
  20.8 28.1 %shard_map.58 = f32[16,32,256]{2,1,0:T(8,128)S(1)} custom-call(bf16[4,32,256]{2,1,0:T(8,128)(2,1)S(1)} %fusion.31.value_ref, f32[16,32,256]{2,1,0:T(8,128)S(1)} %get-tuple-element.26.base_ref), custom_call_target="tpu_custom_call" | custom-call | tf_op jit(solution)/shard_map/pallas_call | solution.py:222
  49.2 0.9 fusion.1
  50.5 0.9 fusion.57
  51.6 1.0 copy-done.6
  52.6 0.9 fusion
  53.7 1.0 mul.114
  54.7 1.0 fusion.30.value_ref
  55.7 24.7 %shard_map.59 = f32[16,32,256]{2,1,0:T(8,128)S(1)} custom-call(bf16[4,32,256]{2,1,0:T(8,128)(2,1)S(1)} %fusion.30.value_ref, f32[16,32,256]{2,1,0:T(8,128)S(1)} %get-tuple-element.26.base_ref), custom_call_target="tpu_custom_call" | custom-call | tf_op jit(solution)/shard_map/pallas_call | solution.py:222
  80.5 0.7 convert_bitcast_fusion
  81.8 1.7 subtract_multiply_fusion
  83.9 0.9 fusion.56
  85.0 1.9 %subtract_multiply_fusion.1 = (f32[16,8,4,256]{3,1,2,0:T(8,128)}, f32[16,8,4,256]{3,1,2,0:T(8,128)}) fusion(bf16[3,3,256,256]{3,2,1,0:T(8,128)(2,1)S(1)} %bitcast.420, bf16[16,8,6,256]{3,2,0,1:T(8,128)(2,1)S(1)} %constant_dynamic-update-slice_fusion.40), kind=kOutput, calls=%fused_computation.20 | convolution fusion | flops 579338240 | bytes 2621440 | tf_op jit(solution)/shard_map/conv_general_dilated | solution.py:31
  87.3 1.2 copy.48
  89.1 0.9 fusion.16
  90.8 1.0 copy-done.2
  91.8 0.9 fusion.14
  93.1 28.7 %shard_map.60 = f32[16,32,256]{2,1,0:T(8,128)S(1)} custom-call(bf16[4,32,256]{2,1,0:T(8,128)(2,1)S(1)} %fusion.28.value_ref, f32[16,32,256]{2,1,0:T(8,128)S(1)} %get-tuple-element.25.base_ref), custom_call_target="tpu_custom_call" | custom-call | tf_op jit(solution)/shard_map/pallas_call | solution.py:222
  122.2 0.9 copy-done.7
  123.1 0.9 fusion.12
  124.4 0.9 multiply_convert_fusion.2
  125.5 1.0 copy-done.3
  126.6 0.9 fusion.10
  127.9 0.9 fusion.27.value_ref
  128.8 25.2 %shard_map.61 = f32[16,32,256]{2,1,0:T(8,128)S(1)} custom-call(bf16[4,32,256]{2,1,0:T(8,128)(2,1)S(1)} %fusion.27.value_ref, f32[16,32,256]{2,1,0:T(8,128)S(1)} %get-tuple-element.25.base_ref), custom_call_target="tpu_custom_call" | custom-call | tf_op jit(solution)/shard_map/pallas_call | solution.py:222
  154.4 0.9 copy-done.8
  155.3 0.9 fusion.8
  158.1 0.7 constant_dynamic-update-slice_fusion.94
  158.7 0.7 constant_dynamic-update-slice_fusion.93
  159.4 0.7 constant_dynamic-update-slice_fusion.92
  161.3 0.7 constant_dynamic-update-slice_fusion.89
  162.6 1.9 %fusion.6 = f32[16,8,4,256]{3,1,2,0:T(8,128)S(1)} fusion(bf16[3,3,256,256]{3,2,1,0:T(8,128)(2,1)S(1)} %bitcast.417, bf16[16,8,6,256]{3,2,0,1:T(8,128)(2,1)} %constant_dynamic-update-slice_fusion.88), kind=kOutput, calls=%fused_computation.23 | convolution fusion | flops 578813952 | bytes 2097152 | tf_op jit(solution)/shard_map/conv_general_dilated | solution.py:31
  164.9 2.5 %convolution_convert_fusion = bf16[64,3,3,256]{3,0,2,1:T(8,128)(2,1)S(1)} fusion(bf16[1,16,32,256]{3,2,1,0:T(8,128)(2,1)S(1)} %bitcast.411, bf16[1,16,32,64]{3,2,1,0:T(8,128)(2,1)S(1)} %dynamic-slice_bitcast_fusion), kind=kOutput, calls=%fused_computation.10 | convolution fusion | flops 141836288 | bytes 622592 | tf_op jit(solution)/shard_map/conv_general_dilated | solution.py:51
  167.9 2.6 %convolution_convert_fusion.1 = bf16[64,3,3,256]{3,0,2,1:T(8,128)(2,1)S(1)} fusion(bf16[1,16,32,256]{3,2,1,0:T(8,128)(2,1)S(1)} %copy-done.11, bf16[1,16,32,64]{3,2,1,0:T(8,128)(2,1)S(1)} %dynamic-slice_bitcast_fusion.1), kind=kOutput, calls=%fused_computation.11 | convolution fusion | flops 141836288 | bytes 622592 | tf_op jit(solution)/shard_map/conv_general_dilated | solution.py:51
  171.0 1.6 fusion.29
  172.6 0.7 fusion.26
  173.3 2.2 %pad_maximum_fusion = bf16[64,2,9,256]{3,1,2,0:T(2,128)(2,1)} fusion(bf16[64,1,9,256]{3,1,2,0:T(2,128)(2,1)S(1)} %copy.67, bf16[64,1,9,256]{3,1,2,0:T(2,128)(2,1)S(1)} %copy.66), kind=kLoop, calls=%fused_computation.12 | loop fusion | flops 1179648 | bytes 1179648 | tf_op jit(solution)/shard_map/stack | solution.py:295
  (166 shorter events, 12.5 us)
Async XLA Ops:
  0.6 5.8 %copy-start.12 = (f32[4,32,256]{2,1,0:T(8,128)S(1)}, f32[4,32,256]{2,1,0:T(8,128)}, u32[]{:S(2)}) copy-start(f32[4,32,256]{2,1,0:T(8,128)} %param.3) | copy-start | bytes 393220
  1.7 9.5 %collective-permute-start.3 = (bf16[4,32,256]{2,1,0:T(8,128)(2,1)S(1)}, bf16[4,32,256]{2,1,0:T(8,128)(2,1)S(1)}, u32[]{:S(2)}, u32[]{:S(2)}) collective-permute-start(bf16[4,32,256]{2,1,0:T(8,128)(2,1)S(1)} %get-tuple-element.21), channel_id=1, source_target_pairs={{0,1},{1,2},{2,3},{3,0},{4,5},{5,6},{6,7},{7,4},{8,9},{9,10},{10,1... | collective-permute-start | bytes 196616 | tf_op jit(solution)/shard_map/ppermute | solution.py:254
  4.8 6.9 %collective-permute-start.4 = (bf16[4,32,256]{2,1,0:T(8,128)(2,1)S(1)}, bf16[4,32,256]{2,1,0:T(8,128)(2,1)S(1)}, u32[]{:S(2)}, u32[]{:S(2)}) collective-permute-start(bf16[4,32,256]{2,1,0:T(8,128)(2,1)S(1)} %get-tuple-element.21), channel_id=1, source_target_pairs={{0,2},{1,3},{2,0},{3,1},{4,6},{5,7},{6,4},{7,5},{8,10},{9,11},{10,... | collective-permute-start | bytes 196616 | tf_op jit(solution)/shard_map/ppermute | solution.py:254
  6.4 6.2 %collective-permute-start.5 = (bf16[4,32,256]{2,1,0:T(8,128)(2,1)S(1)}, bf16[4,32,256]{2,1,0:T(8,128)(2,1)S(1)}, u32[]{:S(2)}, u32[]{:S(2)}) collective-permute-start(bf16[4,32,256]{2,1,0:T(8,128)(2,1)S(1)} %get-tuple-element.21), channel_id=1, source_target_pairs={{0,3},{1,0},{2,1},{3,2},{4,7},{5,4},{6,5},{7,6},{8,11},{9,8},{10,9... | collective-permute-start | bytes 196616 | tf_op jit(solution)/shard_map/ppermute | solution.py:254
  6.5 5.2 %collective-permute-start = (bf16[4,32,256]{2,1,0:T(8,128)(2,1)S(1)}, bf16[4,32,256]{2,1,0:T(8,128)(2,1)S(1)}, u32[]{:S(2)}, u32[]{:S(2)}) collective-permute-start(bf16[4,32,256]{2,1,0:T(8,128)(2,1)S(1)} %get-tuple-element.23), channel_id=1, source_target_pairs={{0,1},{1,2},{2,3},{3,0},{4,5},{5,6},{6,7},{7,4},{8,9},{9,10},{10,1... | collective-permute-start | bytes 196616 | tf_op jit(solution)/shard_map/ppermute | solution.py:254
  8.3 4.2 %collective-permute-start.1 = (bf16[4,32,256]{2,1,0:T(8,128)(2,1)S(1)}, bf16[4,32,256]{2,1,0:T(8,128)(2,1)S(1)}, u32[]{:S(2)}, u32[]{:S(2)}) collective-permute-start(bf16[4,32,256]{2,1,0:T(8,128)(2,1)S(1)} %get-tuple-element.23), channel_id=1, source_target_pairs={{0,2},{1,3},{2,0},{3,1},{4,6},{5,7},{6,4},{7,5},{8,10},{9,11},{10,... | collective-permute-start | bytes 196616 | tf_op jit(solution)/shard_map/ppermute | solution.py:254
  11.2 38.0 %copy-start = (bf16[1,9,256,256]{3,2,1,0:T(8,128)(2,1)}, bf16[1,9,256,256]{3,2,1,0:T(8,128)(2,1)S(1)}, u32[]{:S(2)}) copy-start(bf16[1,9,256,256]{3,2,1,0:T(8,128)(2,1)S(1)} %get-tuple-element.15) | copy-start | bytes 3538948
  11.2 3.7 %collective-permute-start.2 = (bf16[4,32,256]{2,1,0:T(8,128)(2,1)S(1)}, bf16[4,32,256]{2,1,0:T(8,128)(2,1)S(1)}, u32[]{:S(2)}, u32[]{:S(2)}) collective-permute-start(bf16[4,32,256]{2,1,0:T(8,128)(2,1)S(1)} %get-tuple-element.23), channel_id=1, source_target_pairs={{0,3},{1,0},{2,1},{3,2},{4,7},{5,4},{6,5},{7,6},{8,11},{9,8},{10,9... | collective-permute-start | bytes 196616 | tf_op jit(solution)/shard_map/ppermute | solution.py:254
  16.5 1.3 copy-start.5
  51.4 1.3 copy-start.6
  80.5 1.4 copy-start.1
  85.0 1.9 %copy-start.10 = (f32[16,8,4,256]{3,1,2,0:T(8,128)S(1)}, f32[16,8,4,256]{3,1,2,0:T(8,128)}, u32[]{:S(2)}) copy-start(f32[16,8,4,256]{3,1,2,0:T(8,128)} %get-tuple-element.19) | copy-start | bytes 1572868
  90.5 1.3 copy-start.2
  121.8 1.3 copy-start.7
  125.3 1.3 copy-start.3
  154.0 1.3 copy-start.8
  156.6 1.0 copy-start.9
  157.9 4.8 %copy-start.4 = (bf16[1,9,256,256]{3,2,1,0:T(8,128)(2,1)S(1)}, bf16[1,9,256,256]{3,2,1,0:T(8,128)(2,1)}, u32[]{:S(2)}) copy-start(bf16[1,9,256,256]{3,2,1,0:T(8,128)(2,1)} %copy-done) | copy-start | bytes 3538948
  164.9 3.0 %copy-start.11 = (bf16[1,16,32,256]{3,2,1,0:T(8,128)(2,1)S(1)}, bf16[1,16,32,256]{3,2,1,0:T(8,128)(2,1)}, u32[]{:S(2)}) copy-start(bf16[1,16,32,256]{3,2,1,0:T(8,128)(2,1)} %convert_bitcast_fusion) | copy-start | bytes 786436

commit v4 on v1

--- a/solution.py
+++ b/solution.py
@@ -246,16 +246,15 @@
 def gather_space(piece):
     count = lax.axis_size("space")
     place = lax.axis_index("space")
-    rows = piece.shape[0]
-    whole = jnp.zeros((count * rows,) + piece.shape[1:], piece.dtype)
-    whole = lax.dynamic_update_slice_in_dim(whole, piece, place * rows, 0)
-    for shift in range(1, count):
-        part = lax.ppermute(
-            piece, "space", [(i, (i + shift) % count) for i in range(count)]
-        )
-        source = (place + count - shift) % count
-        whole = lax.dynamic_update_slice_in_dim(whole, part, source * rows, 0)
-    return whole
+    parts = [piece] + [
+        lax.ppermute(piece, "space", [(i, (i + shift) % count) for i in range(count)])
+        for shift in range(1, count)
+    ]
+    quarters = [
+        lax.select_n((place + count - quarter) % count, *parts)
+        for quarter in range(count)
+    ]
+    return jnp.concatenate(quarters, axis=0)
 
 
 def own_rows(whole, rows):

time: 170 us -> 172 us (1.012)
  local copies, waits for them, and re-layouts: 27.4 us -> 22.7 us
  other arithmetic: 10.9 us -> 13.7 us
  waiting for transfers between devices: 0.29 us -> 2.59 us
  Pallas kernels: 104 us -> 106 us
    dynamic_update_slice x8 -> x0, local copies, waits for them, and re-layouts: 3.88 us -> none  [the longest x6 2.8 us: gather_space(): whole = lax.dynamic_update_slice_in_dim(whole, part, source * rows, 0)]
    ppermute x6, waiting for transfers between devices: 0.29 us -> 2.59 us  [gather_space(): lax.ppermute(piece, 'space', [(i, (i + shift) % count) for i in range(cou...]
    unnamed x108 -> x114, local copies, waits for them, and re-layouts: 10.1 us -> 12.3 us
    mul x12, local copies, waits for them, and re-layouts: 4.97 us -> 3.12 us  [forward_block(): current = current + step_size * squashed]
    pallas_call x4, Pallas kernels: 104 us -> 106 us  [scan_and_gather(): pl.pallas_call(functools.partial(scan_kernel, n_layer, n_space, reverse),...]
  transfers between devices with their start and end apart: 6 -> 6, of which waited for: 1 -> 2; matrix products, arithmetic and copies ran while one was open for 14% -> 11% of each run, Pallas kernels for 30% -> 30%
where the time goes in v4:
time: 172 us; the launch traced here: 171 us
  Pallas kernels  106 us (62%)
  local copies, waits for them, and re-layouts  22.7 us (13%)
  matrix products  17 us (10%)
  other arithmetic  13.7 us (8%)
  starting transfers between devices  6.92 us (4%)
  waiting for transfers between devices  2.59 us (2%)
  between operations  1.86 us (1%)
    pallas_call x4, Pallas kernels, scan_and_gather(): pl.pallas_call(functools.partial(scan_kernel, n_layer, n_space, reverse),...  106 us
    unnamed x114, local copies, waits for them, and re-layouts  12.3 us
    conv_general_dilated x12, matrix products, chunked_conv(): lax.conv_general_dilated(column_chunks(low), kernel3, (1, 1), ((1, 1), (0...  12 us
    ppermute x6, starting transfers between devices, gather_space(): lax.ppermute(piece, 'space', [(i, (i + shift) % count) for i in range(cou...  6.92 us
    transpose x2, matrix products, on_device(): jnp.transpose(grad, (3, 1, 2, 0)).reshape(quarter, 9, channels)  5.05 us
    convert_element_type x4, other arithmetic, scan_and_gather(): value.astype(link)  3.73 us
  transfers between devices with their start and end apart: 6, of which 2 were waited for; matrix products, arithmetic and copies ran while one was open for 11% of the time, Pallas kernels for 30%

profile of v4, /device:TPU:1, one launch (start us, length us, event | category | flops | bytes accessed | tf_op | source)
XLA Modules:
  0.0 171.0 jit_solution(11314763266459860861)
XLA Ops:
  0.7 3.1 %collective-permute-start = (f32[4,32,256]{2,1,0:T(8,128)}, f32[4,32,256]{2,1,0:T(8,128)S(1)}, u32[]{:S(2)}, u32[]{:S(2)}) collective-permute-start(f32[4,32,256]{2,1,0:T(8,128)} %param.3), channel_id=1, source_target_pairs={{0,1},{1,2},{2,3},{3,0},{4,5},{5,6},{6,7},{7,4},{8,9},{9,10},{10,1... | collective-permute-start | bytes 393224 | tf_op jit(solution)/shard_map/ppermute | solution.py:250
  3.8 1.6 collective-permute-start.1
  5.3 1.7 %collective-permute-start.3 = (f32[4,32,256]{2,1,0:T(8,128)}, f32[4,32,256]{2,1,0:T(8,128)S(1)}, u32[]{:S(2)}, u32[]{:S(2)}) collective-permute-start(f32[4,32,256]{2,1,0:T(8,128)} %param.5), channel_id=1, source_target_pairs={{0,1},{1,2},{2,3},{3,0},{4,5},{5,6},{6,7},{7,4},{8,9},{9,10},{10,1... | collective-permute-start | bytes 393224 | tf_op jit(solution)/shard_map/ppermute | solution.py:250
  7.1 2.8 %fusion.64 = (bf16[1,9,256,256]{3,2,1,0:T(8,128)(2,1)S(1)}, bf16[1,9,256,256]{3,2,1,0:T(8,128)(2,1)}) fusion(bf16[2,9,256,256]{3,2,1,0:T(8,128)(2,1)} %param.4), kind=kLoop, calls=%fused_computation.295 | loop fusion | bytes 4718592 | tf_op jit(solution)/shard_map/unstack | solution.py:267
  10.4 1.0 collective-permute-done.1
  11.5 1.6 collective-permute-done.2
  13.4 0.9 fusion.3
  14.7 0.9 fusion.62
  15.8 1.0 copy-done.4
  16.9 0.9 fusion.2
  18.1 0.9 fusion.31.value_ref
  19.1 27.1 %shard_map.58 = f32[16,32,256]{2,1,0:T(8,128)S(1)} custom-call(bf16[4,32,256]{2,1,0:T(8,128)(2,1)S(1)} %fusion.31.value_ref, f32[16,32,256]{2,1,0:T(8,128)S(1)} %get-tuple-element.26.base_ref), custom_call_target="tpu_custom_call" | custom-call | tf_op jit(solution)/shard_map/pallas_call | solution.py:222
  46.5 0.9 fusion.1
  48.2 1.0 copy-done.5
  49.2 0.9 fusion
  50.2 1.0 mul.97
  51.2 0.9 fusion.30.value_ref
  52.2 24.7 %shard_map.59 = f32[16,32,256]{2,1,0:T(8,128)S(1)} custom-call(bf16[4,32,256]{2,1,0:T(8,128)(2,1)S(1)} %fusion.30.value_ref, f32[16,32,256]{2,1,0:T(8,128)S(1)} %get-tuple-element.26.base_ref), custom_call_target="tpu_custom_call" | custom-call | tf_op jit(solution)/shard_map/pallas_call | solution.py:222
  77.2 1.7 subtract_multiply_fusion
  79.2 0.6 copy-done.11
  80.3 0.9 fusion.60
  81.4 1.0 copy-done.6
  82.5 1.7 subtract_multiply_fusion.1
  84.5 0.7 convert_bitcast_fusion
  85.3 1.0 select_select_fusion.3
  86.7 0.9 copy-done.7
  87.6 0.9 fusion.16
  88.9 0.9 multiply_convert_fusion.4
  90.1 1.0 copy-done.1
  91.1 0.9 fusion.14
  92.4 0.9 fusion.28.value_ref
  93.3 28.8 %shard_map.60 = f32[16,32,256]{2,1,0:T(8,128)S(1)} custom-call(bf16[4,32,256]{2,1,0:T(8,128)(2,1)S(1)} %fusion.28.value_ref, f32[16,32,256]{2,1,0:T(8,128)S(1)} %get-tuple-element.17.base_ref), custom_call_target="tpu_custom_call" | custom-call | tf_op jit(solution)/shard_map/pallas_call | solution.py:222
  122.5 0.9 copy-done.8
  123.4 0.9 fusion.12
  124.7 0.9 multiply_convert_fusion.2
  125.8 1.0 copy-done.2
  126.9 0.9 fusion.10
  128.1 0.9 fusion.27.value_ref
  129.1 25.4 %shard_map.61 = f32[16,32,256]{2,1,0:T(8,128)S(1)} custom-call(bf16[4,32,256]{2,1,0:T(8,128)(2,1)S(1)} %fusion.27.value_ref, f32[16,32,256]{2,1,0:T(8,128)S(1)} %get-tuple-element.17.base_ref), custom_call_target="tpu_custom_call" | custom-call | tf_op jit(solution)/shard_map/pallas_call | solution.py:222
  154.9 0.9 copy-done.9
  155.8 0.9 fusion.8
  157.5 0.6 copy-done.12
  158.0 2.5 %convolution_convert_fusion.1 = bf16[64,3,3,256]{3,0,2,1:T(8,128)(2,1)S(1)} fusion(bf16[1,16,32,256]{3,2,1,0:T(8,128)(2,1)S(1)} %copy-done.12, bf16[1,16,32,64]{3,2,1,0:T(8,128)(2,1)S(1)} %get-tuple-element.34), kind=kOutput, calls=%fused_computation.11 | convolution fusion | flops 141836288 | bytes 622592 | tf_op jit(solution)/shard_map/transpose | solution.py:292
  161.0 2.5 %convolution_convert_fusion = bf16[64,3,3,256]{3,0,2,1:T(8,128)(2,1)S(1)} fusion(bf16[1,16,32,256]{3,2,1,0:T(8,128)(2,1)S(1)} %bitcast.411, bf16[1,16,32,64]{3,2,1,0:T(8,128)(2,1)S(1)} %get-tuple-element.33), kind=kOutput, calls=%fused_computation.10 | convolution fusion | flops 141836288 | bytes 622592 | tf_op jit(solution)/shard_map/transpose | solution.py:292
  164.8 0.9 fusion.6
  166.1 0.6 copy-done.10
  167.2 2.2 %pad_maximum_fusion = bf16[64,2,9,256]{3,1,2,0:T(2,128)(2,1)} fusion(bf16[64,1,9,256]{3,1,2,0:T(2,128)(2,1)S(1)} %copy.67, bf16[64,1,9,256]{3,1,2,0:T(2,128)(2,1)S(1)} %copy.66), kind=kLoop, calls=%fused_computation.12 | loop fusion | flops 1179648 | bytes 1179648 | tf_op jit(solution)/shard_map/stack | solution.py:293
  169.3 1.6 fusion.26
  (161 shorter events, 10.4 us)
Async XLA Ops:
  0.6 12.4 %copy-start.13 = (f32[4,32,256]{2,1,0:T(8,128)S(1)}, f32[4,32,256]{2,1,0:T(8,128)}, u32[]{:S(2)}) copy-start(f32[4,32,256]{2,1,0:T(8,128)} %param.3) | copy-start | bytes 393220
  0.6 9.3 %copy-start.14 = (f32[4,32,256]{2,1,0:T(8,128)S(1)}, f32[4,32,256]{2,1,0:T(8,128)}, u32[]{:S(2)}) copy-start(f32[4,32,256]{2,1,0:T(8,128)} %param.5) | copy-start | bytes 393220
  0.7 9.3 %collective-permute-start = (f32[4,32,256]{2,1,0:T(8,128)}, f32[4,32,256]{2,1,0:T(8,128)S(1)}, u32[]{:S(2)}, u32[]{:S(2)}) collective-permute-start(f32[4,32,256]{2,1,0:T(8,128)} %param.3), channel_id=1, source_target_pairs={{0,1},{1,2},{2,3},{3,0},{4,5},{5,6},{6,7},{7,4},{8,9},{9,10},{10,1... | collective-permute-start | bytes 393224 | tf_op jit(solution)/shard_map/ppermute | solution.py:250
  3.8 7.7 %collective-permute-start.1 = (f32[4,32,256]{2,1,0:T(8,128)}, f32[4,32,256]{2,1,0:T(8,128)S(1)}, u32[]{:S(2)}, u32[]{:S(2)}) collective-permute-start(f32[4,32,256]{2,1,0:T(8,128)} %param.3), channel_id=1, source_target_pairs={{0,2},{1,3},{2,0},{3,1},{4,6},{5,7},{6,4},{7,5},{8,10},{9,11},{10,... | collective-permute-start | bytes 393224 | tf_op jit(solution)/shard_map/ppermute | solution.py:250
  5.3 7.7 %collective-permute-start.2 = (f32[4,32,256]{2,1,0:T(8,128)}, f32[4,32,256]{2,1,0:T(8,128)S(1)}, u32[]{:S(2)}, u32[]{:S(2)}) collective-permute-start(f32[4,32,256]{2,1,0:T(8,128)} %param.3), channel_id=1, source_target_pairs={{0,3},{1,0},{2,1},{3,2},{4,7},{5,4},{6,5},{7,6},{8,11},{9,8},{10,9... | collective-permute-start | bytes 393224 | tf_op jit(solution)/shard_map/ppermute | solution.py:250
  5.3 79.9 %collective-permute-start.3 = (f32[4,32,256]{2,1,0:T(8,128)}, f32[4,32,256]{2,1,0:T(8,128)S(1)}, u32[]{:S(2)}, u32[]{:S(2)}) collective-permute-start(f32[4,32,256]{2,1,0:T(8,128)} %param.5), channel_id=1, source_target_pairs={{0,1},{1,2},{2,3},{3,0},{4,5},{5,6},{6,7},{7,4},{8,9},{9,10},{10,1... | collective-permute-start | bytes 393224 | tf_op jit(solution)/shard_map/ppermute | solution.py:250
  7.1 78.2 %collective-permute-start.4 = (f32[4,32,256]{2,1,0:T(8,128)}, f32[4,32,256]{2,1,0:T(8,128)}, u32[]{:S(2)}, u32[]{:S(2)}) collective-permute-start(f32[4,32,256]{2,1,0:T(8,128)} %param.5), channel_id=1, source_target_pairs={{0,2},{1,3},{2,0},{3,1},{4,6},{5,7},{6,4},{7,5},{8,10},{9,11},{10,... | collective-permute-start | bytes 393224 | tf_op jit(solution)/shard_map/ppermute | solution.py:250
  10.0 67.2 %copy-start = (bf16[1,9,256,256]{3,2,1,0:T(8,128)(2,1)}, bf16[1,9,256,256]{3,2,1,0:T(8,128)(2,1)S(1)}, u32[]{:S(2)}) copy-start(bf16[1,9,256,256]{3,2,1,0:T(8,128)(2,1)S(1)} %get-tuple-element.15) | copy-start | bytes 3538948
  10.0 75.3 %collective-permute-start.5 = (f32[4,32,256]{2,1,0:T(8,128)S(1)}, f32[4,32,256]{2,1,0:T(8,128)}, u32[]{:S(2)}, u32[]{:S(2)}) collective-permute-start(f32[4,32,256]{2,1,0:T(8,128)S(1)} %copy-done.14), channel_id=1, source_target_pairs={{0,3},{1,0},{2,1},{3,2},{4,7},{5,4},{6,5},{7,6},{8,11},{9,8},{10,9... | collective-permute-start | bytes 393224 | tf_op jit(solution)/shard_map/ppermute | solution.py:250
  15.6 1.3 copy-start.4
  47.9 1.3 copy-start.5
  78.8 1.0 copy-start.11
  81.2 1.3 copy-start.6
  86.3 1.3 copy-start.7
  89.8 1.3 copy-start.1
  122.1 1.3 copy-start.8
  125.6 1.3 copy-start.2
  154.5 1.3 copy-start.9
  157.1 1.0 copy-start.12
  163.6 1.3 copy-start.3
  165.7 1.0 copy-start.10

commit v5 on v1

--- a/solution.py
+++ b/solution.py
@@ -258,6 +258,24 @@
     return whole
 
 
+def own_jump(piece, kernels):
+    count = lax.axis_size("space")
+    place = lax.axis_index("space")
+    rows = piece.shape[0]
+    halo = len(kernels)
+    assert halo <= rows
+    top = lax.ppermute(piece[rows - halo :], "space", [(i, i + 1) for i in range(count - 1)])
+    bottom = lax.ppermute(piece[:halo], "space", [(i + 1, i) for i in range(count - 1)])
+    start = jnp.concatenate([top, piece, bottom], axis=0)
+    index = place * rows - halo + jnp.arange(rows + 2 * halo)
+    inside = ((index >= 0) & (index < rows * count))[:, None, None]
+    current = start
+    for kernel3 in kernels:
+        low = jnp.where(inside, current, jnp.zeros_like(current)).astype(jnp.bfloat16)
+        current = current + step_size * jnp.tanh(conv(low, kernel3))
+    return (current - start)[halo : halo + rows]
+
+
 def own_rows(whole, rows):
     return lax.dynamic_slice_in_dim(whole, lax.axis_index("space") * rows, rows, 0)
 
@@ -272,8 +290,11 @@
 
     begin_state = full_input
     for sweep_index in range(ITERS):
-        block_end, _, _ = forward_block(begin_state, kernels)
-        jump = own_rows(block_end - begin_state, rows)
+        if sweep_index == 0:
+            jump = own_jump(input_field, kernels)
+        else:
+            block_end, _, _ = forward_block(begin_state, kernels)
+            jump = own_rows(block_end - begin_state, rows)
         begin_state = scan_and_gather(jump, full_input, False, sweep_index)
     outputs, inputs_low, slopes = forward_block(begin_state, kernels)
 

time: 170 us -> 180 us (1.059)
  waiting for transfers between devices: 0.29 us -> 6.19 us
  starting transfers between devices: 6.9 us -> 11.6 us
  Pallas kernels: 104 us -> 106 us
    ppermute x0 -> x2, starting transfers between devices: none -> 4.46 us  [the longest x1 2.54 us: own_jump(): lax.ppermute(piece[:halo], 'space', [(i + 1, i) for i in range(count - 1)])]
    ppermute x0 -> x2, waiting for transfers between devices: none -> 3.07 us  [the longest x1 3.07 us: own_jump(): lax.ppermute(piece[:halo], 'space', [(i + 1, i) for i in range(count - 1)])]
    ppermute x6, waiting for transfers between devices: 0.29 us -> 3.12 us  [gather_space(): lax.ppermute(piece, 'space', [(i, (i + shift) % count) for i in range(cou...]
    pallas_call x4, Pallas kernels: 104 us -> 106 us  [scan_and_gather(): pl.pallas_call(functools.partial(scan_kernel, n_layer, n_space, reverse),...]
    mul x12 -> x8, local copies, waits for them, and re-layouts: 4.97 us -> 3.4 us  [forward_block(): current = current + step_size * squashed]
    unnamed x108 -> x111, local copies, waits for them, and re-layouts: 10.1 us -> 9.95 us
  transfers between devices with their start and end apart: 6 -> 8, of which waited for: 1 -> 3; matrix products, arithmetic and copies ran while one was open for 14% -> 12% of each run, Pallas kernels for 30% -> 29%
where the time goes in v5:
time: 180 us
  Pallas kernels  106 us (59%)
  local copies, waits for them, and re-layouts  26.8 us (15%)
  matrix products  16.7 us (9%)
  starting transfers between devices  11.6 us (6%)
  other arithmetic  10.1 us (6%)
  waiting for transfers between devices  6.19 us (3%)
  between operations  2.03 us (1%)
    pallas_call x4, Pallas kernels, scan_and_gather(): pl.pallas_call(functools.partial(scan_kernel, n_layer, n_space, reverse),...  106 us
    conv_general_dilated x12, matrix products, chunked_conv(): lax.conv_general_dilated(column_chunks(low), kernel3, (1, 1), ((1, 1), (0...  11.5 us
    unnamed x111, local copies, waits for them, and re-layouts  9.95 us
    ppermute x6, starting transfers between devices, gather_space(): lax.ppermute(piece, 'space', [(i, (i + shift) % count) for i in range(cou...  7.12 us
    transpose x2, matrix products, on_device(): jnp.transpose(grad, (3, 1, 2, 0)).reshape(quarter, 9, channels)  5.2 us
    dynamic_update_slice x6, local copies, waits for them, and re-layouts, gather_space(): whole = lax.dynamic_update_slice_in_dim(whole, part, source * rows, 0)  3.69 us
  transfers between devices with their start and end apart: 8, of which 3 were waited for; matrix products, arithmetic and copies ran while one was open for 12% of the time, Pallas kernels for 29%

profile of v5, /device:TPU:1, one launch (start us, length us, event | category | flops | bytes accessed | tf_op | source)
XLA Modules:
  0.0 179.6 jit_solution(15885393603716390747)
XLA Ops:
  0.6 3.1 %collective-permute-start.5 = (f32[4,32,256]{2,1,0:T(8,128)}, f32[4,32,256]{2,1,0:T(8,128)}, u32[]{:S(2)}, u32[]{:S(2)}) collective-permute-start(f32[4,32,256]{2,1,0:T(8,128)} %param.5), channel_id=1, source_target_pairs={{0,1},{1,2},{2,3},{3,0},{4,5},{5,6},{6,7},{7,4},{8,9},{9,10},{10,1... | collective-permute-start | bytes 393224 | tf_op jit(solution)/shard_map/ppermute | solution.py:253
  4.0 1.3 collective-permute-start.6
  5.3 2.0 %collective-permute-start.2 = (f32[4,32,256]{2,1,0:T(8,128)}, f32[4,32,256]{2,1,0:T(8,128)S(1)}, u32[]{:S(2)}, u32[]{:S(2)}) collective-permute-start(f32[4,32,256]{2,1,0:T(8,128)} %param.3), channel_id=1, source_target_pairs={{0,1},{1,2},{2,3},{3,0},{4,5},{5,6},{6,7},{7,4},{8,9},{9,10},{10,1... | collective-permute-start | bytes 393224 | tf_op jit(solution)/shard_map/ppermute | solution.py:253
  7.3 0.9 fusion.59
  8.2 1.9 %collective-permute-start = (f32[2,32,256]{2,1,0:T(8,128)S(1)}, f32[2,32,256]{2,1,0:T(8,128)S(1)}, u32[]{:S(2)}, u32[]{:S(2)}) collective-permute-start(f32[2,32,256]{2,1,0:T(8,128)S(1)} %get-tuple-element.24), channel_id=1, source_target_pairs={{0,1},{1,2},{2,3},{4,5},{5,6},{6,7},{8,9},{9,10},{10,11},{12,13},{... | collective-permute-start | bytes 196616 | tf_op jit(solution)/shard_map/ppermute | solution.py:267
  10.2 2.9 %fusion.58 = (bf16[1,9,256,256]{3,2,1,0:T(8,128)(2,1)S(1)}, bf16[1,9,256,256]{3,2,1,0:T(8,128)(2,1)}) fusion(bf16[2,9,256,256]{3,2,1,0:T(8,128)(2,1)} %param.4), kind=kLoop, calls=%fused_computation.295 | loop fusion | bytes 4718592 | tf_op jit(solution)/shard_map/unstack | solution.py:286
  13.2 2.5 %collective-permute-start.1 = (f32[2,32,256]{2,1,0:T(8,128)S(1)}, f32[2,32,256]{2,1,0:T(8,128)S(1)}, u32[]{:S(2)}, u32[]{:S(2)}) collective-permute-start(f32[2,32,256]{2,1,0:T(8,128)S(1)} %get-tuple-element.23), channel_id=1, source_target_pairs={{1,0},{2,1},{3,2},{5,4},{6,5},{7,6},{9,8},{10,9},{11,10},{13,12},{... | collective-permute-start | bytes 196616 | tf_op jit(solution)/shard_map/ppermute | solution.py:268
  15.8 3.1 %collective-permute-done.1 = f32[2,32,256]{2,1,0:T(8,128)S(1)} collective-permute-done((f32[2,32,256]{2,1,0:T(8,128)S(1)}, f32[2,32,256]{2,1,0:T(8,128)S(1)}, u32[]{:S(2)}, u32[]{:S(2)}) %collective-permute-start.1) | collective-permute-done | bytes 65568 | tf_op jit(solution)/shard_map/ppermute | solution.py:268
  20.2 1.0 copy-done.5
  22.4 0.6 collective-permute-done.3
  23.0 0.9 constant_dynamic-update-slice_fusion.104
  24.0 2.5 %collective-permute-done.4 = f32[4,32,256]{2,1,0:T(8,128)S(1)} collective-permute-done((f32[4,32,256]{2,1,0:T(8,128)S(1)}, f32[4,32,256]{2,1,0:T(8,128)S(1)}, u32[]{:S(2)}, u32[]{:S(2)}) %collective-permute-start.4) | collective-permute-done | bytes 131104 | tf_op jit(solution)/shard_map/ppermute | solution.py:253
  26.5 27.8 %shard_map.58 = f32[16,32,256]{2,1,0:T(8,128)S(1)} custom-call(bf16[4,32,256]{2,1,0:T(8,128)(2,1)S(1)} %fusion.31.value_ref, f32[16,32,256]{2,1,0:T(8,128)S(1)} %constant_dynamic-update-slice_fusion.103.base_ref), custom_call_target="tpu_custom_call" | custom-call | tf_op jit(solution)/shard_map/pallas_call | solution.py:222
  54.6 0.9 fusion.1
  55.9 0.9 fusion.57
  57.0 1.0 copy-done.6
  58.0 0.9 fusion
  59.1 1.0 mul.114
  60.1 1.0 fusion.30.value_ref
  61.1 24.7 %shard_map.59 = f32[16,32,256]{2,1,0:T(8,128)S(1)} custom-call(bf16[4,32,256]{2,1,0:T(8,128)(2,1)S(1)} %fusion.30.value_ref, f32[16,32,256]{2,1,0:T(8,128)S(1)} %constant_dynamic-update-slice_fusion.103.base_ref), custom_call_target="tpu_custom_call" | custom-call | tf_op jit(solution)/shard_map/pallas_call | solution.py:222
  86.1 1.0 copy-done.1
  87.1 1.7 subtract_multiply_fusion
  89.1 0.9 fusion.56
  90.3 1.9 %subtract_multiply_fusion.1 = (f32[16,8,4,256]{3,1,2,0:T(8,128)}, f32[16,8,4,256]{3,1,2,0:T(8,128)}) fusion(bf16[3,3,256,256]{3,2,1,0:T(8,128)(2,1)S(1)} %bitcast.420, bf16[16,8,6,256]{3,2,0,1:T(8,128)(2,1)S(1)} %constant_dynamic-update-slice_fusion.43), kind=kOutput, calls=%fused_computation.20 | convolution fusion | flops 579338240 | bytes 2621440 | tf_op jit(solution)/shard_map/conv_general_dilated | solution.py:31
  92.2 0.7 convert_bitcast_fusion
  92.9 0.9 constant_dynamic-update-slice_fusion.101
  94.2 1.2 copy.48
  95.7 0.9 constant_dynamic-update-slice_fusion.100
  96.6 0.9 constant_dynamic-update-slice_fusion.99.base_ref
  97.9 0.9 fusion.16
  99.6 1.0 copy-done.2
  100.6 0.9 fusion.14
  101.9 29.8 %shard_map.60 = f32[16,32,256]{2,1,0:T(8,128)S(1)} custom-call(bf16[4,32,256]{2,1,0:T(8,128)(2,1)S(1)} %fusion.28.value_ref, f32[16,32,256]{2,1,0:T(8,128)S(1)} %constant_dynamic-update-slice_fusion.99.base_ref), custom_call_target="tpu_custom_call" | custom-call | tf_op jit(solution)/shard_map/pallas_call | solution.py:222
  132.1 0.9 copy-done.7
  133.0 0.9 fusion.12
  134.3 0.9 multiply_convert_fusion.2
  135.4 1.0 copy-done.3
  136.4 0.9 fusion.10
  137.7 0.9 fusion.27.value_ref
  138.7 23.9 %shard_map.61 = f32[16,32,256]{2,1,0:T(8,128)S(1)} custom-call(bf16[4,32,256]{2,1,0:T(8,128)(2,1)S(1)} %fusion.27.value_ref, f32[16,32,256]{2,1,0:T(8,128)S(1)} %constant_dynamic-update-slice_fusion.99.base_ref), custom_call_target="tpu_custom_call" | custom-call | tf_op jit(solution)/shard_map/pallas_call | solution.py:222
  162.9 0.9 copy-done.8
  163.8 0.9 fusion.8
  166.1 2.6 %convolution_convert_fusion.1 = bf16[64,3,3,256]{3,0,2,1:T(8,128)(2,1)S(1)} fusion(bf16[1,16,32,256]{3,2,1,0:T(8,128)(2,1)S(1)} %copy-done.11, bf16[1,16,32,64]{3,2,1,0:T(8,128)(2,1)S(1)} %get-tuple-element.28), kind=kOutput, calls=%fused_computation.7 | convolution fusion | flops 141836288 | bytes 622592 | tf_op jit(solution)/shard_map/transpose | solution.py:314
  169.2 2.6 %convolution_convert_fusion = bf16[64,3,3,256]{3,0,2,1:T(8,128)(2,1)S(1)} fusion(bf16[1,16,32,256]{3,2,1,0:T(8,128)(2,1)S(1)} %bitcast.411, bf16[1,16,32,64]{3,2,1,0:T(8,128)(2,1)S(1)} %get-tuple-element.27), kind=kOutput, calls=%fused_computation.6 | convolution fusion | flops 141836288 | bytes 622592 | tf_op jit(solution)/shard_map/transpose | solution.py:314
  173.0 0.9 fusion.6
  174.3 1.2 copy.47
  175.8 2.2 %pad_maximum_fusion = bf16[64,2,9,256]{3,1,2,0:T(2,128)(2,1)} fusion(bf16[64,1,9,256]{3,1,2,0:T(2,128)(2,1)S(1)} %copy.67, bf16[64,1,9,256]{3,1,2,0:T(2,128)(2,1)S(1)} %copy.66), kind=kLoop, calls=%fused_computation.12 | loop fusion | flops 1179648 | bytes 1179648 | tf_op jit(solution)/shard_map/stack | solution.py:315
  177.9 1.6 fusion.26
  (173 shorter events, 11.6 us)
Async XLA Ops:
  0.6 92.3 %collective-permute-start.5 = (f32[4,32,256]{2,1,0:T(8,128)}, f32[4,32,256]{2,1,0:T(8,128)}, u32[]{:S(2)}, u32[]{:S(2)}) collective-permute-start(f32[4,32,256]{2,1,0:T(8,128)} %param.5), channel_id=1, source_target_pairs={{0,1},{1,2},{2,3},{3,0},{4,5},{5,6},{6,7},{7,4},{8,9},{9,10},{10,1... | collective-permute-start | bytes 393224 | tf_op jit(solution)/shard_map/ppermute | solution.py:253
  3.7 92.9 %collective-permute-start.7 = (f32[4,32,256]{2,1,0:T(8,128)}, f32[4,32,256]{2,1,0:T(8,128)}, u32[]{:S(2)}, u32[]{:S(2)}) collective-permute-start(f32[4,32,256]{2,1,0:T(8,128)} %param.5), channel_id=1, source_target_pairs={{0,3},{1,0},{2,1},{3,2},{4,7},{5,4},{6,5},{7,6},{8,11},{9,8},{10,9... | collective-permute-start | bytes 393224 | tf_op jit(solution)/shard_map/ppermute | solution.py:253
  4.0 91.6 %collective-permute-start.6 = (f32[4,32,256]{2,1,0:T(8,128)}, f32[4,32,256]{2,1,0:T(8,128)}, u32[]{:S(2)}, u32[]{:S(2)}) collective-permute-start(f32[4,32,256]{2,1,0:T(8,128)} %param.5), channel_id=1, source_target_pairs={{0,2},{1,3},{2,0},{3,1},{4,6},{5,7},{6,4},{7,5},{8,10},{9,11},{10,... | collective-permute-start | bytes 393224 | tf_op jit(solution)/shard_map/ppermute | solution.py:253
  5.3 16.6 %collective-permute-start.2 = (f32[4,32,256]{2,1,0:T(8,128)}, f32[4,32,256]{2,1,0:T(8,128)S(1)}, u32[]{:S(2)}, u32[]{:S(2)}) collective-permute-start(f32[4,32,256]{2,1,0:T(8,128)} %param.3), channel_id=1, source_target_pairs={{0,1},{1,2},{2,3},{3,0},{4,5},{5,6},{6,7},{7,4},{8,9},{9,10},{10,1... | collective-permute-start | bytes 393224 | tf_op jit(solution)/shard_map/ppermute | solution.py:253
  8.2 5.0 %collective-permute-start = (f32[2,32,256]{2,1,0:T(8,128)S(1)}, f32[2,32,256]{2,1,0:T(8,128)S(1)}, u32[]{:S(2)}, u32[]{:S(2)}) collective-permute-start(f32[2,32,256]{2,1,0:T(8,128)S(1)} %get-tuple-element.24), channel_id=1, source_target_pairs={{0,1},{1,2},{2,3},{4,5},{5,6},{6,7},{8,9},{9,10},{10,11},{12,13},{... | collective-permute-start | bytes 196616 | tf_op jit(solution)/shard_map/ppermute | solution.py:267
  10.2 3.0 %copy-start.12 = (f32[4,32,256]{2,1,0:T(8,128)S(1)}, f32[4,32,256]{2,1,0:T(8,128)}, u32[]{:S(2)}) copy-start(f32[4,32,256]{2,1,0:T(8,128)} %param.5) | copy-start | bytes 393220
  13.1 41.5 %copy-start = (bf16[1,9,256,256]{3,2,1,0:T(8,128)(2,1)}, bf16[1,9,256,256]{3,2,1,0:T(8,128)(2,1)S(1)}, u32[]{:S(2)}) copy-start(bf16[1,9,256,256]{3,2,1,0:T(8,128)(2,1)S(1)} %get-tuple-element.15) | copy-start | bytes 3538948
  13.1 2.7 %copy-start.10 = (f32[4,32,256]{2,1,0:T(8,128)S(1)}, f32[4,32,256]{2,1,0:T(8,128)}, u32[]{:S(2)}) copy-start(f32[4,32,256]{2,1,0:T(8,128)} %param.3) | copy-start | bytes 393220
  13.2 5.7 %collective-permute-start.1 = (f32[2,32,256]{2,1,0:T(8,128)S(1)}, f32[2,32,256]{2,1,0:T(8,128)S(1)}, u32[]{:S(2)}, u32[]{:S(2)}) collective-permute-start(f32[2,32,256]{2,1,0:T(8,128)S(1)} %get-tuple-element.23), channel_id=1, source_target_pairs={{1,0},{2,1},{3,2},{5,4},{6,5},{7,6},{9,8},{10,9},{11,10},{13,12},{... | collective-permute-start | bytes 196616 | tf_op jit(solution)/shard_map/ppermute | solution.py:268
  18.9 4.1 %collective-permute-start.3 = (f32[4,32,256]{2,1,0:T(8,128)S(1)}, f32[4,32,256]{2,1,0:T(8,128)}, u32[]{:S(2)}, u32[]{:S(2)}) collective-permute-start(f32[4,32,256]{2,1,0:T(8,128)S(1)} %copy-done.10), channel_id=1, source_target_pairs={{0,2},{1,3},{2,0},{3,1},{4,6},{5,7},{6,4},{7,5},{8,10},{9,11},{10,... | collective-permute-start | bytes 393224 | tf_op jit(solution)/shard_map/ppermute | solution.py:253
  19.9 1.3 copy-start.5
  22.0 4.5 %collective-permute-start.4 = (f32[4,32,256]{2,1,0:T(8,128)S(1)}, f32[4,32,256]{2,1,0:T(8,128)S(1)}, u32[]{:S(2)}, u32[]{:S(2)}) collective-permute-start(f32[4,32,256]{2,1,0:T(8,128)S(1)} %copy-done.10), channel_id=1, source_target_pairs={{0,3},{1,0},{2,1},{3,2},{4,7},{5,4},{6,5},{7,6},{8,11},{9,8},{10,9... | collective-permute-start | bytes 393224 | tf_op jit(solution)/shard_map/ppermute | solution.py:253
  56.8 1.3 copy-start.6
  85.8 1.3 copy-start.1
  92.2 1.7 copy-start.9
  99.3 1.3 copy-start.2
  131.7 1.3 copy-start.7
  135.2 1.3 copy-start.3
  162.6 1.3 copy-start.8
  165.1 1.0 copy-start.11
  171.7 1.3 copy-start.4

commit v6 on v1

--- a/solution.py
+++ b/solution.py
@@ -267,8 +267,9 @@
     channels = weights.shape[3]
     kernels = [w.reshape(3, 3, channels, channels) for w in weights]
     flipped = [k[::-1, ::-1] for k in kernels]
-    full_input = gather_space(input_field)
-    full_cotangent = gather_space(cotangent)
+    both = gather_space(jnp.stack([input_field, cotangent], axis=1))
+    full_input = both[:, 0]
+    full_cotangent = both[:, 1]
 
     begin_state = full_input
     for sweep_index in range(ITERS):

time: 170 us -> 185 us (1.088)
  waiting for transfers between devices: 0.29 us -> 6.88 us
  other arithmetic: 10.9 us -> 15.5 us
  Pallas kernels: 104 us -> 108 us
  local copies, waits for them, and re-layouts: 27.4 us -> 29.4 us
  starting transfers between devices: 6.9 us -> 4.96 us
    ppermute x6 -> x3, waiting for transfers between devices: 0.29 us -> 6.88 us  [gather_space(): lax.ppermute(piece, 'space', [(i, (i + shift) % count) for i in range(cou...]
    pallas_call x4, Pallas kernels: 104 us -> 108 us  [scan_and_gather(): pl.pallas_call(functools.partial(scan_kernel, n_layer, n_space, reverse),...]
    mul x12, local copies, waits for them, and re-layouts: 4.97 us -> 8.65 us  [forward_block(): current = current + step_size * squashed]
    dynamic_update_slice x6 -> x3, local copies, waits for them, and re-layouts: 2.8 us -> 0.07 us  [gather_space(): whole = lax.dynamic_update_slice_in_dim(whole, part, source * rows, 0)]
    convert_element_type x6, other arithmetic: 1.48 us -> 4.08 us  [backward_block(): scaled = (step_size * slopes[index] * adjoint).astype(jnp.bfloat16)]
    unnamed x108 -> x112, local copies, waits for them, and re-layouts: 10.1 us -> 12.4 us
    ppermute x6 -> x3, starting transfers between devices: 6.9 us -> 4.96 us  [gather_space(): lax.ppermute(piece, 'space', [(i, (i + shift) % count) for i in range(cou...]
  transfers between devices with their start and end apart: 6 -> 3, of which waited for: 1 -> 2; matrix products, arithmetic and copies ran while one was open for 14% -> 2% of each run, Pallas kernels for 30% -> 0%
where the time goes in v6:
time: 185 us; the launch traced here: 184 us
  Pallas kernels  108 us (58%)
  local copies, waits for them, and re-layouts  29.4 us (16%)
  matrix products  17 us (9%)
  other arithmetic  15.5 us (8%)
  waiting for transfers between devices  6.88 us (4%)
  starting transfers between devices  4.96 us (3%)
  between operations  1.85 us (1%)
    pallas_call x4, Pallas kernels, scan_and_gather(): pl.pallas_call(functools.partial(scan_kernel, n_layer, n_space, reverse),...  108 us
    unnamed x112, local copies, waits for them, and re-layouts  12.4 us
    conv_general_dilated x12, matrix products, chunked_conv(): lax.conv_general_dilated(column_chunks(low), kernel3, (1, 1), ((1, 1), (0...  12 us
    mul x12, local copies, waits for them, and re-layouts, forward_block(): current = current + step_size * squashed  8.65 us
    ppermute x3, waiting for transfers between devices, gather_space(): lax.ppermute(piece, 'space', [(i, (i + shift) % count) for i in range(cou...  6.88 us
    transpose x2, matrix products, on_device(): jnp.transpose(grad, (3, 1, 2, 0)).reshape(quarter, 9, channels)  5.05 us
    ppermute x3, starting transfers between devices, gather_space(): lax.ppermute(piece, 'space', [(i, (i + shift) % count) for i in range(cou...  4.96 us
    convert_element_type x6, other arithmetic, backward_block(): scaled = (step_size * slopes[index] * adjoint).astype(jnp.bfloat16)  4.08 us
  transfers between devices with their start and end apart: 3, of which 2 were waited for; matrix products, arithmetic and copies ran while one was open for 2% of the time, Pallas kernels for 0%

profile of v6, /device:TPU:1, one launch (start us, length us, event | category | flops | bytes accessed | tf_op | source)
XLA Modules:
  0.0 183.8 jit_solution(1846046624249747111)
XLA Ops:
  0.8 1.0 pad_maximum_fusion.1
  1.8 2.6 %collective-permute-start.1 = (f32[4,2,32,256]{3,2,0,1:T(8,128)S(1)}, f32[4,2,32,256]{3,2,0,1:T(8,128)S(1)}, u32[]{:S(2)}, u32[]{:S(2)}) collective-permute-start(f32[4,2,32,256]{3,2,0,1:T(8,128)S(1)} %get-tuple-element.23), channel_id=1, source_target_pairs={{0,2},{1,3},{2,0},{3,1},{4,6},{5,7},{6,4},{7,5},{8,10},{9,11},{10,... | collective-permute-start | bytes 786440 | tf_op jit(solution)/shard_map/ppermute | solution.py:253
  4.3 2.4 %collective-permute-start = (f32[4,2,32,256]{3,2,0,1:T(8,128)S(1)}, f32[4,2,32,256]{3,2,0,1:T(8,128)S(1)}, u32[]{:S(2)}, u32[]{:S(2)}) collective-permute-start(f32[4,2,32,256]{3,2,0,1:T(8,128)S(1)} %get-tuple-element.23), channel_id=1, source_target_pairs={{0,1},{1,2},{2,3},{3,0},{4,5},{5,6},{6,7},{7,4},{8,9},{9,10},{10,1... | collective-permute-start | bytes 786440 | tf_op jit(solution)/shard_map/ppermute | solution.py:253
  6.7 2.8 %fusion.64 = (bf16[1,9,256,256]{3,2,1,0:T(8,128)(2,1)S(1)}, bf16[1,9,256,256]{3,2,1,0:T(8,128)(2,1)}) fusion(bf16[2,9,256,256]{3,2,1,0:T(8,128)(2,1)} %param.4), kind=kLoop, calls=%fused_computation.292 | loop fusion | bytes 4718592 | tf_op jit(solution)/shard_map/unstack | solution.py:268
  9.6 5.3 %collective-permute-done = f32[4,2,32,256]{3,2,0,1:T(8,128)S(1)} collective-permute-done((f32[4,2,32,256]{3,2,0,1:T(8,128)S(1)}, f32[4,2,32,256]{3,2,0,1:T(8,128)S(1)}, u32[]{:S(2)}, u32[]{:S(2)}) %collective-permute-start) | collective-permute-done | bytes 262176 | tf_op jit(solution)/shard_map/ppermute | solution.py:253
  15.0 1.5 collective-permute-done.2
  18.6 1.0 copy-done.6
  19.6 0.9 fusion.2
  20.7 1.0 mul.106
  21.6 0.9 fusion.31.value_ref
  22.6 29.2 %shard_map.58 = f32[16,32,256]{2,1,0:T(8,128)S(1)} custom-call(bf16[4,32,256]{2,1,0:T(8,128)(2,1)S(1)} %fusion.31.value_ref, f32[16,32,256]{2,1,0:T(8,128)S(1)} %get-tuple-element.18.base_ref), custom_call_target="tpu_custom_call" | custom-call | tf_op jit(solution)/shard_map/pallas_call | solution.py:222
  52.0 1.0 copy-done.1
  53.9 1.0 copy.41
  54.9 1.2 mul.108
  56.1 0.9 fusion.61
  57.2 1.0 copy-done.7
  59.3 1.0 mul.110
  60.3 1.0 fusion.30.value_ref
  61.3 24.8 %shard_map.59 = f32[16,32,256]{2,1,0:T(8,128)S(1)} custom-call(bf16[4,32,256]{2,1,0:T(8,128)(2,1)S(1)} %fusion.30.value_ref, f32[16,32,256]{2,1,0:T(8,128)S(1)} %get-tuple-element.18.base_ref), custom_call_target="tpu_custom_call" | custom-call | tf_op jit(solution)/shard_map/pallas_call | solution.py:222
  87.5 1.7 subtract_multiply_fusion
  89.6 2.1 %copy.45 = f32[16,8,4,256]{3,2,1,0:T(4,128)} copy(f32[16,8,4,256]{3,1,2,0:T(8,128)} %get-tuple-element.22) | data formatting | bytes 1048576 | tf_op jit(solution)/shard_map/mul | solution.py:69
  91.6 1.2 mul.112
  92.9 0.9 fusion.60
  94.0 1.0 copy-done.8
  95.0 1.7 subtract_multiply_fusion.1
  97.4 0.9 copy-done.9
  98.4 0.9 fusion.16
  99.5 1.0 reshape.58
  100.5 2.0 %multiply_convert_fusion.4 = (bf16[16,32,256]{2,1,0:T(8,128)(2,1)S(1)}, f32[16,32,256]{2,1,0:T(8,128)}) fusion(f32[16,32,256]{2,1,0:T(8,128)S(1)} %mul.121, f32[16,32,256]{2,1,0:T(8,128)} %reshape.58, f32[16,2,32,256]{3,2,0,1:T(8,128)S(1)} %constant_dynamic-update-slice_fusion.96), kind=kLoop, calls=%fused_computation.19 | loop fusion | flops 393216 | bytes 2359296 | tf_op jit(solution)/shard_map/convert_element_type | solution.py:76
  102.7 1.0 copy-done.3
  103.7 0.9 fusion.14
  105.0 0.9 fusion.28.value_ref
  105.9 28.9 %shard_map.60 = f32[16,32,256]{2,1,0:T(8,128)S(1)} custom-call(bf16[4,32,256]{2,1,0:T(8,128)(2,1)S(1)} %fusion.28.value_ref, f32[16,32,256]{2,1,0:T(8,128)S(1)} %get-tuple-element.17.base_ref), custom_call_target="tpu_custom_call" | custom-call | tf_op jit(solution)/shard_map/pallas_call | solution.py:222
  135.2 0.9 copy-done.10
  136.1 0.9 fusion.12
  137.4 0.9 multiply_convert_fusion.2
  138.6 1.0 copy-done.4
  139.6 0.9 fusion.10
  140.9 0.9 fusion.27.value_ref
  141.8 25.4 %shard_map.61 = f32[16,32,256]{2,1,0:T(8,128)S(1)} custom-call(bf16[4,32,256]{2,1,0:T(8,128)(2,1)S(1)} %fusion.27.value_ref, f32[16,32,256]{2,1,0:T(8,128)S(1)} %get-tuple-element.17.base_ref), custom_call_target="tpu_custom_call" | custom-call | tf_op jit(solution)/shard_map/pallas_call | solution.py:222
  167.6 0.9 copy-done.11
  168.5 0.9 fusion.8
  169.8 0.9 multiply_convert_fusion
  170.9 2.5 %convolution_convert_fusion.1 = bf16[64,3,3,256]{3,0,2,1:T(8,128)(2,1)S(1)} fusion(bf16[1,16,32,256]{3,2,1,0:T(8,128)(2,1)S(1)} %copy-done.13, bf16[1,16,32,64]{3,2,1,0:T(8,128)(2,1)S(1)} %get-tuple-element.28), kind=kOutput, calls=%fused_computation.11 | convolution fusion | flops 141836288 | bytes 622592 | tf_op jit(solution)/shard_map/transpose | solution.py:294
  173.8 2.5 %convolution_convert_fusion = bf16[64,3,3,256]{3,0,2,1:T(8,128)(2,1)S(1)} fusion(bf16[1,16,32,256]{3,2,1,0:T(8,128)(2,1)S(1)} %bitcast.427, bf16[1,16,32,64]{3,2,1,0:T(8,128)(2,1)S(1)} %get-tuple-element.27), kind=kOutput, calls=%fused_computation.10 | convolution fusion | flops 141836288 | bytes 622592 | tf_op jit(solution)/shard_map/transpose | solution.py:294
  177.6 0.9 fusion.6
  180.0 2.2 %pad_maximum_fusion = bf16[64,2,9,256]{3,1,2,0:T(2,128)(2,1)} fusion(bf16[64,1,9,256]{3,1,2,0:T(2,128)(2,1)S(1)} %copy.67, bf16[64,1,9,256]{3,1,2,0:T(2,128)(2,1)S(1)} %copy.66), kind=kLoop, calls=%fused_computation.12 | loop fusion | flops 1179648 | bytes 1179648 | tf_op jit(solution)/shard_map/stack | solution.py:295
  182.1 1.7 fusion.26
  (157 shorter events, 13.0 us)
Async XLA Ops:
  1.8 13.2 %collective-permute-start.1 = (f32[4,2,32,256]{3,2,0,1:T(8,128)S(1)}, f32[4,2,32,256]{3,2,0,1:T(8,128)S(1)}, u32[]{:S(2)}, u32[]{:S(2)}) collective-permute-start(f32[4,2,32,256]{3,2,0,1:T(8,128)S(1)} %get-tuple-element.23), channel_id=1, source_target_pairs={{0,2},{1,3},{2,0},{3,1},{4,6},{5,7},{6,4},{7,5},{8,10},{9,11},{10,... | collective-permute-start | bytes 786440 | tf_op jit(solution)/shard_map/ppermute | solution.py:253
  4.3 10.6 %collective-permute-start = (f32[4,2,32,256]{3,2,0,1:T(8,128)S(1)}, f32[4,2,32,256]{3,2,0,1:T(8,128)S(1)}, u32[]{:S(2)}, u32[]{:S(2)}) collective-permute-start(f32[4,2,32,256]{3,2,0,1:T(8,128)S(1)} %get-tuple-element.23), channel_id=1, source_target_pairs={{0,1},{1,2},{2,3},{3,0},{4,5},{5,6},{6,7},{7,4},{8,9},{9,10},{10,1... | collective-permute-start | bytes 786440 | tf_op jit(solution)/shard_map/ppermute | solution.py:253
  6.7 9.8 %collective-permute-start.2 = (f32[4,2,32,256]{3,2,0,1:T(8,128)S(1)}, f32[4,2,32,256]{3,2,0,1:T(8,128)S(1)}, u32[]{:S(2)}, u32[]{:S(2)}) collective-permute-start(f32[4,2,32,256]{3,2,0,1:T(8,128)S(1)} %get-tuple-element.23), channel_id=1, source_target_pairs={{0,3},{1,0},{2,1},{3,2},{4,7},{5,4},{6,5},{7,6},{8,11},{9,8},{10,9... | collective-permute-start | bytes 786440 | tf_op jit(solution)/shard_map/ppermute | solution.py:253
  9.6 7.4 %copy-start = (bf16[1,9,256,256]{3,2,1,0:T(8,128)(2,1)}, bf16[1,9,256,256]{3,2,1,0:T(8,128)(2,1)S(1)}, u32[]{:S(2)}) copy-start(bf16[1,9,256,256]{3,2,1,0:T(8,128)(2,1)S(1)} %get-tuple-element.15) | copy-start | bytes 3538948
  18.3 1.3 copy-start.6
  51.7 1.3 copy-start.1
  57.0 1.3 copy-start.7
  86.2 1.4 copy-start.2
  93.8 1.3 copy-start.8
  97.1 1.3 copy-start.9
  102.4 1.3 copy-start.3
  134.8 1.3 copy-start.10
  138.3 1.3 copy-start.4
  167.2 1.3 copy-start.11
  169.8 1.1 copy-start.13
  176.4 1.3 copy-start.5
  178.5 1.0 copy-start.12

commit v7 on v1

--- a/solution.py
+++ b/solution.py
@@ -258,6 +258,47 @@
     return whole
 
 
+def window_conv(low_window, kernel3, spec):
+    height, width, channels = low_window.shape
+    out = lax.conv_general_dilated(
+        column_chunks(low_window),
+        kernel3,
+        (1, 1),
+        ((0, 0), (0, 0)),
+        dimension_numbers=("HNWC", spec, "HNWC"),
+        preferred_element_type=jnp.float32,
+    )
+    return out.reshape(height - 2, width, channels)
+
+
+def window_rows(whole, rows):
+    padded = jnp.pad(whole, ((1, 1), (0, 0), (0, 0)))
+    return lax.dynamic_slice_in_dim(padded, lax.axis_index("space") * rows, rows + 2, 0)
+
+
+def forward_jump(current, kernels, rows):
+    start = current
+    for kernel3 in kernels[:-1]:
+        current = current + step_size * jnp.tanh(conv(current.astype(jnp.bfloat16), kernel3))
+    low = window_rows(current.astype(jnp.bfloat16), rows)
+    last = own_rows(current, rows) + step_size * jnp.tanh(
+        window_conv(low, kernels[-1], "HWIO")
+    )
+    return last - own_rows(start, rows)
+
+
+def backward_jump(adjoint, flipped, slopes, rows):
+    start = adjoint
+    for index in reversed(range(1, len(flipped))):
+        scaled = (step_size * slopes[index] * adjoint).astype(jnp.bfloat16)
+        adjoint = adjoint + conv_transposed(scaled, flipped[index])
+    scaled = (step_size * slopes[0] * adjoint).astype(jnp.bfloat16)
+    last = own_rows(adjoint, rows) + window_conv(
+        window_rows(scaled, rows), flipped[0], "HWOI"
+    )
+    return last - own_rows(start, rows)
+
+
 def own_rows(whole, rows):
     return lax.dynamic_slice_in_dim(whole, lax.axis_index("space") * rows, rows, 0)
 
@@ -272,15 +313,13 @@
 
     begin_state = full_input
     for sweep_index in range(ITERS):
-        block_end, _, _ = forward_block(begin_state, kernels)
-        jump = own_rows(block_end - begin_state, rows)
+        jump = forward_jump(begin_state, kernels, rows)
         begin_state = scan_and_gather(jump, full_input, False, sweep_index)
     outputs, inputs_low, slopes = forward_block(begin_state, kernels)
 
     finish = full_cotangent
     for sweep_index in range(ITERS):
-        begins, _ = backward_block(finish, flipped, slopes)
-        back = own_rows(begins - finish, rows)
+        back = backward_jump(finish, flipped, slopes, rows)
         finish = scan_and_gather(back, full_cotangent, True, ITERS + sweep_index)
     begins, scaled_list = backward_block(finish, flipped, slopes)
 

time: 170 us -> 178 us (1.047)
  local copies, waits for them, and re-layouts: 27.4 us -> 31.9 us
  other arithmetic: 10.9 us -> 14.8 us
  matrix products: 17.4 us -> 15.6 us
    convert_element_type x0 -> x8, other arithmetic: none -> 4.34 us  [the longest x2 3.1 us: backward_jump(): scaled = (step_size * slopes[0] * adjoint).astype(jnp.bfloat16)]
    mul x12 -> x4, local copies, waits for them, and re-layouts: 4.97 us -> 0.78 us  [forward_block(): current = current + step_size * squashed]
    conv_general_dilated x12 -> x8, matrix products: 12.2 us -> 8.75 us  [chunked_conv(): lax.conv_general_dilated(column_chunks(low), kernel3, (1, 1), ((1, 1), (0...]
    reshape x0 -> x2, local copies, waits for them, and re-layouts: none -> 3.21 us  [window_conv(): return out.reshape(height - 2, width, channels)]
    reshape x6 -> x4, local copies, waits for them, and re-layouts: 1.09 us -> 4.15 us  [chunked_conv(): out.reshape(height, width, kernel3.shape[3] if spec == 'HWIO' else kernel...]
    mul x4 -> x12, local copies, waits for them, and re-layouts: 1.82 us -> 4.63 us  [the longest x4 2.61 us: forward_jump(): step_size * jnp.tanh(conv(current.astype(jnp.bfloat16), kernel3))]
    unnamed x108 -> x104, local copies, waits for them, and re-layouts: 10.1 us -> 8.92 us
  transfers between devices with their start and end apart: 6 -> 6, of which waited for: 1 -> 1; matrix products, arithmetic and copies ran while one was open for 14% -> 12% of each run, Pallas kernels for 30% -> 29%
where the time goes in v7:
time: 178 us; the launch traced here: 177 us
  Pallas kernels  105 us (59%)
  local copies, waits for them, and re-layouts  31.9 us (18%)
  matrix products  15.6 us (9%)
  other arithmetic  14.8 us (8%)
  starting transfers between devices  6.9 us (4%)
  between operations  1.88 us (1%)
    pallas_call x4, Pallas kernels, scan_and_gather(): pl.pallas_call(functools.partial(scan_kernel, n_layer, n_space, reverse),...  105 us
    unnamed x104, local copies, waits for them, and re-layouts  8.92 us
    conv_general_dilated x8, matrix products, chunked_conv(): lax.conv_general_dilated(column_chunks(low), kernel3, (1, 1), ((1, 1), (0...  8.75 us
    ppermute x6, starting transfers between devices, gather_space(): lax.ppermute(piece, 'space', [(i, (i + shift) % count) for i in range(cou...  6.9 us
    transpose x2, matrix products, on_device(): jnp.transpose(grad, (3, 1, 2, 0)).reshape(quarter, 9, channels)  5.09 us
    reshape x4, local copies, waits for them, and re-layouts, chunked_conv(): out.reshape(height, width, kernel3.shape[3] if spec == 'HWIO' else kernel...  4.15 us
  transfers between devices with their start and end apart: 6, of which 1 were waited for; matrix products, arithmetic and copies ran while one was open for 12% of the time, Pallas kernels for 29%

profile of v7, /device:TPU:1, one launch (start us, length us, event | category | flops | bytes accessed | tf_op | source)
XLA Modules:
  0.0 176.7 jit_solution(9596638992123182941)
XLA Ops:
  0.6 3.1 %collective-permute-start = (f32[4,32,256]{2,1,0:T(8,128)}, f32[4,32,256]{2,1,0:T(8,128)S(1)}, u32[]{:S(2)}, u32[]{:S(2)}) collective-permute-start(f32[4,32,256]{2,1,0:T(8,128)} %param.3), channel_id=1, source_target_pairs={{0,1},{1,2},{2,3},{3,0},{4,5},{5,6},{6,7},{7,4},{8,9},{9,10},{10,1... | collective-permute-start | bytes 393224 | tf_op jit(solution)/shard_map/ppermute | solution.py:253
  4.0 1.3 collective-permute-start.1
  5.3 2.0 %collective-permute-start.3 = (f32[4,32,256]{2,1,0:T(8,128)}, f32[4,32,256]{2,1,0:T(8,128)S(1)}, u32[]{:S(2)}, u32[]{:S(2)}) collective-permute-start(f32[4,32,256]{2,1,0:T(8,128)} %param.5), channel_id=1, source_target_pairs={{0,1},{1,2},{2,3},{3,0},{4,5},{5,6},{6,7},{7,4},{8,9},{9,10},{10,1... | collective-permute-start | bytes 393224 | tf_op jit(solution)/shard_map/ppermute | solution.py:253
  7.3 2.9 %fusion.55 = (bf16[1,9,256,256]{3,2,1,0:T(8,128)(2,1)S(1)}, bf16[1,9,256,256]{3,2,1,0:T(8,128)(2,1)}) fusion(bf16[2,9,256,256]{3,2,1,0:T(8,128)(2,1)} %param.4), kind=kLoop, calls=%fused_computation.286 | loop fusion | bytes 4718592 | tf_op jit(solution)/shard_map/unstack | solution.py:309
  10.4 0.9 constant_dynamic-update-slice_fusion.99
  12.3 0.9 fusion.1
  14.0 0.9 copy-done
  15.5 25.7 %shard_map.58 = f32[16,32,256]{2,1,0:T(8,128)S(1)} custom-call(bf16[4,32,256]{2,1,0:T(8,128)(2,1)S(1)} %subtract_convert_fusion.3.value_ref, f32[16,32,256]{2,1,0:T(8,128)S(1)} %constant_dynamic-update-slice_fusion.100.base_ref), custom_call_target="tpu_custom_call" | custom-call | tf_op jit(solution)/shard_map/pallas_call | solution.py:222
  41.5 0.9 fusion
  42.3 1.0 copy.41
  43.3 1.2 mul.120
  44.6 0.9 fusion.53
  45.8 1.0 copy-done.1
  47.2 0.9 subtract_convert_fusion.2.value_ref
  48.1 25.1 %shard_map.59 = f32[16,32,256]{2,1,0:T(8,128)S(1)} custom-call(bf16[4,32,256]{2,1,0:T(8,128)(2,1)S(1)} %subtract_convert_fusion.2.value_ref, f32[16,32,256]{2,1,0:T(8,128)S(1)} %constant_dynamic-update-slice_fusion.100.base_ref), custom_call_target="tpu_custom_call" | custom-call | tf_op jit(solution)/shard_map/pallas_call | solution.py:222
  73.5 1.7 subtract_multiply_fusion
  75.6 0.9 fusion.52
  76.7 1.0 copy-done.2
  77.7 1.9 %subtract_multiply_fusion.1 = (f32[16,8,4,256]{3,1,2,0:T(8,128)}, f32[16,8,4,256]{3,1,2,0:T(8,128)}) fusion(bf16[3,3,256,256]{3,2,1,0:T(8,128)(2,1)S(1)} %bitcast.372, bf16[16,8,6,256]{3,2,0,1:T(8,128)(2,1)S(1)} %constant_dynamic-update-slice_fusion.40), kind=kOutput, calls=%fused_computation.20 | convolution fusion | flops 579338240 | bytes 2621440 | tf_op jit(solution)/shard_map/conv_general_dilated | solution.py:31
  79.6 0.7 convert_bitcast_fusion
  81.1 1.2 copy.48
  82.6 0.9 constant_dynamic-update-slice_fusion.97
  83.5 0.9 constant_dynamic-update-slice_fusion.96.base_ref
  84.8 0.9 copy-done.3
  85.7 0.9 fusion.12
  86.8 1.0 reshape.58
  87.8 1.2 multiply_convert_fusion.4
  89.8 0.7 copy.53
  90.5 1.6 reshape.59
  92.1 0.9 subtract_convert_fusion.1.value_ref
  93.1 29.6 %shard_map.60 = f32[16,32,256]{2,1,0:T(8,128)S(1)} custom-call(bf16[4,32,256]{2,1,0:T(8,128)(2,1)S(1)} %subtract_convert_fusion.1.value_ref, f32[16,32,256]{2,1,0:T(8,128)S(1)} %constant_dynamic-update-slice_fusion.96.base_ref), custom_call_target="tpu_custom_call" | custom-call | tf_op jit(solution)/shard_map/pallas_call | solution.py:222
  123.0 0.9 copy-done.4
  123.9 0.9 fusion.10
  124.8 1.0 copy.55
  125.8 2.0 %reshape.60 = f32[16,32,256]{2,1,0:T(8,128)} reshape(f32[16,8,4,256]{3,2,1,0:T(4,128)} %copy.55) | data formatting | bytes 1048576 | tf_op jit(solution)/shard_map/reshape | solution.py:39
  127.8 1.9 %multiply_convert_fusion.2 = (bf16[16,32,256]{2,1,0:T(8,128)(2,1)S(1)}, f32[16,32,256]{2,1,0:T(8,128)}) fusion(f32[16,32,256]{2,1,0:T(8,128)S(1)} %mul.133, f32[16,32,256]{2,1,0:T(8,128)S(1)} %shard_map.60, f32[16,32,256]{2,1,0:T(8,128)} %reshape.60), kind=kLoop, calls=%fused_computation.15 | loop fusion | flops 393216 | bytes 2359296 | tf_op jit(solution)/shard_map/convert_element_type | solution.py:295
  131.3 1.6 reshape.61
  133.0 1.0 subtract_convert_fusion.value_ref
  133.9 24.8 %shard_map.61 = f32[16,32,256]{2,1,0:T(8,128)S(1)} custom-call(bf16[4,32,256]{2,1,0:T(8,128)(2,1)S(1)} %subtract_convert_fusion.value_ref, f32[16,32,256]{2,1,0:T(8,128)S(1)} %constant_dynamic-update-slice_fusion.96.base_ref), custom_call_target="tpu_custom_call" | custom-call | tf_op jit(solution)/shard_map/pallas_call | solution.py:222
  159.1 0.9 copy-done.5
  160.0 0.9 fusion.8
  161.1 1.0 reshape.62
  162.1 2.0 %multiply_convert_fusion = (bf16[16,32,256]{2,1,0:T(8,128)(2,1)S(1)}, f32[16,32,256]{2,1,0:T(8,128)}) fusion(f32[16,32,256]{2,1,0:T(8,128)S(1)} %mul.133, f32[16,32,256]{2,1,0:T(8,128)S(1)} %shard_map.61, f32[16,32,256]{2,1,0:T(8,128)} %reshape.62), kind=kLoop, calls=%fused_computation.13 | loop fusion | flops 393216 | bytes 2359296 | tf_op jit(solution)/shard_map/convert_element_type | solution.py:76
  164.2 2.5 %convolution_convert_fusion.1 = bf16[64,3,3,256]{3,0,2,1:T(8,128)(2,1)S(1)} fusion(bf16[1,16,32,256]{3,2,1,0:T(8,128)(2,1)S(1)} %copy-done.8, bf16[1,16,32,64]{3,2,1,0:T(8,128)(2,1)S(1)} %get-tuple-element.24), kind=kOutput, calls=%fused_computation.7 | convolution fusion | flops 141836288 | bytes 622592 | tf_op jit(solution)/shard_map/transpose | solution.py:332
  167.2 2.6 %convolution_convert_fusion = bf16[64,3,3,256]{3,0,2,1:T(8,128)(2,1)S(1)} fusion(bf16[1,16,32,256]{3,2,1,0:T(8,128)(2,1)S(1)} %bitcast.369, bf16[1,16,32,64]{3,2,1,0:T(8,128)(2,1)S(1)} %get-tuple-element.23), kind=kOutput, calls=%fused_computation.6 | convolution fusion | flops 141836288 | bytes 622592 | tf_op jit(solution)/shard_map/transpose | solution.py:332
  170.5 0.9 fusion.6
  172.8 2.2 %pad_maximum_fusion = bf16[64,2,9,256]{3,1,2,0:T(2,128)(2,1)} fusion(bf16[64,1,9,256]{3,1,2,0:T(2,128)(2,1)S(1)} %copy.67, bf16[64,1,9,256]{3,1,2,0:T(2,128)(2,1)S(1)} %copy.66), kind=kLoop, calls=%fused_computation.12 | loop fusion | flops 1179648 | bytes 1179648 | tf_op jit(solution)/shard_map/stack | solution.py:333
  175.0 1.7 fusion.26
  (163 shorter events, 11.4 us)
Async XLA Ops:
  0.6 10.7 %collective-permute-start = (f32[4,32,256]{2,1,0:T(8,128)}, f32[4,32,256]{2,1,0:T(8,128)S(1)}, u32[]{:S(2)}, u32[]{:S(2)}) collective-permute-start(f32[4,32,256]{2,1,0:T(8,128)} %param.3), channel_id=1, source_target_pairs={{0,1},{1,2},{2,3},{3,0},{4,5},{5,6},{6,7},{7,4},{8,9},{9,10},{10,1... | collective-permute-start | bytes 393224 | tf_op jit(solution)/shard_map/ppermute | solution.py:253
  3.7 8.3 %collective-permute-start.2 = (f32[4,32,256]{2,1,0:T(8,128)}, f32[4,32,256]{2,1,0:T(8,128)S(1)}, u32[]{:S(2)}, u32[]{:S(2)}) collective-permute-start(f32[4,32,256]{2,1,0:T(8,128)} %param.3), channel_id=1, source_target_pairs={{0,3},{1,0},{2,1},{3,2},{4,7},{5,4},{6,5},{7,6},{8,11},{9,8},{10,9... | collective-permute-start | bytes 393224 | tf_op jit(solution)/shard_map/ppermute | solution.py:253
  4.0 7.9 %collective-permute-start.1 = (f32[4,32,256]{2,1,0:T(8,128)}, f32[4,32,256]{2,1,0:T(8,128)S(1)}, u32[]{:S(2)}, u32[]{:S(2)}) collective-permute-start(f32[4,32,256]{2,1,0:T(8,128)} %param.3), channel_id=1, source_target_pairs={{0,2},{1,3},{2,0},{3,1},{4,6},{5,7},{6,4},{7,5},{8,10},{9,11},{10,... | collective-permute-start | bytes 393224 | tf_op jit(solution)/shard_map/ppermute | solution.py:253
  5.3 75.0 %collective-permute-start.3 = (f32[4,32,256]{2,1,0:T(8,128)}, f32[4,32,256]{2,1,0:T(8,128)S(1)}, u32[]{:S(2)}, u32[]{:S(2)}) collective-permute-start(f32[4,32,256]{2,1,0:T(8,128)} %param.5), channel_id=1, source_target_pairs={{0,1},{1,2},{2,3},{3,0},{4,5},{5,6},{6,7},{7,4},{8,9},{9,10},{10,1... | collective-permute-start | bytes 393224 | tf_op jit(solution)/shard_map/ppermute | solution.py:253
  7.3 76.2 %collective-permute-start.5 = (f32[4,32,256]{2,1,0:T(8,128)}, f32[4,32,256]{2,1,0:T(8,128)}, u32[]{:S(2)}, u32[]{:S(2)}) collective-permute-start(f32[4,32,256]{2,1,0:T(8,128)} %param.5), channel_id=1, source_target_pairs={{0,3},{1,0},{2,1},{3,2},{4,7},{5,4},{6,5},{7,6},{8,11},{9,8},{10,9... | collective-permute-start | bytes 393224 | tf_op jit(solution)/shard_map/ppermute | solution.py:253
  7.3 3.0 %copy-start.9 = (f32[4,32,256]{2,1,0:T(8,128)S(1)}, f32[4,32,256]{2,1,0:T(8,128)}, u32[]{:S(2)}) copy-start(f32[4,32,256]{2,1,0:T(8,128)} %param.3) | copy-start | bytes 393220
  11.4 71.2 %collective-permute-start.4 = (f32[4,32,256]{2,1,0:T(8,128)}, f32[4,32,256]{2,1,0:T(8,128)}, u32[]{:S(2)}, u32[]{:S(2)}) collective-permute-start(f32[4,32,256]{2,1,0:T(8,128)} %param.5), channel_id=1, source_target_pairs={{0,2},{1,3},{2,0},{3,1},{4,6},{5,7},{6,4},{7,5},{8,10},{9,11},{10,... | collective-permute-start | bytes 393224 | tf_op jit(solution)/shard_map/ppermute | solution.py:253
  13.7 1.3 copy-start
  45.5 1.3 copy-start.1
  76.5 1.3 copy-start.2
  79.6 1.1 copy-start.7
  84.5 1.3 copy-start.3
  122.7 1.3 copy-start.4
  158.7 1.3 copy-start.5
  162.1 2.2 %copy-start.8 = (bf16[1,16,32,256]{3,2,1,0:T(8,128)(2,1)S(1)}, bf16[1,16,32,256]{3,2,1,0:T(8,128)(2,1)}, u32[]{:S(2)}) copy-start(bf16[1,16,32,256]{3,2,1,0:T(8,128)(2,1)} %convert_bitcast_fusion) | copy-start | bytes 786436
  171.4 1.0 copy-start.6

commit v8 on v7

--- a/solution.py
+++ b/solution.py
@@ -287,18 +287,6 @@
     return last - own_rows(start, rows)
 
 
-def backward_jump(adjoint, flipped, slopes, rows):
-    start = adjoint
-    for index in reversed(range(1, len(flipped))):
-        scaled = (step_size * slopes[index] * adjoint).astype(jnp.bfloat16)
-        adjoint = adjoint + conv_transposed(scaled, flipped[index])
-    scaled = (step_size * slopes[0] * adjoint).astype(jnp.bfloat16)
-    last = own_rows(adjoint, rows) + window_conv(
-        window_rows(scaled, rows), flipped[0], "HWOI"
-    )
-    return last - own_rows(start, rows)
-
-
 def own_rows(whole, rows):
     return lax.dynamic_slice_in_dim(whole, lax.axis_index("space") * rows, rows, 0)
 
@@ -319,7 +307,8 @@
 
     finish = full_cotangent
     for sweep_index in range(ITERS):
-        back = backward_jump(finish, flipped, slopes, rows)
+        begins, _ = backward_block(finish, flipped, slopes)
+        back = own_rows(begins - finish, rows)
         finish = scan_and_gather(back, full_cotangent, True, ITERS + sweep_index)
     begins, scaled_list = backward_block(finish, flipped, slopes)
 

time: 178 us -> 167 us (0.938)
  local copies, waits for them, and re-layouts: 31.9 us -> 25.2 us
  other arithmetic: 14.8 us -> 9.95 us
    convert_element_type x4 -> x0, other arithmetic: 3.28 us -> none  [the longest x2 3.1 us: backward_jump(): scaled = (step_size * slopes[0] * adjoint).astype(jnp.bfloat16)]
    reshape x2 -> x0, local copies, waits for them, and re-layouts: 3.21 us -> none  [window_conv(): return out.reshape(height - 2, width, channels)]
    reshape x4 -> x6, local copies, waits for them, and re-layouts: 4.15 us -> 1.09 us  [chunked_conv(): out.reshape(height, width, kernel3.shape[3] if spec == 'HWIO' else kernel...]
    mul x4, local copies, waits for them, and re-layouts: 2.61 us -> 0.78 us  [forward_jump(): step_size * jnp.tanh(conv(current.astype(jnp.bfloat16), kernel3))]
    conv_general_dilated x8 -> x10, matrix products: 8.75 us -> 10.5 us  [chunked_conv(): lax.conv_general_dilated(column_chunks(low), kernel3, (1, 1), ((1, 1), (0...]
    unnamed x104 -> x108, local copies, waits for them, and re-layouts: 8.92 us -> 10.1 us
  transfers between devices with their start and end apart: 6 -> 6, of which waited for: 1 -> 1; matrix products, arithmetic and copies ran while one was open for 12% -> 12% of each run, Pallas kernels for 29% -> 31%
where the time goes in v8:
time: 167 us; the launch traced here: 166 us
  Pallas kernels  105 us (63%)
  local copies, waits for them, and re-layouts  25.2 us (15%)
  matrix products  16.4 us (10%)
  other arithmetic  9.95 us (6%)
  starting transfers between devices  6.9 us (4%)
  between operations  2 us (1%)
    pallas_call x4, Pallas kernels, scan_and_gather(): pl.pallas_call(functools.partial(scan_kernel, n_layer, n_space, reverse),...  105 us
    conv_general_dilated x10, matrix products, chunked_conv(): lax.conv_general_dilated(column_chunks(low), kernel3, (1, 1), ((1, 1), (0...  10.5 us
    unnamed x108, local copies, waits for them, and re-layouts  10.1 us
    ppermute x6, starting transfers between devices, gather_space(): lax.ppermute(piece, 'space', [(i, (i + shift) % count) for i in range(cou...  6.9 us
    transpose x2, matrix products, on_device(): jnp.transpose(grad, (3, 1, 2, 0)).reshape(quarter, 9, channels)  5.2 us
  transfers between devices with their start and end apart: 6, of which 1 were waited for; matrix products, arithmetic and copies ran while one was open for 12% of the time, Pallas kernels for 31%

profile of v8, /device:TPU:1, one launch (start us, length us, event | category | flops | bytes accessed | tf_op | source)
XLA Modules:
  0.0 166.0 jit_solution(9191939117532498469)
XLA Ops:
  0.6 3.1 %collective-permute-start = (f32[4,32,256]{2,1,0:T(8,128)}, f32[4,32,256]{2,1,0:T(8,128)S(1)}, u32[]{:S(2)}, u32[]{:S(2)}) collective-permute-start(f32[4,32,256]{2,1,0:T(8,128)} %param.3), channel_id=1, source_target_pairs={{0,1},{1,2},{2,3},{3,0},{4,5},{5,6},{6,7},{7,4},{8,9},{9,10},{10,1... | collective-permute-start | bytes 393224 | tf_op jit(solution)/shard_map/ppermute | solution.py:253
  3.7 0.3 collective-permute-start.2
  4.0 1.3 collective-permute-start.1
  5.3 2.0 %collective-permute-start.3 = (f32[4,32,256]{2,1,0:T(8,128)}, f32[4,32,256]{2,1,0:T(8,128)}, u32[]{:S(2)}, u32[]{:S(2)}) collective-permute-start(f32[4,32,256]{2,1,0:T(8,128)} %param.5), channel_id=1, source_target_pairs={{0,1},{1,2},{2,3},{3,0},{4,5},{5,6},{6,7},{7,4},{8,9},{9,10},{10,1... | collective-permute-start | bytes 393224 | tf_op jit(solution)/shard_map/ppermute | solution.py:253
  7.3 2.9 %fusion.57 = (bf16[1,9,256,256]{3,2,1,0:T(8,128)(2,1)S(1)}, bf16[1,9,256,256]{3,2,1,0:T(8,128)(2,1)}) fusion(bf16[2,9,256,256]{3,2,1,0:T(8,128)(2,1)} %param.4), kind=kLoop, calls=%fused_computation.288 | loop fusion | bytes 4718592 | tf_op jit(solution)/shard_map/unstack | solution.py:297
  10.3 1.1 constant_dynamic-update-slice_fusion.99
  12.3 0.9 fusion.1
  14.0 0.9 copy-done.5
  15.0 0.3 fusion.2
  15.5 25.7 %shard_map.58 = f32[16,32,256]{2,1,0:T(8,128)S(1)} custom-call(bf16[4,32,256]{2,1,0:T(8,128)(2,1)S(1)} %subtract_convert_fusion.1.value_ref, f32[16,32,256]{2,1,0:T(8,128)S(1)} %constant_dynamic-update-slice_fusion.100.base_ref), custom_call_target="tpu_custom_call" | custom-call | tf_op jit(solution)/shard_map/pallas_call | solution.py:222
  41.5 0.9 fusion
  42.7 0.9 fusion.55
  44.0 1.0 copy-done.6
  44.9 0.3 fusion.3
  45.4 0.9 subtract_convert_fusion.value_ref
  46.3 25.2 %shard_map.59 = f32[16,32,256]{2,1,0:T(8,128)S(1)} custom-call(bf16[4,32,256]{2,1,0:T(8,128)(2,1)S(1)} %subtract_convert_fusion.value_ref, f32[16,32,256]{2,1,0:T(8,128)S(1)} %constant_dynamic-update-slice_fusion.100.base_ref), custom_call_target="tpu_custom_call" | custom-call | tf_op jit(solution)/shard_map/pallas_call | solution.py:222
  71.8 1.0 copy-done.1
  72.8 1.7 subtract_multiply_fusion
  74.8 0.9 fusion.54
  76.0 1.9 %subtract_multiply_fusion.1 = (f32[16,8,4,256]{3,1,2,0:T(8,128)}, f32[16,8,4,256]{3,1,2,0:T(8,128)}) fusion(bf16[3,3,256,256]{3,2,1,0:T(8,128)(2,1)S(1)} %bitcast.396, bf16[16,8,6,256]{3,2,0,1:T(8,128)(2,1)S(1)} %constant_dynamic-update-slice_fusion.40), kind=kOutput, calls=%fused_computation.20 | convolution fusion | flops 579338240 | bytes 2621440 | tf_op jit(solution)/shard_map/conv_general_dilated | solution.py:31
  77.8 0.7 convert_bitcast_fusion
  78.6 0.9 constant_dynamic-update-slice_fusion.98
  79.9 1.2 copy.48
  81.4 0.9 constant_dynamic-update-slice_fusion.97
  82.3 0.9 constant_dynamic-update-slice_fusion.96.base_ref
  83.6 0.9 fusion.16
  85.3 1.0 copy-done.2
  86.3 0.9 fusion.14
  87.6 29.0 %shard_map.60 = f32[16,32,256]{2,1,0:T(8,128)S(1)} custom-call(bf16[4,32,256]{2,1,0:T(8,128)(2,1)S(1)} %fusion.28.value_ref, f32[16,32,256]{2,1,0:T(8,128)S(1)} %constant_dynamic-update-slice_fusion.96.base_ref), custom_call_target="tpu_custom_call" | custom-call | tf_op jit(solution)/shard_map/pallas_call | solution.py:222
  116.9 0.9 copy-done.7
  117.9 0.9 fusion.12
  119.2 0.9 multiply_convert_fusion.2
  120.3 1.0 copy-done.3
  121.3 0.9 fusion.10
  122.6 0.9 fusion.27.value_ref
  123.6 25.4 %shard_map.61 = f32[16,32,256]{2,1,0:T(8,128)S(1)} custom-call(bf16[4,32,256]{2,1,0:T(8,128)(2,1)S(1)} %fusion.27.value_ref, f32[16,32,256]{2,1,0:T(8,128)S(1)} %constant_dynamic-update-slice_fusion.96.base_ref), custom_call_target="tpu_custom_call" | custom-call | tf_op jit(solution)/shard_map/pallas_call | solution.py:222
  149.3 0.9 copy-done.8
  150.2 0.9 fusion.8
  151.9 0.6 copy-done.10
  152.5 2.6 %convolution_convert_fusion.1 = bf16[64,3,3,256]{3,0,2,1:T(8,128)(2,1)S(1)} fusion(bf16[1,16,32,256]{3,2,1,0:T(8,128)(2,1)S(1)} %copy-done.10, bf16[1,16,32,64]{3,2,1,0:T(8,128)(2,1)S(1)} %get-tuple-element.24), kind=kOutput, calls=%fused_computation.7 | convolution fusion | flops 141836288 | bytes 622592 | tf_op jit(solution)/shard_map/transpose | solution.py:321
  155.1 0.5 copy.66
  155.6 2.6 %convolution_convert_fusion = bf16[64,3,3,256]{3,0,2,1:T(8,128)(2,1)S(1)} fusion(bf16[1,16,32,256]{3,2,1,0:T(8,128)(2,1)S(1)} %bitcast.387, bf16[1,16,32,64]{3,2,1,0:T(8,128)(2,1)S(1)} %get-tuple-element.23), kind=kOutput, calls=%fused_computation.6 | convolution fusion | flops 141836288 | bytes 622592 | tf_op jit(solution)/shard_map/transpose | solution.py:321
  158.2 0.5 copy.67
  158.8 0.6 copy-done.4
  159.4 0.9 fusion.6
  160.7 1.2 copy.47
  162.2 2.2 %pad_maximum_fusion = bf16[64,2,9,256]{3,1,2,0:T(2,128)(2,1)} fusion(bf16[64,1,9,256]{3,1,2,0:T(2,128)(2,1)S(1)} %copy.67, bf16[64,1,9,256]{3,1,2,0:T(2,128)(2,1)S(1)} %copy.66), kind=kLoop, calls=%fused_computation.12 | loop fusion | flops 1179648 | bytes 1179648 | tf_op jit(solution)/shard_map/stack | solution.py:322
  164.3 1.6 fusion.26
  (165 shorter events, 8.4 us)
Async XLA Ops:
  0.6 10.8 %collective-permute-start = (f32[4,32,256]{2,1,0:T(8,128)}, f32[4,32,256]{2,1,0:T(8,128)S(1)}, u32[]{:S(2)}, u32[]{:S(2)}) collective-permute-start(f32[4,32,256]{2,1,0:T(8,128)} %param.3), channel_id=1, source_target_pairs={{0,1},{1,2},{2,3},{3,0},{4,5},{5,6},{6,7},{7,4},{8,9},{9,10},{10,1... | collective-permute-start | bytes 393224 | tf_op jit(solution)/shard_map/ppermute | solution.py:253
  3.7 8.3 %collective-permute-start.2 = (f32[4,32,256]{2,1,0:T(8,128)}, f32[4,32,256]{2,1,0:T(8,128)S(1)}, u32[]{:S(2)}, u32[]{:S(2)}) collective-permute-start(f32[4,32,256]{2,1,0:T(8,128)} %param.3), channel_id=1, source_target_pairs={{0,3},{1,0},{2,1},{3,2},{4,7},{5,4},{6,5},{7,6},{8,11},{9,8},{10,9... | collective-permute-start | bytes 393224 | tf_op jit(solution)/shard_map/ppermute | solution.py:253
  4.0 7.9 %collective-permute-start.1 = (f32[4,32,256]{2,1,0:T(8,128)}, f32[4,32,256]{2,1,0:T(8,128)S(1)}, u32[]{:S(2)}, u32[]{:S(2)}) collective-permute-start(f32[4,32,256]{2,1,0:T(8,128)} %param.3), channel_id=1, source_target_pairs={{0,2},{1,3},{2,0},{3,1},{4,6},{5,7},{6,4},{7,5},{8,10},{9,11},{10,... | collective-permute-start | bytes 393224 | tf_op jit(solution)/shard_map/ppermute | solution.py:253
  5.3 73.2 %collective-permute-start.3 = (f32[4,32,256]{2,1,0:T(8,128)}, f32[4,32,256]{2,1,0:T(8,128)}, u32[]{:S(2)}, u32[]{:S(2)}) collective-permute-start(f32[4,32,256]{2,1,0:T(8,128)} %param.5), channel_id=1, source_target_pairs={{0,1},{1,2},{2,3},{3,0},{4,5},{5,6},{6,7},{7,4},{8,9},{9,10},{10,1... | collective-permute-start | bytes 393224 | tf_op jit(solution)/shard_map/ppermute | solution.py:253
  7.3 75.0 %collective-permute-start.5 = (f32[4,32,256]{2,1,0:T(8,128)}, f32[4,32,256]{2,1,0:T(8,128)}, u32[]{:S(2)}, u32[]{:S(2)}) collective-permute-start(f32[4,32,256]{2,1,0:T(8,128)} %param.5), channel_id=1, source_target_pairs={{0,3},{1,0},{2,1},{3,2},{4,7},{5,4},{6,5},{7,6},{8,11},{9,8},{10,9... | collective-permute-start | bytes 393224 | tf_op jit(solution)/shard_map/ppermute | solution.py:253
  7.3 2.9 %copy-start.11 = (f32[4,32,256]{2,1,0:T(8,128)S(1)}, f32[4,32,256]{2,1,0:T(8,128)}, u32[]{:S(2)}) copy-start(f32[4,32,256]{2,1,0:T(8,128)} %param.3) | copy-start | bytes 393220
  10.2 31.3 %copy-start = (bf16[1,9,256,256]{3,2,1,0:T(8,128)(2,1)}, bf16[1,9,256,256]{3,2,1,0:T(8,128)(2,1)S(1)}, u32[]{:S(2)}) copy-start(bf16[1,9,256,256]{3,2,1,0:T(8,128)(2,1)S(1)} %get-tuple-element.15) | copy-start | bytes 3538948
  11.5 69.9 %collective-permute-start.4 = (f32[4,32,256]{2,1,0:T(8,128)}, f32[4,32,256]{2,1,0:T(8,128)}, u32[]{:S(2)}, u32[]{:S(2)}) collective-permute-start(f32[4,32,256]{2,1,0:T(8,128)} %param.5), channel_id=1, source_target_pairs={{0,2},{1,3},{2,0},{3,1},{4,6},{5,7},{6,4},{7,5},{8,10},{9,11},{10,... | collective-permute-start | bytes 393224 | tf_op jit(solution)/shard_map/ppermute | solution.py:253
  13.7 1.3 copy-start.5
  43.6 1.3 copy-start.6
  71.5 1.3 copy-start.1
  77.8 1.7 %copy-start.9 = (f32[16,8,4,256]{3,1,2,0:T(8,128)S(1)}, f32[16,8,4,256]{3,1,2,0:T(8,128)}, u32[]{:S(2)}) copy-start(f32[16,8,4,256]{3,1,2,0:T(8,128)} %get-tuple-element.19) | copy-start | bytes 1572868
  85.0 1.3 copy-start.2
  116.6 1.3 copy-start.7
  120.1 1.3 copy-start.3
  149.0 1.3 copy-start.8
  151.5 1.0 copy-start.10
  158.1 1.3 copy-start.4

commit v9 on v8

--- a/solution.py
+++ b/solution.py
@@ -277,14 +277,18 @@
 
 
 def forward_jump(current, kernels, rows):
-    start = current
-    for kernel3 in kernels[:-1]:
-        current = current + step_size * jnp.tanh(conv(current.astype(jnp.bfloat16), kernel3))
-    low = window_rows(current.astype(jnp.bfloat16), rows)
-    last = own_rows(current, rows) + step_size * jnp.tanh(
-        window_conv(low, kernels[-1], "HWIO")
-    )
-    return last - own_rows(start, rows)
+    halo = len(kernels)
+    height = current.shape[0]
+    first = lax.axis_index("space") * rows
+    padded = jnp.pad(current, ((halo, halo), (0, 0), (0, 0)))
+    window = lax.dynamic_slice_in_dim(padded, first, rows + 2 * halo, 0)
+    index = first - halo + jnp.arange(rows + 2 * halo)
+    inside = ((index >= 0) & (index < height))[:, None, None]
+    for kernel3 in kernels:
+        low = jnp.where(inside, window, jnp.zeros_like(window)).astype(jnp.bfloat16)
+        window = window[1:-1] + step_size * jnp.tanh(window_conv(low, kernel3, "HWIO"))
+        inside = inside[1:-1]
+    return window - own_rows(current, rows)
 
 
 def own_rows(whole, rows):

time: 167 us -> 169 us (1.012)
  local copies, waits for them, and re-layouts: 25.2 us -> 27.3 us
  matrix products: 16.4 us -> 14.7 us
    conv_general_dilated x10 -> x8, matrix products: 10.5 us -> 7.95 us  [chunked_conv(): lax.conv_general_dilated(column_chunks(low), kernel3, (1, 1), ((1, 1), (0...]
    dynamic_update_slice x6, local copies, waits for them, and re-layouts: 2.8 us -> 4.6 us  [gather_space(): whole = lax.dynamic_update_slice_in_dim(whole, part, source * rows, 0)]
    mul x8, local copies, waits for them, and re-layouts: 0.98 us -> 2.77 us  [forward_jump(): step_size * jnp.tanh(window_conv(low, kernel3, 'HWIO'))]
    unnamed x108 -> x110, local copies, waits for them, and re-layouts: 10.1 us -> 10.7 us
  transfers between devices with their start and end apart: 6 -> 6, of which waited for: 1 -> 1; matrix products, arithmetic and copies ran while one was open for 12% -> 12% of each run, Pallas kernels for 31% -> 30%
where the time goes in v9:
time: 169 us; the launch traced here: 168 us
  Pallas kernels  106 us (63%)
  local copies, waits for them, and re-layouts  27.3 us (16%)
  matrix products  14.7 us (9%)
  other arithmetic  10.8 us (6%)
  starting transfers between devices  6.86 us (4%)
  between operations  2.01 us (1%)
    pallas_call x4, Pallas kernels, scan_and_gather(): pl.pallas_call(functools.partial(scan_kernel, n_layer, n_space, reverse),...  106 us
    unnamed x110, local copies, waits for them, and re-layouts  10.7 us
    conv_general_dilated x8, matrix products, chunked_conv(): lax.conv_general_dilated(column_chunks(low), kernel3, (1, 1), ((1, 1), (0...  7.95 us
    ppermute x6, starting transfers between devices, gather_space(): lax.ppermute(piece, 'space', [(i, (i + shift) % count) for i in range(cou...  6.86 us
    transpose x2, matrix products, on_device(): jnp.transpose(grad, (3, 1, 2, 0)).reshape(quarter, 9, channels)  5.16 us
    dynamic_update_slice x6, local copies, waits for them, and re-layouts, gather_space(): whole = lax.dynamic_update_slice_in_dim(whole, part, source * rows, 0)  4.6 us
  transfers between devices with their start and end apart: 6, of which 1 were waited for; matrix products, arithmetic and copies ran while one was open for 12% of the time, Pallas kernels for 30%

profile of v9, /device:TPU:1, one launch (start us, length us, event | category | flops | bytes accessed | tf_op | source)
XLA Modules:
  0.0 167.9 jit_solution(1592219774065197190)
XLA Ops:
  0.6 3.1 %collective-permute-start = (f32[4,32,256]{2,1,0:T(8,128)}, f32[4,32,256]{2,1,0:T(8,128)}, u32[]{:S(2)}, u32[]{:S(2)}) collective-permute-start(f32[4,32,256]{2,1,0:T(8,128)} %param.3), channel_id=1, source_target_pairs={{0,1},{1,2},{2,3},{3,0},{4,5},{5,6},{6,7},{7,4},{8,9},{9,10},{10,1... | collective-permute-start | bytes 393224 | tf_op jit(solution)/shard_map/ppermute | solution.py:253
  4.0 1.3 collective-permute-start.1
  5.3 2.0 %collective-permute-start.3 = (f32[4,32,256]{2,1,0:T(8,128)}, f32[4,32,256]{2,1,0:T(8,128)}, u32[]{:S(2)}, u32[]{:S(2)}) collective-permute-start(f32[4,32,256]{2,1,0:T(8,128)} %param.5), channel_id=1, source_target_pairs={{0,1},{1,2},{2,3},{3,0},{4,5},{5,6},{6,7},{7,4},{8,9},{9,10},{10,1... | collective-permute-start | bytes 393224 | tf_op jit(solution)/shard_map/ppermute | solution.py:253
  7.3 1.8 %fusion.67 = (bf16[1,9,256,256]{3,2,1,0:T(8,128)(2,1)S(1)}, bf16[1,9,256,256]{3,2,1,0:T(8,128)(2,1)S(1)}) fusion(bf16[2,9,256,256]{3,2,1,0:T(8,128)(2,1)} %param.4), kind=kLoop, calls=%fused_computation.301 | loop fusion | bytes 4718592 | tf_op jit(solution)/shard_map/unstack | solution.py:301
  9.3 0.9 copy-done.12
  10.6 0.9 constant_dynamic-update-slice_fusion.102
  11.5 0.6 collective-permute-done.1
  12.1 0.9 constant_dynamic-update-slice_fusion.101
  13.0 0.9 constant_dynamic-update-slice_fusion.100.base_ref
  14.6 0.8 copy.37
  15.4 1.7 mul.110
  17.1 1.6 select_convert_fusion.1
  19.3 0.9 fusion.39.value_ref
  20.2 25.7 %shard_map.58 = f32[16,32,256]{2,1,0:T(8,128)S(1)} custom-call(bf16[4,32,256]{2,1,0:T(8,128)(2,1)S(1)} %fusion.39.value_ref, f32[16,32,256]{2,1,0:T(8,128)S(1)} %constant_dynamic-update-slice_fusion.100.base_ref), custom_call_target="tpu_custom_call" | custom-call | tf_op jit(solution)/shard_map/pallas_call | solution.py:222
  47.1 1.0 copy-done.5
  48.6 24.9 %shard_map.59 = f32[16,32,256]{2,1,0:T(8,128)S(1)} custom-call(bf16[4,32,256]{2,1,0:T(8,128)(2,1)S(1)} %fusion.37.value_ref, f32[16,32,256]{2,1,0:T(8,128)S(1)} %constant_dynamic-update-slice_fusion.100.base_ref), custom_call_target="tpu_custom_call" | custom-call | tf_op jit(solution)/shard_map/pallas_call | solution.py:222
  73.8 0.9 subtract_multiply_fusion
  75.1 0.9 fusion.64
  76.2 1.0 copy-done.6
  77.2 1.8 %subtract_multiply_fusion.1 = (f32[16,8,4,256]{3,1,2,0:T(8,128)}, f32[16,8,4,256]{3,1,2,0:T(8,128)}) fusion(bf16[3,3,256,256]{3,2,1,0:T(8,128)(2,1)S(1)} %bitcast.420, bf16[16,8,6,256]{3,2,0,1:T(8,128)(2,1)S(1)} %constant_dynamic-update-slice_fusion.40), kind=kOutput, calls=%fused_computation.24 | convolution fusion | flops 579338240 | bytes 2621440 | tf_op jit(solution)/shard_map/conv_general_dilated | solution.py:31
  79.1 0.8 convert_bitcast_fusion
  79.8 0.9 constant_dynamic-update-slice_fusion.98
  81.2 1.2 copy.48
  82.6 0.9 constant_dynamic-update-slice_fusion.96.base_ref
  83.9 0.9 copy-done.7
  84.8 0.9 fusion.16
  86.5 1.0 copy-done.1
  87.5 0.9 fusion.14
  88.9 29.3 %shard_map.60 = f32[16,32,256]{2,1,0:T(8,128)S(1)} custom-call(bf16[4,32,256]{2,1,0:T(8,128)(2,1)S(1)} %fusion.34.value_ref, f32[16,32,256]{2,1,0:T(8,128)S(1)} %constant_dynamic-update-slice_fusion.96.base_ref), custom_call_target="tpu_custom_call" | custom-call | tf_op jit(solution)/shard_map/pallas_call | solution.py:222
  118.5 0.9 copy-done.8
  119.5 0.9 fusion.12
  120.7 0.9 multiply_convert_fusion.2
  121.9 1.0 copy-done.2
  122.9 0.9 fusion.10
  124.2 0.9 fusion.33.value_ref
  125.1 25.8 %shard_map.61 = f32[16,32,256]{2,1,0:T(8,128)S(1)} custom-call(bf16[4,32,256]{2,1,0:T(8,128)(2,1)S(1)} %fusion.33.value_ref, f32[16,32,256]{2,1,0:T(8,128)S(1)} %constant_dynamic-update-slice_fusion.96.base_ref), custom_call_target="tpu_custom_call" | custom-call | tf_op jit(solution)/shard_map/pallas_call | solution.py:222
  151.3 0.9 copy-done.9
  152.2 0.9 fusion.8
  153.9 0.6 copy-done.10
  154.5 2.6 %convolution_convert_fusion.1 = bf16[64,3,3,256]{3,0,2,1:T(8,128)(2,1)S(1)} fusion(bf16[1,16,32,256]{3,2,1,0:T(8,128)(2,1)S(1)} %copy-done.10, bf16[1,16,32,64]{3,2,1,0:T(8,128)(2,1)S(1)} %get-tuple-element.24), kind=kOutput, calls=%fused_computation.3 | convolution fusion | flops 141836288 | bytes 622592 | tf_op jit(solution)/shard_map/transpose | solution.py:325
  157.1 0.5 copy.66
  157.6 2.5 %convolution_convert_fusion = bf16[64,3,3,256]{3,0,2,1:T(8,128)(2,1)S(1)} fusion(bf16[1,16,32,256]{3,2,1,0:T(8,128)(2,1)S(1)} %bitcast.411, bf16[1,16,32,64]{3,2,1,0:T(8,128)(2,1)S(1)} %get-tuple-element.23), kind=kOutput, calls=%fused_computation.2 | convolution fusion | flops 141836288 | bytes 622592 | tf_op jit(solution)/shard_map/transpose | solution.py:325
  160.1 0.5 copy.67
  160.8 0.6 copy-done.3
  161.4 0.9 fusion.6
  162.7 1.2 copy.47
  164.1 2.2 %pad_maximum_fusion = bf16[64,2,9,256]{3,1,2,0:T(2,128)(2,1)} fusion(bf16[64,1,9,256]{3,1,2,0:T(2,128)(2,1)S(1)} %copy.67, bf16[64,1,9,256]{3,1,2,0:T(2,128)(2,1)S(1)} %copy.66), kind=kLoop, calls=%fused_computation.16 | loop fusion | flops 1179648 | bytes 1179648 | tf_op jit(solution)/shard_map/stack | solution.py:326
  166.3 1.6 fusion.32
  (167 shorter events, 9.1 us)
Async XLA Ops:
  0.6 9.8 %collective-permute-start = (f32[4,32,256]{2,1,0:T(8,128)}, f32[4,32,256]{2,1,0:T(8,128)}, u32[]{:S(2)}, u32[]{:S(2)}) collective-permute-start(f32[4,32,256]{2,1,0:T(8,128)} %param.3), channel_id=1, source_target_pairs={{0,1},{1,2},{2,3},{3,0},{4,5},{5,6},{6,7},{7,4},{8,9},{9,10},{10,1... | collective-permute-start | bytes 393224 | tf_op jit(solution)/shard_map/ppermute | solution.py:253
  3.7 9.3 %collective-permute-start.2 = (f32[4,32,256]{2,1,0:T(8,128)}, f32[4,32,256]{2,1,0:T(8,128)}, u32[]{:S(2)}, u32[]{:S(2)}) collective-permute-start(f32[4,32,256]{2,1,0:T(8,128)} %param.3), channel_id=1, source_target_pairs={{0,3},{1,0},{2,1},{3,2},{4,7},{5,4},{6,5},{7,6},{8,11},{9,8},{10,9... | collective-permute-start | bytes 393224 | tf_op jit(solution)/shard_map/ppermute | solution.py:253
  4.0 8.0 %collective-permute-start.1 = (f32[4,32,256]{2,1,0:T(8,128)}, f32[4,32,256]{2,1,0:T(8,128)}, u32[]{:S(2)}, u32[]{:S(2)}) collective-permute-start(f32[4,32,256]{2,1,0:T(8,128)} %param.3), channel_id=1, source_target_pairs={{0,2},{1,3},{2,0},{3,1},{4,6},{5,7},{6,4},{7,5},{8,10},{9,11},{10,... | collective-permute-start | bytes 393224 | tf_op jit(solution)/shard_map/ppermute | solution.py:253
  5.3 74.5 %collective-permute-start.3 = (f32[4,32,256]{2,1,0:T(8,128)}, f32[4,32,256]{2,1,0:T(8,128)}, u32[]{:S(2)}, u32[]{:S(2)}) collective-permute-start(f32[4,32,256]{2,1,0:T(8,128)} %param.5), channel_id=1, source_target_pairs={{0,1},{1,2},{2,3},{3,0},{4,5},{5,6},{6,7},{7,4},{8,9},{9,10},{10,1... | collective-permute-start | bytes 393224 | tf_op jit(solution)/shard_map/ppermute | solution.py:253
  7.3 75.3 %collective-permute-start.5 = (f32[4,32,256]{2,1,0:T(8,128)}, f32[4,32,256]{2,1,0:T(8,128)}, u32[]{:S(2)}, u32[]{:S(2)}) collective-permute-start(f32[4,32,256]{2,1,0:T(8,128)} %param.5), channel_id=1, source_target_pairs={{0,3},{1,0},{2,1},{3,2},{4,7},{5,4},{6,5},{7,6},{8,11},{9,8},{10,9... | collective-permute-start | bytes 393224 | tf_op jit(solution)/shard_map/ppermute | solution.py:253
  7.3 1.9 %copy-start.11 = (f32[4,32,256]{2,1,0:T(8,128)S(1)}, f32[4,32,256]{2,1,0:T(8,128)}, u32[]{:S(2)}) copy-start(f32[4,32,256]{2,1,0:T(8,128)} %param.3) | copy-start | bytes 393220
  9.1 9.7 %copy-start.4 = (bf16[1,9,256,256]{3,2,1,0:T(8,128)(2,1)}, bf16[1,9,256,256]{3,2,1,0:T(8,128)(2,1)S(1)}, u32[]{:S(2)}) copy-start(bf16[1,9,256,256]{3,2,1,0:T(8,128)(2,1)S(1)} %get-tuple-element.16) | copy-start | bytes 3538948
  9.2 64.6 %copy-start = (bf16[1,9,256,256]{3,2,1,0:T(8,128)(2,1)}, bf16[1,9,256,256]{3,2,1,0:T(8,128)(2,1)S(1)}, u32[]{:S(2)}) copy-start(bf16[1,9,256,256]{3,2,1,0:T(8,128)(2,1)S(1)} %get-tuple-element.15) | copy-start | bytes 3538948
  9.2 1.1 copy-start.12
  10.4 72.2 %collective-permute-start.4 = (f32[4,32,256]{2,1,0:T(8,128)}, f32[4,32,256]{2,1,0:T(8,128)S(1)}, u32[]{:S(2)}, u32[]{:S(2)}) collective-permute-start(f32[4,32,256]{2,1,0:T(8,128)} %param.5), channel_id=1, source_target_pairs={{0,2},{1,3},{2,0},{3,1},{4,6},{5,7},{6,4},{7,5},{8,10},{9,11},{10,... | collective-permute-start | bytes 393224 | tf_op jit(solution)/shard_map/ppermute | solution.py:253
  46.9 1.3 copy-start.5
  76.0 1.3 copy-start.6
  83.6 1.3 copy-start.7
  86.3 1.3 copy-start.1
  118.2 1.3 copy-start.8
  121.7 1.3 copy-start.2
  151.0 1.3 copy-start.9
  153.5 1.0 copy-start.10
  160.1 1.3 copy-start.3

commit v10 on v7

--- a/solution.py
+++ b/solution.py
@@ -292,10 +292,8 @@
     for index in reversed(range(1, len(flipped))):
         scaled = (step_size * slopes[index] * adjoint).astype(jnp.bfloat16)
         adjoint = adjoint + conv_transposed(scaled, flipped[index])
-    scaled = (step_size * slopes[0] * adjoint).astype(jnp.bfloat16)
-    last = own_rows(adjoint, rows) + window_conv(
-        window_rows(scaled, rows), flipped[0], "HWOI"
-    )
+    window = window_rows(step_size * slopes[0] * adjoint, rows).astype(jnp.bfloat16)
+    last = own_rows(adjoint, rows) + window_conv(window, flipped[0], "HWOI")
     return last - own_rows(start, rows)
 
 

time: 178 us -> 177 us (level)
    convert_element_type x2 -> x0, other arithmetic: 3.1 us -> none  [backward_jump(): scaled = (step_size * slopes[0] * adjoint).astype(jnp.bfloat16)]
    mul x0 -> x2, other arithmetic: none -> 3.1 us  [backward_jump(): step_size * slopes[0] * adjoint]
where the time goes in v10:
time: 177 us; the launch traced here: 176 us
  Pallas kernels  105 us (59%)
  local copies, waits for them, and re-layouts  31.6 us (18%)
  matrix products  15.6 us (9%)
  other arithmetic  14.8 us (8%)
  starting transfers between devices  6.9 us (4%)
  between operations  1.9 us (1%)
    pallas_call x4, Pallas kernels, scan_and_gather(): pl.pallas_call(functools.partial(scan_kernel, n_layer, n_space, reverse),...  105 us
    conv_general_dilated x8, matrix products, chunked_conv(): lax.conv_general_dilated(column_chunks(low), kernel3, (1, 1), ((1, 1), (0...  8.75 us
    unnamed x104, local copies, waits for them, and re-layouts  8.64 us
    ppermute x6, starting transfers between devices, gather_space(): lax.ppermute(piece, 'space', [(i, (i + shift) % count) for i in range(cou...  6.9 us
    transpose x2, matrix products, on_device(): jnp.transpose(grad, (3, 1, 2, 0)).reshape(quarter, 9, channels)  5.09 us
    reshape x4, local copies, waits for them, and re-layouts, chunked_conv(): out.reshape(height, width, kernel3.shape[3] if spec == 'HWIO' else kernel...  4.15 us
  transfers between devices with their start and end apart: 6, of which 1 were waited for; matrix products, arithmetic and copies ran while one was open for 12% of the time, Pallas kernels for 29%

profile of v10, /device:TPU:1, one launch (start us, length us, event | category | flops | bytes accessed | tf_op | source)
XLA Modules:
  0.0 176.4 jit_solution(5146423604613094940)
XLA Ops:
  0.6 3.1 %collective-permute-start = (f32[4,32,256]{2,1,0:T(8,128)}, f32[4,32,256]{2,1,0:T(8,128)S(1)}, u32[]{:S(2)}, u32[]{:S(2)}) collective-permute-start(f32[4,32,256]{2,1,0:T(8,128)} %param.3), channel_id=1, source_target_pairs={{0,1},{1,2},{2,3},{3,0},{4,5},{5,6},{6,7},{7,4},{8,9},{9,10},{10,1... | collective-permute-start | bytes 393224 | tf_op jit(solution)/shard_map/ppermute | solution.py:253
  4.0 1.3 collective-permute-start.1
  5.3 2.0 %collective-permute-start.3 = (f32[4,32,256]{2,1,0:T(8,128)}, f32[4,32,256]{2,1,0:T(8,128)S(1)}, u32[]{:S(2)}, u32[]{:S(2)}) collective-permute-start(f32[4,32,256]{2,1,0:T(8,128)} %param.5), channel_id=1, source_target_pairs={{0,1},{1,2},{2,3},{3,0},{4,5},{5,6},{6,7},{7,4},{8,9},{9,10},{10,1... | collective-permute-start | bytes 393224 | tf_op jit(solution)/shard_map/ppermute | solution.py:253
  7.3 2.9 %fusion.59 = (bf16[1,9,256,256]{3,2,1,0:T(8,128)(2,1)S(1)}, bf16[1,9,256,256]{3,2,1,0:T(8,128)(2,1)}) fusion(bf16[2,9,256,256]{3,2,1,0:T(8,128)(2,1)} %param.4), kind=kLoop, calls=%fused_computation.288 | loop fusion | bytes 4718592 | tf_op jit(solution)/shard_map/unstack | solution.py:307
  10.4 0.9 constant_dynamic-update-slice_fusion.99
  12.3 0.9 fusion.1
  14.0 0.9 copy-done
  15.5 25.7 %shard_map.58 = f32[16,32,256]{2,1,0:T(8,128)S(1)} custom-call(bf16[4,32,256]{2,1,0:T(8,128)(2,1)S(1)} %subtract_convert_fusion.3.value_ref, f32[16,32,256]{2,1,0:T(8,128)S(1)} %constant_dynamic-update-slice_fusion.100.base_ref), custom_call_target="tpu_custom_call" | custom-call | tf_op jit(solution)/shard_map/pallas_call | solution.py:222
  41.5 0.9 fusion
  42.3 1.0 copy.41
  43.3 1.2 mul.120
  44.6 0.9 fusion.57
  45.8 1.0 copy-done.1
  47.2 0.9 subtract_convert_fusion.2.value_ref
  48.1 25.1 %shard_map.59 = f32[16,32,256]{2,1,0:T(8,128)S(1)} custom-call(bf16[4,32,256]{2,1,0:T(8,128)(2,1)S(1)} %subtract_convert_fusion.2.value_ref, f32[16,32,256]{2,1,0:T(8,128)S(1)} %constant_dynamic-update-slice_fusion.100.base_ref), custom_call_target="tpu_custom_call" | custom-call | tf_op jit(solution)/shard_map/pallas_call | solution.py:222
  73.5 1.7 subtract_multiply_fusion
  75.6 0.9 fusion.56
  76.7 1.0 copy-done.2
  77.7 1.9 %subtract_multiply_fusion.1 = (f32[16,8,4,256]{3,1,2,0:T(8,128)}, f32[16,8,4,256]{3,1,2,0:T(8,128)}) fusion(bf16[3,3,256,256]{3,2,1,0:T(8,128)(2,1)S(1)} %bitcast.396, bf16[16,8,6,256]{3,2,0,1:T(8,128)(2,1)S(1)} %constant_dynamic-update-slice_fusion.40), kind=kOutput, calls=%fused_computation.20 | convolution fusion | flops 579338240 | bytes 2621440 | tf_op jit(solution)/shard_map/conv_general_dilated | solution.py:31
  79.6 0.7 convert_bitcast_fusion
  81.1 1.2 copy.48
  82.6 0.9 constant_dynamic-update-slice_fusion.97
  83.5 0.9 constant_dynamic-update-slice_fusion.96.base_ref
  84.8 0.9 copy-done.3
  85.7 0.9 fusion.12
  86.8 1.0 reshape.58
  87.8 1.2 fusion.55
  89.7 0.7 copy.53
  90.4 1.6 reshape.59
  92.0 0.9 subtract_convert_fusion.1.value_ref
  92.9 29.6 %shard_map.60 = f32[16,32,256]{2,1,0:T(8,128)S(1)} custom-call(bf16[4,32,256]{2,1,0:T(8,128)(2,1)S(1)} %subtract_convert_fusion.1.value_ref, f32[16,32,256]{2,1,0:T(8,128)S(1)} %constant_dynamic-update-slice_fusion.96.base_ref), custom_call_target="tpu_custom_call" | custom-call | tf_op jit(solution)/shard_map/pallas_call | solution.py:222
  122.9 0.9 copy-done.4
  123.8 0.9 fusion.10
  124.7 1.0 copy.55
  125.7 2.0 %reshape.60 = f32[16,32,256]{2,1,0:T(8,128)} reshape(f32[16,8,4,256]{3,2,1,0:T(4,128)} %copy.55) | data formatting | bytes 1048576 | tf_op jit(solution)/shard_map/reshape | solution.py:39
  127.7 1.9 %fusion.54 = (bf16[16,32,256]{2,1,0:T(8,128)(2,1)S(1)}, f32[16,32,256]{2,1,0:T(8,128)}) fusion(f32[16,32,256]{2,1,0:T(8,128)S(1)} %mul.133, f32[16,32,256]{2,1,0:T(8,128)S(1)} %shard_map.60, f32[16,32,256]{2,1,0:T(8,128)} %reshape.60), kind=kLoop, calls=%fused_computation.283 | loop fusion | flops 393216 | bytes 2359296 | tf_op jit(solution)/shard_map/mul | solution.py:295
  131.1 1.6 reshape.61
  132.7 1.0 subtract_convert_fusion.value_ref
  133.7 24.8 %shard_map.61 = f32[16,32,256]{2,1,0:T(8,128)S(1)} custom-call(bf16[4,32,256]{2,1,0:T(8,128)(2,1)S(1)} %subtract_convert_fusion.value_ref, f32[16,32,256]{2,1,0:T(8,128)S(1)} %constant_dynamic-update-slice_fusion.96.base_ref), custom_call_target="tpu_custom_call" | custom-call | tf_op jit(solution)/shard_map/pallas_call | solution.py:222
  158.8 0.9 copy-done.5
  159.7 0.9 fusion.8
  160.8 1.0 reshape.62
  161.8 2.0 %multiply_convert_fusion = (bf16[16,32,256]{2,1,0:T(8,128)(2,1)S(1)}, f32[16,32,256]{2,1,0:T(8,128)}) fusion(f32[16,32,256]{2,1,0:T(8,128)S(1)} %mul.133, f32[16,32,256]{2,1,0:T(8,128)S(1)} %shard_map.61, f32[16,32,256]{2,1,0:T(8,128)} %reshape.62), kind=kLoop, calls=%fused_computation.15 | loop fusion | flops 393216 | bytes 2359296 | tf_op jit(solution)/shard_map/convert_element_type | solution.py:76
  164.0 2.5 %convolution_convert_fusion.1 = bf16[64,3,3,256]{3,0,2,1:T(8,128)(2,1)S(1)} fusion(bf16[1,16,32,256]{3,2,1,0:T(8,128)(2,1)S(1)} %copy-done.8, bf16[1,16,32,64]{3,2,1,0:T(8,128)(2,1)S(1)} %get-tuple-element.24), kind=kOutput, calls=%fused_computation.7 | convolution fusion | flops 141836288 | bytes 622592 | tf_op jit(solution)/shard_map/transpose | solution.py:330
  167.0 2.6 %convolution_convert_fusion = bf16[64,3,3,256]{3,0,2,1:T(8,128)(2,1)S(1)} fusion(bf16[1,16,32,256]{3,2,1,0:T(8,128)(2,1)S(1)} %bitcast.393, bf16[1,16,32,64]{3,2,1,0:T(8,128)(2,1)S(1)} %get-tuple-element.23), kind=kOutput, calls=%fused_computation.6 | convolution fusion | flops 141836288 | bytes 622592 | tf_op jit(solution)/shard_map/transpose | solution.py:330
  170.2 0.9 fusion.6
  172.5 2.2 %pad_maximum_fusion = bf16[64,2,9,256]{3,1,2,0:T(2,128)(2,1)} fusion(bf16[64,1,9,256]{3,1,2,0:T(2,128)(2,1)S(1)} %copy.67, bf16[64,1,9,256]{3,1,2,0:T(2,128)(2,1)S(1)} %copy.66), kind=kLoop, calls=%fused_computation.12 | loop fusion | flops 1179648 | bytes 1179648 | tf_op jit(solution)/shard_map/stack | solution.py:331
  174.7 1.7 fusion.28
  (163 shorter events, 11.1 us)
Async XLA Ops:
  0.6 10.7 %collective-permute-start = (f32[4,32,256]{2,1,0:T(8,128)}, f32[4,32,256]{2,1,0:T(8,128)S(1)}, u32[]{:S(2)}, u32[]{:S(2)}) collective-permute-start(f32[4,32,256]{2,1,0:T(8,128)} %param.3), channel_id=1, source_target_pairs={{0,1},{1,2},{2,3},{3,0},{4,5},{5,6},{6,7},{7,4},{8,9},{9,10},{10,1... | collective-permute-start | bytes 393224 | tf_op jit(solution)/shard_map/ppermute | solution.py:253
  3.7 8.3 %collective-permute-start.2 = (f32[4,32,256]{2,1,0:T(8,128)}, f32[4,32,256]{2,1,0:T(8,128)S(1)}, u32[]{:S(2)}, u32[]{:S(2)}) collective-permute-start(f32[4,32,256]{2,1,0:T(8,128)} %param.3), channel_id=1, source_target_pairs={{0,3},{1,0},{2,1},{3,2},{4,7},{5,4},{6,5},{7,6},{8,11},{9,8},{10,9... | collective-permute-start | bytes 393224 | tf_op jit(solution)/shard_map/ppermute | solution.py:253
  4.0 7.9 %collective-permute-start.1 = (f32[4,32,256]{2,1,0:T(8,128)}, f32[4,32,256]{2,1,0:T(8,128)S(1)}, u32[]{:S(2)}, u32[]{:S(2)}) collective-permute-start(f32[4,32,256]{2,1,0:T(8,128)} %param.3), channel_id=1, source_target_pairs={{0,2},{1,3},{2,0},{3,1},{4,6},{5,7},{6,4},{7,5},{8,10},{9,11},{10,... | collective-permute-start | bytes 393224 | tf_op jit(solution)/shard_map/ppermute | solution.py:253
  5.3 75.0 %collective-permute-start.3 = (f32[4,32,256]{2,1,0:T(8,128)}, f32[4,32,256]{2,1,0:T(8,128)S(1)}, u32[]{:S(2)}, u32[]{:S(2)}) collective-permute-start(f32[4,32,256]{2,1,0:T(8,128)} %param.5), channel_id=1, source_target_pairs={{0,1},{1,2},{2,3},{3,0},{4,5},{5,6},{6,7},{7,4},{8,9},{9,10},{10,1... | collective-permute-start | bytes 393224 | tf_op jit(solution)/shard_map/ppermute | solution.py:253
  7.3 76.2 %collective-permute-start.5 = (f32[4,32,256]{2,1,0:T(8,128)}, f32[4,32,256]{2,1,0:T(8,128)}, u32[]{:S(2)}, u32[]{:S(2)}) collective-permute-start(f32[4,32,256]{2,1,0:T(8,128)} %param.5), channel_id=1, source_target_pairs={{0,3},{1,0},{2,1},{3,2},{4,7},{5,4},{6,5},{7,6},{8,11},{9,8},{10,9... | collective-permute-start | bytes 393224 | tf_op jit(solution)/shard_map/ppermute | solution.py:253
  7.3 3.0 %copy-start.9 = (f32[4,32,256]{2,1,0:T(8,128)S(1)}, f32[4,32,256]{2,1,0:T(8,128)}, u32[]{:S(2)}) copy-start(f32[4,32,256]{2,1,0:T(8,128)} %param.3) | copy-start | bytes 393220
  11.4 71.2 %collective-permute-start.4 = (f32[4,32,256]{2,1,0:T(8,128)}, f32[4,32,256]{2,1,0:T(8,128)}, u32[]{:S(2)}, u32[]{:S(2)}) collective-permute-start(f32[4,32,256]{2,1,0:T(8,128)} %param.5), channel_id=1, source_target_pairs={{0,2},{1,3},{2,0},{3,1},{4,6},{5,7},{6,4},{7,5},{8,10},{9,11},{10,... | collective-permute-start | bytes 393224 | tf_op jit(solution)/shard_map/ppermute | solution.py:253
  13.7 1.3 copy-start
  45.5 1.3 copy-start.1
  76.5 1.3 copy-start.2
  79.6 1.1 copy-start.7
  84.5 1.3 copy-start.3
  122.5 1.3 copy-start.4
  158.4 1.3 copy-start.5
  161.8 2.2 %copy-start.8 = (bf16[1,16,32,256]{3,2,1,0:T(8,128)(2,1)S(1)}, bf16[1,16,32,256]{3,2,1,0:T(8,128)(2,1)}, u32[]{:S(2)}) copy-start(bf16[1,16,32,256]{3,2,1,0:T(8,128)(2,1)} %convert_bitcast_fusion) | copy-start | bytes 786436
  171.1 1.0 copy-start.6

commit v11 on v8

--- a/solution.py
+++ b/solution.py
@@ -238,7 +238,6 @@
         compiler_params=pltpu.CompilerParams(
             collective_id=collective_id,
             has_side_effects=True,
-            vmem_limit_bytes=8 * 1024 * 1024,
         ),
     )(value.astype(link), base)
 

time: 167 us -> 177 us (1.060)
  Pallas kernels: 105 us -> 112 us
  other arithmetic: 9.95 us -> 13.4 us
    pallas_call x4, Pallas kernels: 105 us -> 112 us  [scan_and_gather(): pl.pallas_call(functools.partial(scan_kernel, n_layer, n_space, reverse),...]
    unnamed x108 -> x122, local copies, waits for them, and re-layouts: 10.1 us -> 11.4 us
where the time goes in v11:
time: 177 us; the launch traced here: 176 us
  Pallas kernels  112 us (63%)
  local copies, waits for them, and re-layouts  25.5 us (14%)
  matrix products  16.2 us (9%)
  other arithmetic  13.4 us (8%)
  starting transfers between devices  6.9 us (4%)
  between operations  2.07 us (1%)
    pallas_call x4, Pallas kernels, scan_and_gather(): pl.pallas_call(functools.partial(scan_kernel, n_layer, n_space, reverse),...  112 us
    unnamed x122, local copies, waits for them, and re-layouts  11.4 us
    conv_general_dilated x10, matrix products, chunked_conv(): lax.conv_general_dilated(column_chunks(low), kernel3, (1, 1), ((1, 1), (0...  10.5 us
    ppermute x6, starting transfers between devices, gather_space(): lax.ppermute(piece, 'space', [(i, (i + shift) % count) for i in range(cou...  6.9 us
    transpose x2, matrix products, on_device(): jnp.transpose(grad, (3, 1, 2, 0)).reshape(quarter, 9, channels)  5.05 us
  transfers between devices with their start and end apart: 6, of which 1 were waited for; matrix products, arithmetic and copies ran while one was open for 12% of the time, Pallas kernels for 31%

profile of v11, /device:TPU:1, one launch (start us, length us, event | category | flops | bytes accessed | tf_op | source)
XLA Modules:
  0.0 176.2 jit_solution(10910510244099748603)
XLA Ops:
  0.6 3.1 %collective-permute-start = (f32[4,32,256]{2,1,0:T(8,128)}, f32[4,32,256]{2,1,0:T(8,128)S(1)}, u32[]{:S(2)}, u32[]{:S(2)}) collective-permute-start(f32[4,32,256]{2,1,0:T(8,128)} %param.3), channel_id=1, source_target_pairs={{0,1},{1,2},{2,3},{3,0},{4,5},{5,6},{6,7},{7,4},{8,9},{9,10},{10,1... | collective-permute-start | bytes 393224 | tf_op jit(solution)/shard_map/ppermute | solution.py:252
  4.0 1.3 collective-permute-start.1
  5.3 2.0 %collective-permute-start.3 = (f32[4,32,256]{2,1,0:T(8,128)}, f32[4,32,256]{2,1,0:T(8,128)}, u32[]{:S(2)}, u32[]{:S(2)}) collective-permute-start(f32[4,32,256]{2,1,0:T(8,128)} %param.5), channel_id=1, source_target_pairs={{0,1},{1,2},{2,3},{3,0},{4,5},{5,6},{6,7},{7,4},{8,9},{9,10},{10,1... | collective-permute-start | bytes 393224 | tf_op jit(solution)/shard_map/ppermute | solution.py:252
  7.3 2.9 %fusion.57 = (bf16[1,9,256,256]{3,2,1,0:T(8,128)(2,1)S(1)}, bf16[1,9,256,256]{3,2,1,0:T(8,128)(2,1)}) fusion(bf16[2,9,256,256]{3,2,1,0:T(8,128)(2,1)} %param.4), kind=kLoop, calls=%fused_computation.288 | loop fusion | bytes 4718592 | tf_op jit(solution)/shard_map/unstack | solution.py:296
  10.3 1.1 constant_dynamic-update-slice_fusion.99
  12.3 0.9 fusion.1
  14.0 0.9 copy-done.10
  15.4 0.7 subtract_convert_fusion.1.value_ref
  16.1 27.3 %shard_map.58 = f32[16,32,256]{2,1,0:T(8,128)} custom-call(bf16[4,32,256]{2,1,0:T(8,128)(2,1)} %subtract_convert_fusion.1.value_ref, f32[16,32,256]{2,1,0:T(8,128)} %copy-done), custom_call_target="tpu_custom_call" | custom-call | tf_op jit(solution)/shard_map/pallas_call | solution.py:222
  43.5 1.1 convert_element_type.69
  44.8 0.9 fusion
  46.1 0.6 copy-done.3
  47.1 0.9 copy-done.11
  48.5 0.7 subtract_convert_fusion.value_ref
  49.2 26.8 %shard_map.59 = f32[16,32,256]{2,1,0:T(8,128)} custom-call(bf16[4,32,256]{2,1,0:T(8,128)(2,1)} %subtract_convert_fusion.value_ref, f32[16,32,256]{2,1,0:T(8,128)} %copy-done), custom_call_target="tpu_custom_call" | custom-call | tf_op jit(solution)/shard_map/pallas_call | solution.py:222
  76.0 1.1 convert_element_type.72
  77.3 1.7 subtract_multiply_fusion
  79.4 0.6 copy-done.2
  80.0 0.9 fusion.54
  81.2 1.0 copy-done.12
  82.2 1.9 %subtract_multiply_fusion.1 = (f32[16,8,4,256]{3,1,2,0:T(8,128)}, f32[16,8,4,256]{3,1,2,0:T(8,128)}) fusion(bf16[3,3,256,256]{3,2,1,0:T(8,128)(2,1)S(1)} %bitcast.396, bf16[16,8,6,256]{3,2,0,1:T(8,128)(2,1)S(1)} %constant_dynamic-update-slice_fusion.40), kind=kOutput, calls=%fused_computation.20 | convolution fusion | flops 579338240 | bytes 2621440 | tf_op jit(solution)/shard_map/conv_general_dilated | solution.py:31
  84.1 0.7 convert_bitcast_fusion
  84.8 0.9 constant_dynamic-update-slice_fusion.98
  86.2 1.2 copy.48
  87.6 0.9 constant_dynamic-update-slice_fusion.97
  88.5 0.9 constant_dynamic-update-slice_fusion.96.base_ref
  89.8 0.9 fusion.16
  91.5 1.0 copy-done.7
  92.5 0.9 fusion.14
  93.8 0.7 fusion.28.value_ref
  94.5 30.6 %shard_map.60 = f32[16,32,256]{2,1,0:T(8,128)} custom-call(bf16[4,32,256]{2,1,0:T(8,128)(2,1)} %fusion.28.value_ref, f32[16,32,256]{2,1,0:T(8,128)} %copy-done.1), custom_call_target="tpu_custom_call" | custom-call | tf_op jit(solution)/shard_map/pallas_call | solution.py:222
  125.2 1.2 multiply_convert_fusion.3
  126.6 0.9 fusion.12
  127.9 0.6 copy-done.4
  128.9 1.0 copy-done.8
  129.9 0.9 fusion.10
  131.2 0.7 fusion.27.value_ref
  131.9 27.1 %shard_map.61 = f32[16,32,256]{2,1,0:T(8,128)} custom-call(bf16[4,32,256]{2,1,0:T(8,128)(2,1)} %fusion.27.value_ref, f32[16,32,256]{2,1,0:T(8,128)} %copy-done.1), custom_call_target="tpu_custom_call" | custom-call | tf_op jit(solution)/shard_map/pallas_call | solution.py:222
  159.0 1.2 multiply_convert_fusion.1
  160.5 0.9 fusion.8
  161.8 0.6 copy-done.5
  162.7 0.6 copy-done.17
  163.3 2.5 %convolution_convert_fusion.1 = bf16[64,3,3,256]{3,0,2,1:T(8,128)(2,1)S(1)} fusion(bf16[1,16,32,256]{3,2,1,0:T(8,128)(2,1)S(1)} %copy-done.17, bf16[1,16,32,64]{3,2,1,0:T(8,128)(2,1)S(1)} %get-tuple-element.24), kind=kOutput, calls=%fused_computation.7 | convolution fusion | flops 141836288 | bytes 622592 | tf_op jit(solution)/shard_map/transpose | solution.py:320
  166.3 2.5 %convolution_convert_fusion = bf16[64,3,3,256]{3,0,2,1:T(8,128)(2,1)S(1)} fusion(bf16[1,16,32,256]{3,2,1,0:T(8,128)(2,1)S(1)} %bitcast.387, bf16[1,16,32,64]{3,2,1,0:T(8,128)(2,1)S(1)} %get-tuple-element.23), kind=kOutput, calls=%fused_computation.6 | convolution fusion | flops 141836288 | bytes 622592 | tf_op jit(solution)/shard_map/transpose | solution.py:320
  170.1 0.9 fusion.6
  171.4 0.6 copy-done.15
  172.5 2.2 %pad_maximum_fusion = bf16[64,2,9,256]{3,1,2,0:T(2,128)(2,1)} fusion(bf16[64,1,9,256]{3,1,2,0:T(2,128)(2,1)S(1)} %copy.67, bf16[64,1,9,256]{3,1,2,0:T(2,128)(2,1)S(1)} %copy.66), kind=kLoop, calls=%fused_computation.12 | loop fusion | flops 1179648 | bytes 1179648 | tf_op jit(solution)/shard_map/stack | solution.py:321
  174.6 1.6 fusion.26
  (179 shorter events, 11.1 us)
Async XLA Ops:
  0.6 10.8 %collective-permute-start = (f32[4,32,256]{2,1,0:T(8,128)}, f32[4,32,256]{2,1,0:T(8,128)S(1)}, u32[]{:S(2)}, u32[]{:S(2)}) collective-permute-start(f32[4,32,256]{2,1,0:T(8,128)} %param.3), channel_id=1, source_target_pairs={{0,1},{1,2},{2,3},{3,0},{4,5},{5,6},{6,7},{7,4},{8,9},{9,10},{10,1... | collective-permute-start | bytes 393224 | tf_op jit(solution)/shard_map/ppermute | solution.py:252
  3.7 8.3 %collective-permute-start.2 = (f32[4,32,256]{2,1,0:T(8,128)}, f32[4,32,256]{2,1,0:T(8,128)S(1)}, u32[]{:S(2)}, u32[]{:S(2)}) collective-permute-start(f32[4,32,256]{2,1,0:T(8,128)} %param.3), channel_id=1, source_target_pairs={{0,3},{1,0},{2,1},{3,2},{4,7},{5,4},{6,5},{7,6},{8,11},{9,8},{10,9... | collective-permute-start | bytes 393224 | tf_op jit(solution)/shard_map/ppermute | solution.py:252
  4.0 7.9 %collective-permute-start.1 = (f32[4,32,256]{2,1,0:T(8,128)}, f32[4,32,256]{2,1,0:T(8,128)S(1)}, u32[]{:S(2)}, u32[]{:S(2)}) collective-permute-start(f32[4,32,256]{2,1,0:T(8,128)} %param.3), channel_id=1, source_target_pairs={{0,2},{1,3},{2,0},{3,1},{4,6},{5,7},{6,4},{7,5},{8,10},{9,11},{10,... | collective-permute-start | bytes 393224 | tf_op jit(solution)/shard_map/ppermute | solution.py:252
  5.3 79.5 %collective-permute-start.3 = (f32[4,32,256]{2,1,0:T(8,128)}, f32[4,32,256]{2,1,0:T(8,128)}, u32[]{:S(2)}, u32[]{:S(2)}) collective-permute-start(f32[4,32,256]{2,1,0:T(8,128)} %param.5), channel_id=1, source_target_pairs={{0,1},{1,2},{2,3},{3,0},{4,5},{5,6},{6,7},{7,4},{8,9},{9,10},{10,1... | collective-permute-start | bytes 393224 | tf_op jit(solution)/shard_map/ppermute | solution.py:252
  7.3 81.2 %collective-permute-start.5 = (f32[4,32,256]{2,1,0:T(8,128)}, f32[4,32,256]{2,1,0:T(8,128)}, u32[]{:S(2)}, u32[]{:S(2)}) collective-permute-start(f32[4,32,256]{2,1,0:T(8,128)} %param.5), channel_id=1, source_target_pairs={{0,3},{1,0},{2,1},{3,2},{4,7},{5,4},{6,5},{7,6},{8,11},{9,8},{10,9... | collective-permute-start | bytes 393224 | tf_op jit(solution)/shard_map/ppermute | solution.py:252
  7.3 2.9 %copy-start.18 = (f32[4,32,256]{2,1,0:T(8,128)S(1)}, f32[4,32,256]{2,1,0:T(8,128)}, u32[]{:S(2)}) copy-start(f32[4,32,256]{2,1,0:T(8,128)} %param.3) | copy-start | bytes 393220
  10.2 67.1 %copy-start.6 = (bf16[1,9,256,256]{3,2,1,0:T(8,128)(2,1)}, bf16[1,9,256,256]{3,2,1,0:T(8,128)(2,1)S(1)}, u32[]{:S(2)}) copy-start(bf16[1,9,256,256]{3,2,1,0:T(8,128)(2,1)S(1)} %get-tuple-element.15) | copy-start | bytes 3538948
  11.5 76.1 %collective-permute-start.4 = (f32[4,32,256]{2,1,0:T(8,128)}, f32[4,32,256]{2,1,0:T(8,128)}, u32[]{:S(2)}, u32[]{:S(2)}) collective-permute-start(f32[4,32,256]{2,1,0:T(8,128)} %param.5), channel_id=1, source_target_pairs={{0,2},{1,3},{2,0},{3,1},{4,6},{5,7},{6,4},{7,5},{8,10},{9,11},{10,... | collective-permute-start | bytes 393224 | tf_op jit(solution)/shard_map/ppermute | solution.py:252
  12.0 3.4 %copy-start = (f32[16,32,256]{2,1,0:T(8,128)}, f32[16,32,256]{2,1,0:T(8,128)S(1)}, u32[]{:S(2)}) copy-start(f32[16,32,256]{2,1,0:T(8,128)S(1)} %constant_dynamic-update-slice_fusion.100.base_ref) | copy-start | bytes 1572868
  13.7 1.3 copy-start.10
  45.6 1.0 copy-start.3
  46.8 1.3 copy-start.11
  79.0 1.0 copy-start.2
  80.9 1.3 copy-start.12
  84.1 1.7 copy-start.16
  89.5 4.4 %copy-start.1 = (f32[16,32,256]{2,1,0:T(8,128)}, f32[16,32,256]{2,1,0:T(8,128)S(1)}, u32[]{:S(2)}) copy-start(f32[16,32,256]{2,1,0:T(8,128)S(1)} %constant_dynamic-update-slice_fusion.96.base_ref) | copy-start | bytes 1572868
  91.3 1.3 copy-start.7
  125.1 1.5 copy-start.13
  127.5 1.0 copy-start.4
  128.7 1.3 copy-start.8
  159.0 1.5 copy-start.14
  161.3 1.0 copy-start.5
  162.4 0.9 copy-start.17
  168.8 1.3 copy-start.9
  171.0 1.0 copy-start.15
